TPU v7x, 32 devices: a whole 2x2x4 slice. The times are simulated.
32 devices in a mesh: table: 8 (over y, x, core), rep: 4 (over z).
Axes of the slice: x: 2, y: 2, z: 4, core: 2. Of those that a mesh axis runs over, the one named last changes fastest.
Arguments:
- feature_table: bfloat16 [73728, 1024], P('table'), may hold values from -6 to 6
- neighbour_query_weight: bfloat16 [1024, 1024], replicated, may hold values from -0.1875 to 0.1875
- query_bias: float32 [1024], replicated, may hold values from -1.8 to 1.8
- mix_weight: bfloat16 [2048, 1024], replicated, may hold values from -0.125 to 0.125
- mix_bias: float32 [1024], replicated, may hold values from -1.8 to 1.8
- lookup_ids: int32 [6144, 51], P(('table', 'rep')), may hold values from 0 to 73727, as said below
- present_counts: int32 [6144], P(('table', 'rep')), may hold values from 5 to 50, as said below
- importance: float32 [6144, 50], P(('table', 'rep')), may hold values from 0.75 to 1
- embed_cot: bfloat16 [6144, 1024], P(('table', 'rep')), may hold values from -6 to 6
Outputs:
- embed: bfloat16 [6144, 1024], P(('table', 'rep'))
- table_grad: float32 [73728, 1024], P('table', 'rep')
- query_weight_grad: float32 [1024, 1024], replicated
- query_bias_grad: float32 [1024], replicated
- mix_weight_grad: float32 [2048, 1024], replicated
- mix_bias_grad: float32 [1024], replicated
- statistics: float32 [2], replicated
Inputs may be any that keep to these rules, and one draw needn't show every extreme that they name: `lookup_ids`: within the 192 rows of one device (rows in the order of table+rep), the slots whose id lies in one table index's range (id // 9216) number at most 2448, and one range takes exactly 2448 of them. Of that device's present slots (slot 0, and neighbour slot j + 1 where j < the row's count) at most 1368 lie in one range; on every device one range takes exactly 1368. `present_counts`: the 192 targets of one device come in pairs whose counts add up to one value for that device, from 30 to 55; on the first device it is 55.
All inputs are finite; a program needn't handle non-finite values.
Results may differ from a plain program's by a relative error of at most 0.014.
The roundings to bfloat16 on the way count: a program that leaves them out, or rounds other values in their place, can miss the bound.
Values may be sent and summed in bfloat16 or wider, within the bound.
No kernel may reach another device: no remote copies, remote signals or barrier semaphores. Data moves between devices by JAX's collectives and lax.ppermute only.
A program may use at most 384 MiB of HBM per device.

v0:
```python
import jax
import jax.numpy as jnp
from jax import lax
from jax.sharding import PartitionSpec as P


def local(
    feature_table,
    neighbour_query_weight,
    query_bias,
    mix_weight,
    mix_bias,
    lookup_ids,
    present_counts,
    importance,
    embed_cot,
):
    owners = lax.axis_size("table")
    groups = lax.axis_size("rep")
    rows_owned, width = feature_table.shape
    batch_rows, slot_count = lookup_ids.shape
    slot_total = batch_rows * slot_count
    flat_ids = lookup_ids.reshape(slot_total)
    owner_of = flat_ids // rows_owned
    local_rows = flat_ids - owner_of * rows_owned
    capacity = (2 * slot_total + owners - 1) // owners
    counted = jnp.ones((slot_total,), jnp.bool_)
    onehot = (
        (owner_of[:, None] == jnp.arange(owners, dtype=jnp.int32)[None, :]) & counted[:, None]
    ).astype(jnp.int32)
    placement = jnp.where(
        counted, jnp.sum(jnp.cumsum(onehot, axis=0) * onehot, axis=1) - 1, capacity
    )
    requests = (
        jnp.zeros((owners, capacity), jnp.int32)
        .at[owner_of, placement]
        .set(local_rows, mode="drop")
    )
    wanted = lax.all_to_all(requests, "table", split_axis=0, concat_axis=0, tiled=True)
    reading = jnp.minimum(placement, capacity - 1)
    arrived = lax.all_to_all(
        feature_table[wanted], "table", split_axis=0, concat_axis=0, tiled=True
    )
    rows_flat = arrived[owner_of, reading]
    gathered_rows = rows_flat.reshape(batch_rows, slot_count, width)
    self_rows = gathered_rows[:, 0, :]
    neighbour_rows = gathered_rows[:, 1:, :]
    present = (
        jnp.arange(slot_count - 1, dtype=jnp.int32)[None, :] < present_counts[:, None]
    ).astype(jnp.float32)
    masked_weight = importance * present
    row_portions = (masked_weight / jnp.sum(masked_weight, axis=1, keepdims=True)).astype(
        jnp.bfloat16
    )
    before_relu = (
        jnp.einsum(
            "wsa,ai->wsi",
            neighbour_rows,
            neighbour_query_weight,
            preferred_element_type=jnp.float32,
        )
        + query_bias
    )
    hidden_output = jax.nn.relu(before_relu).astype(jnp.bfloat16)
    pooled_neighbours = jnp.einsum(
        "ef,efq->eq", row_portions, hidden_output, preferred_element_type=jnp.float32
    ).astype(jnp.bfloat16)
    joined = jnp.concatenate([self_rows, pooled_neighbours], axis=1)
    mixed = jnp.dot(joined, mix_weight, preferred_element_type=jnp.float32) + mix_bias
    activation = jax.nn.relu(mixed)
    inverse = lax.rsqrt(jnp.mean(activation * activation, axis=1, keepdims=True) + 1e-06)
    embed = (activation * inverse).astype(jnp.bfloat16)
    cotangent = embed_cot.astype(jnp.float32)
    grad_act = inverse * cotangent - activation * (inverse * inverse * inverse) * jnp.mean(
        activation * cotangent, axis=1, keepdims=True
    )
    grad_mixed = jnp.where(mixed > 0, grad_act, 0.0).astype(jnp.bfloat16)
    mix_weight_grad = lax.dot_general(
        joined, grad_mixed, (((0,), (0,)), ((), ())), preferred_element_type=jnp.float32
    )
    mix_bias_grad = jnp.sum(grad_mixed.astype(jnp.float32), axis=0)
    local_stats = jnp.stack([jnp.sum(present), jnp.sum(masked_weight)])
    grad_joined = lax.dot_general(
        grad_mixed, mix_weight, (((1,), (1,)), ((), ())), preferred_element_type=jnp.float32
    )
    grad_pooled = grad_joined[:, width:]
    grad_hidden = row_portions.astype(jnp.float32)[:, :, None] * grad_pooled[:, None, :]
    gradient_before_relu = jnp.where(before_relu > 0, grad_hidden, 0.0).astype(jnp.bfloat16)
    query_weight_grad = jnp.einsum(
        "mcn,mcf->nf", neighbour_rows, gradient_before_relu, preferred_element_type=jnp.float32
    )
    query_bias_grad = jnp.sum(gradient_before_relu.astype(jnp.float32), axis=(0, 1))
    grad_near = jnp.einsum(
        "vhg,jg->vhj",
        gradient_before_relu,
        neighbour_query_weight,
        preferred_element_type=jnp.float32,
    )
    slot_grads = jnp.concatenate([grad_joined[:, None, :width], grad_near], axis=1).astype(
        jnp.bfloat16
    )
    slot_grads = slot_grads.reshape(slot_total, width)
    outgoing = (
        jnp.zeros((owners, capacity, width), jnp.bfloat16)
        .at[owner_of, placement]
        .set(slot_grads, mode="drop")
    )
    returned = lax.all_to_all(outgoing, "table", split_axis=0, concat_axis=0, tiled=True)
    owned_grad = (
        jnp.zeros((rows_owned, width), jnp.float32)
        .at[wanted.reshape(-1)]
        .add(returned.reshape(owners * capacity, width).astype(jnp.float32))
    )
    table_grad = lax.psum_scatter(
        owned_grad.astype(jnp.bfloat16), "rep", scatter_dimension=1, tiled=True
    ).astype(jnp.float32)
    query_weight_grad, query_bias_grad, mix_weight_grad, mix_bias_grad, local_stats = lax.psum(
        (query_weight_grad, query_bias_grad, mix_weight_grad, mix_bias_grad, local_stats),
        ("table", "rep"),
    )
    statistics = local_stats / (batch_rows * owners * groups)
    return (
        embed,
        table_grad,
        query_weight_grad,
        query_bias_grad,
        mix_weight_grad,
        mix_bias_grad,
        statistics,
    )


def solution(mesh):
    in_specs = (
        P("table", None),
        P(),
        P(),
        P(),
        P(),
        P(("table", "rep"), None),
        P(("table", "rep")),
        P(("table", "rep"), None),
        P(("table", "rep"), None),
    )
    out_specs = (P(("table", "rep"), None), P("table", "rep"), P(), P(), P(), P(), P())
    return jax.shard_map(local, mesh=mesh, in_specs=in_specs, out_specs=out_specs, check_vma=False)
```

profile of v0, /device:TPU:0, one launch (start us, length us, event | category | flops | bytes accessed | tf_op | source)
XLA Modules:
  0.0 2419.1 jit_solution(3866985616971926282)
XLA Ops:
  8.0 1.0 fusion.30
  9.0 0.8 broadcast_divide_fusion
  9.9 0.9 copy.24
  10.8 0.1 copy.22
  10.9 0.2 and.20
  11.2 0.1 copy.23
  11.3 0.2 div.39
  11.5 0.2 reshape.228
  11.9 2.5 reduce-window.6
  14.4 0.3 slice_reduce_fusion
  14.7 0.2 reduce-window.9
  14.9 0.2 add_bitcast_fusion
  15.2 0.1 fusion.26
  15.4 0.3 fusion.39
  15.7 0.9 and_reduce_fusion
  16.6 0.8 multiply_reduce_fusion.1
  17.4 46.4 %scatter_custom_fusion.1 = s32[19584]{0:T(1024)S(1)} fusion(s32[9792]{0:T(1024)S(1)} %broadcast_select_fusion, s32[9792]{0:T(1024)S(1)} %get-tuple-element.28, s32[]{:T(128)} %constant.16.clone.1), kind=kCustom, calls=%fused_computation.73 | custom fusion | bytes 78340
  63.9 0.1 all_to_all.14
  64.0 10.1 all_to_all.22
  74.1 0.6 copy-done.8
  74.7 0.2 fusion.27
  75.1 93.0 %gather_fusion = bf16[19584,1024]{1,0:T(8,128)(2,1)} fusion(bf16[9216,1024]{1,0:T(8,128)(2,1)} %param.9, s32[20480]{0:T(1024)S(1)} %pad_clamp_fusion), kind=kCustom, calls=%fused_computation | custom fusion | bytes 80294400 | tf_op jit(solution)/shard_map/gather | solution.py:42
  168.1 8.0 all-to-all-start.1
  176.2 0.7 fusion.31
  176.8 0.1 copy.28
  177.0 9.2 sort
  186.2 0.6 pad_clamp_fusion.1
  186.8 423.3 %all-to-all-done.1 = bf16[8,2448,1024]{2,1,0:T(8,128)(2,1)} async-done(((bf16[8,2448,1024]{2,1,0:T(8,128)(2,1)}), bf16[8,2448,1024]{2,1,0:T(8,128)(2,1)}, u32[]{:S(2)}, u32[]{:S(2)}) %all-to-all-start.1) | async-done | bytes 40108064 | tf_op jit(solution)/shard_map/all_to_all | solution.py:41
  610.0 174.8 %gather_fusion.1 = bf16[9792,1024]{1,0:T(8,128)(2,1)} fusion(bf16[8,2448,1024]{2,1,0:T(8,128)(2,1)} %all-to-all-done.1, s32[9792]{0:T(1024)S(1)} %get-tuple-element.23), kind=kCustom, calls=%fused_computation.1 | custom fusion | bytes 40186368 | tf_op jit(solution)/shard_map/gather | solution.py:44
  784.8 25.1 %reshape.231 = bf16[192,51,1024]{2,1,0:T(8,128)(2,1)} reshape(bf16[9792,1024]{1,0:T(8,128)(2,1)} %gather_fusion.1) | data formatting | bytes 40108032 | tf_op jit(solution)/shard_map/reshape | solution.py:45
  809.9 2.5 slice.37
  812.4 23.2 slice.38
  835.6 0.1 copy.48
  835.8 39.7 %maximum_convert_fusion = (bf16[192,50,1024]{2,0,1:T(8,128)(2,1)}, f32[192,50,1024]{2,0,1:T(8,128)}) fusion(f32[1024]{0:T(1024)S(1)} %copy-done.14, bf16[1024,1024]{1,0:T(8,128)(2,1)S(1)} %copy-done, bf16[192,50,1024]{2,1,0:T(8,128)(2,1)} %slice.38), kind=kOutput, calls=%fused_computation.10 | convolution fusion | flops 20162150400 | bytes 80744448 | tf_op jit(solution)/shard_map/wsa,ai->wsi/dot_general | solution.py:56
  875.5 49.6 %fusion.3 = bf16[192,1,1024]{2,1,0:T(2,128)(2,1)S(1)} fusion(bf16[192,50,1]{1,2,0:T(2,128)(2,1)S(1)} %copy.28, bf16[192,50,1024]{2,0,1:T(8,128)(2,1)} %get-tuple-element.35), kind=kOutput, calls=%fused_computation.11 | convolution fusion | flops 19660800 | bytes 20073216 | tf_op jit(solution)/shard_map/ef,efq->eq/dot_general | solution.py:65
  925.1 0.1 copy.47
  925.3 1.2 fusion.23
  926.5 1.7 convert_reduce_fusion.1
  928.3 1.5 fusion.45
  929.9 23.5 convert_reduce_fusion
  953.4 30.4 %convolution_convert_fusion = bf16[192,50,1024]{2,0,1:T(8,128)(2,1)} fusion(bf16[192,50,1024]{2,0,1:T(8,128)(2,1)} %get-tuple-element.22, bf16[1024,1024]{1,0:T(8,128)(2,1)S(1)} %copy-done), kind=kOutput, calls=%fused_computation.22 | convolution fusion | flops 20142489600 | bytes 41418752 | tf_op jit(solution)/shard_map/vhg,jg->vhj/dot_general | solution.py:93
  983.8 9.7 pad_maximum_fusion
  993.6 35.6 %copy.27 = bf16[192,51,1024]{2,1,0:T(8,128)(2,1)} copy(bf16[192,51,1024]{2,0,1:T(8,128)(2,1)S(1)} %pad_maximum_fusion) | data formatting | bytes 40108032 | tf_op jit(solution)/shard_map/concatenate | solution.py:99
  1029.2 25.6 %reshape.274 = bf16[9792,1024]{1,0:T(8,128)(2,1)} reshape(bf16[192,51,1024]{2,1,0:T(8,128)(2,1)} %copy.27) | data formatting | bytes 40108032 | tf_op jit(solution)/shard_map/convert_element_type | solution.py:99
  1054.7 165.4 %scatter_custom_fusion.2 = bf16[19584,1024]{1,0:T(8,128)(2,1)} fusion(s32[9792]{0:T(1024)} %get-tuple-element.7, bf16[9792,1024]{1,0:T(8,128)(2,1)} %reshape.274, s32[10240]{0:T(1024)} %pad_clamp_fusion.1, bf16[]{:T(256)} %constant.54.clone.1), kind=kCustom, calls=%fused_computation.13 | custom fusion | bytes 40108544
  1220.1 7.8 all-to-all-start.2
  1227.8 0.4 reduce-scatter.2.cloned.1.call-start
  1228.3 0.2 reduce.7
  1228.5 0.2 reshape.232
  1228.7 0.2 fusion.28
  1228.9 432.8 %all-to-all-done.2 = bf16[8,2448,1024]{2,1,0:T(8,128)(2,1)} async-done(((bf16[8,2448,1024]{2,1,0:T(8,128)(2,1)}), bf16[8,2448,1024]{2,1,0:T(8,128)(2,1)}, u32[]{:S(2)}, u32[]{:S(2)}) %all-to-all-start.2) | async-done | bytes 40108064 | tf_op jit(solution)/shard_map/all_to_all | solution.py:108
  1661.8 180.2 %scatter_custom_fusion = f32[9216,1024]{1,0:T(8,128)} fusion(s32[19584]{0:T(1024)S(1)} %fusion.28, bf16[19584,1024]{1,0:T(8,128)(2,1)} %bitcast.13, f32[]{:T(128)} %constant.26.clone.1), kind=kCustom, calls=%fused_computation.6 | custom fusion | flops 40108032 | bytes 77856768 | tf_op jit(solution)/shard_map/scatter-add | solution.py:112
  1841.9 21.0 convert_element_type.63
  1862.9 0.2 all-reduce.5.cloned.1.call-start
  1863.1 4.7 fusion.24
  1867.9 40.5 %fusion.15 = f32[1024,1024]{1,0:T(8,128)} fusion(bf16[192,50,1024]{2,0,1:T(8,128)(2,1)} %get-tuple-element.22, bf16[192,50,1024]{2,1,0:T(8,128)(2,1)} %slice.38), kind=kOutput, calls=%fused_computation.23 | convolution fusion | flops 20132659200 | bytes 43515904 | tf_op jit(solution)/shard_map/mcn,mcf->nf/dot_general | solution.py:89
  1908.4 1.3 pad_maximum_fusion.4
  1909.7 44.6 %all-reduce.1 = (f32[1024]{0:T(1024)}, f32[1024]{0:T(1024)}, f32[2]{0:T(128)S(1)}) all-reduce(f32[1024]{0:T(1024)S(1)} %copy-done.13, f32[1024]{0:T(1024)S(1)} %copy-done.12, f32[2]{0:T(128)S(1)} %pad_maximum_fusion.4), channel_id=1, replica_groups=mesh['table'=8,'rep'=4] {'table','rep'}, use_global_device_ids=true, to_apply=%region_12.13 | all-reduce | flops 2050 | bytes 16400 | tf_op jit(solution)/shard_map/psum | solution.py:117
  1954.3 0.5 broadcast_multiply_fusion.1
  1954.9 264.6 %reduce-scatter.2.cloned.1.call-done = bf16[9216,256]{1,0:T(8,128)(2,1)} async-done(((bf16[9216,1024]{1,0:T(8,128)(2,1)}), bf16[9216,256]{1,0:T(8,128)(2,1)}) %reduce-scatter.2.cloned.1.call-update) | async-done | bytes 4718608 | tf_op jit(solution)/shard_map/reduce_scatter | solution.py:114
  2219.5 5.8 convert_element_type.64
  2225.3 172.9 %all-reduce.5.cloned.1.call-done = (f32[1024,1024]{1,0:T(8,128)}, f32[2048,1024]{1,0:T(8,128)}) async-done(((f32[1024,1024]{1,0:T(8,128)}, f32[2048,1024]{1,0:T(8,128)}), (f32[1024,1024]{1,0:T(8,128)}, f32[2048,1024]{1,0:T(8,128)})) %all-reduce.5.cloned.1.call-update) | async-done | bytes 12582928 | tf_op jit(solution)/shard_map/psum | solution.py:117
  2398.2 4.8 copy.52
  2403.0 8.4 copy.53
  (49 shorter events, 0.7 us)
Async XLA Ops:
  8.0 827.8 %copy-start = (bf16[1024,1024]{1,0:T(8,128)(2,1)S(1)}, bf16[1024,1024]{1,0:T(8,128)(2,1)}, u32[]{:S(2)}) copy-start(bf16[1024,1024]{1,0:T(8,128)(2,1)} %param.10) | copy-start | bytes 6291460
  74.1 0.6 copy-start.8
  168.1 8.0 copy-start.11
  168.1 8.0 copy-start.15
  168.1 442.0 %all-to-all-start.1 = ((bf16[8,2448,1024]{2,1,0:T(8,128)(2,1)}), bf16[8,2448,1024]{2,1,0:T(8,128)(2,1)}, u32[]{:S(2)}, u32[]{:S(2)}) async-start(bf16[8,2448,1024]{2,1,0:T(8,128)(2,1)} %bitcast.47), calls=%async_computation.1 | async-start | bytes 80216064 | tf_op jit(solution)/shard_map/all_to_all | solution.py:41
  812.4 23.3 copy-start.14
  835.8 89.5 %copy-start.4 = (bf16[192,1,1024]{2,0,1:T(8,128)(2,1)}, bf16[192,1,1024]{2,0,1:T(8,128)(2,1)S(1)}, u32[]{:S(2)}) copy-start(bf16[192,1,1024]{2,0,1:T(8,128)(2,1)S(1)} %copy.48) | copy-start | bytes 1179652
  875.5 49.8 %copy-start.1 = (bf16[2048,1024]{1,0:T(8,128)(2,1)S(1)}, bf16[2048,1024]{1,0:T(8,128)(2,1)}, u32[]{:S(2)}) copy-start(bf16[2048,1024]{1,0:T(8,128)(2,1)} %param.12) | copy-start | bytes 12582916
  875.5 49.8 %copy-start.10 = (bf16[192,1024]{1,0:T(8,128)(2,1)S(1)}, bf16[192,1024]{1,0:T(8,128)(2,1)}, u32[]{:S(2)}) copy-start(bf16[192,1024]{1,0:T(8,128)(2,1)} %param.17) | copy-start | bytes 1179652
  875.5 49.8 %copy-start.16 = (f32[1024]{0:T(1024)S(1)}, f32[1024]{0:T(1024)}, u32[]{:S(2)}) copy-start(f32[1024]{0:T(1024)} %param.13) | copy-start | bytes 12292
  925.3 4.7 copy-start.6
  928.2 1.7 copy-start.2
  1220.1 8.2 copy-start.9
  1220.1 441.7 %all-to-all-start.2 = ((bf16[8,2448,1024]{2,1,0:T(8,128)(2,1)}), bf16[8,2448,1024]{2,1,0:T(8,128)(2,1)}, u32[]{:S(2)}, u32[]{:S(2)}) async-start(bf16[8,2448,1024]{2,1,0:T(8,128)(2,1)} %bitcast.48), calls=%async_computation.2 | async-start | bytes 80216064 | tf_op jit(solution)/shard_map/all_to_all | solution.py:108
  1227.8 991.6 %reduce-scatter.2.cloned.1.call-start = ((), (), s32[]{:S(2)}) async-start(), calls=%async_computation.4 | async-start | bytes 23592960 | tf_op jit(solution)/shard_map/reduce_scatter | solution.py:114
  1841.9 21.2 copy-start.3
  1841.9 21.2 copy-start.5
  1841.9 21.2 copy-start.7
  1862.9 535.3 %all-reduce.5.cloned.1.call-start = ((), (), s32[]{:S(2)}) async-start(), calls=%async_computation.5 | async-start | bytes 25165824 | tf_op jit(solution)/shard_map/psum | solution.py:117
  1867.8 41.8 %copy-start.12 = (f32[1024]{0:T(1024)S(1)}, f32[1024]{0:T(1024)}, u32[]{:S(2)}) copy-start(f32[1024]{0:T(1024)} %get-tuple-element.19) | copy-start | bytes 12292
  1867.8 41.8 %copy-start.13 = (f32[1024]{0:T(1024)S(1)}, f32[1024]{0:T(1024)}, u32[]{:S(2)}) copy-start(f32[1024]{0:T(1024)} %get-tuple-element.21) | copy-start | bytes 12292
Sparse Core Ops, SparseCore 0:
  1863.0 356.3 reduce-scatter.1
Sparse Core Ops, SparseCore 1:
  1908.4 489.7 all-reduce.4
where the time goes:
time: 2430 us; the launch traced here: 2420 us
  waiting for transfers between devices  1290 us (53%)
  local copies, waits for them, and re-layouts  609 us (25%)
  other arithmetic  262 us (11%)
  matrix products  168 us (7%)
  blocking collectives  54.8 us (2%)
    all_to_all x1, waiting for transfers between devices, local(): lax.all_to_all(outgoing, 'table', split_axis=0, concat_axis=0, tiled=True)  433 us
    all_to_all x1, waiting for transfers between devices, local(): lax.all_to_all(feature_table[wanted], 'table', split_axis=0, concat_axis=...  423 us
    reduce_scatter x1, waiting for transfers between devices, local(): lax.psum_scatter(owned_grad.astype(jnp.bfloat16), 'rep', scatter_dimensio...  265 us
    unnamed x42, local copies, waits for them, and re-layouts  227 us
    scatter-add x1, other arithmetic, local(): owned_grad = jnp.zeros((rows_owned, width), jnp.float32).at[wanted.reshap...  180 us
    gather x1, local copies, waits for them, and re-layouts, local(): rows_flat = arrived[owner_of, reading]  175 us
    psum x1, waiting for transfers between devices, local(): lax.psum((query_weight_grad, query_bias_grad, mix_weight_grad, mix_bias_g...  173 us
    gather x1, local copies, waits for them, and re-layouts, local(): feature_table[wanted]  93 us
  transfers between devices with their start and end apart: 4, of which 4 were waited for; matrix products, arithmetic and copies ran while one was open for 3% of the time, Pallas kernels for 0%

commit v1 on v0

v1 whole, which is shorter than its diff:
```python
import functools

import jax
import jax.numpy as jnp
from jax import lax
from jax.experimental import pallas as pl
from jax.experimental.pallas import tpu as pltpu
from jax.sharding import PartitionSpec as P

F32 = jnp.float32
BF16 = jnp.bfloat16
I32 = jnp.int32
LANES = 128
SUBLANES = 8
ROW_BLOCK = 512
SHIFT = 256
UNROLL = 4
VMEM_BYTES = 60 << 20


def row_at(ref, row):
    return ref[pl.ds(pl.multiple_of(row * SUBLANES, SUBLANES), SUBLANES), :]


def put_row(ref, row, value):
    ref[pl.ds(pl.multiple_of(row * SUBLANES, SUBLANES), SUBLANES), :] = value


def clear_rows(ref, rows):
    zero = jnp.zeros((SUBLANES * SUBLANES, LANES), F32)

    def step(i, carry):
        ref[pl.ds(pl.multiple_of(i * SUBLANES * SUBLANES, SUBLANES), SUBLANES * SUBLANES), :] = zero
        return carry

    lax.fori_loop(0, rows // SUBLANES, step, 0)


def walk(first, last, entry):
    count = last - first
    groups = count // UNROLL

    def group(i, carry):
        for u in range(UNROLL):
            entry(first + i * UNROLL + u)
        return carry

    def single(k, carry):
        entry(k)
        return carry

    lax.fori_loop(0, groups, group, 0)
    lax.fori_loop(first + groups * UNROLL, last, single, 0)


def forward_kernel(blocks, bounds, table, query, bias, codes, shares, hidden, pooled, hidden_rows, pooled_rows):
    step = pl.program_id(0)
    width = table.shape[1]
    chunks = width // LANES
    sub = 128

    @pl.when(step < blocks)
    def _():
        def part(j, carry):
            start = pl.multiple_of(j * sub, sub)
            pre = jnp.dot(table[pl.ds(start, sub), :], query[...], preferred_element_type=F32) + bias[...]
            tiny = jnp.finfo(BF16).tiny
            kept = jnp.where(pre > 0, jnp.maximum(pre, tiny), 0.0).astype(BF16)
            hidden[pl.ds(start, sub), :] = kept
            wide = kept.astype(F32)
            base = (step * ROW_BLOCK + start) * SUBLANES
            for g in range(sub // SUBLANES):
                for c in range(chunks):
                    hidden_rows[pl.ds(base + g * SUBLANES * SUBLANES + c, SUBLANES, stride=SUBLANES), :] = wide[
                        g * SUBLANES : (g + 1) * SUBLANES, c * LANES : (c + 1) * LANES
                    ]
            return carry

        lax.fori_loop(0, ROW_BLOCK // sub, part, 0)

    @pl.when(step >= blocks)
    def _():
        device = step - blocks
        targets = pooled.shape[0]
        clear_rows(pooled_rows, targets)

        def entry(k):
            code = codes[0, 0, k]
            node = lax.shift_right_logical(code, 8)
            target = code & (SHIFT - 1)
            put_row(
                pooled_rows,
                target,
                row_at(pooled_rows, target) + shares[0, 0, k] * row_at(hidden_rows, node),
            )

        walk(bounds[device, 0], bounds[device, 1], entry)

        def part(g, carry):
            for c in range(chunks):
                pooled[
                    pl.ds(pl.multiple_of(g * SUBLANES, SUBLANES), SUBLANES), c * LANES : (c + 1) * LANES
                ] = pooled_rows[pl.ds(g * SUBLANES * SUBLANES + c, SUBLANES, stride=SUBLANES), :]
            return carry

        lax.fori_loop(0, targets // SUBLANES, part, 0)


def owner_forward(table, query, bias, codes, shares, bounds, targets):
    rows, width = table.shape
    blocks = rows // ROW_BLOCK
    devices, _, length = codes.shape
    return pl.pallas_call(
        functools.partial(forward_kernel, blocks),
        grid_spec=pltpu.PrefetchScalarGridSpec(
            num_scalar_prefetch=1,
            grid=(blocks + devices,),
            in_specs=[
                pl.BlockSpec((ROW_BLOCK, width), lambda i, b: (jnp.minimum(i, blocks - 1), 0)),
                pl.BlockSpec((width, width), lambda i, b: (0, 0)),
                pl.BlockSpec((1, width), lambda i, b: (0, 0)),
                pl.BlockSpec(
                    (1, 1, length),
                    lambda i, b: (jnp.maximum(i - blocks, 0), 0, 0),
                    memory_space=pltpu.SMEM,
                ),
                pl.BlockSpec(
                    (1, 1, length),
                    lambda i, b: (jnp.maximum(i - blocks, 0), 0, 0),
                    memory_space=pltpu.SMEM,
                ),
            ],
            out_specs=[
                pl.BlockSpec((ROW_BLOCK, width), lambda i, b: (jnp.minimum(i, blocks - 1), 0)),
                pl.BlockSpec((targets, width), lambda i, b: (jnp.maximum(i - blocks, 0), 0)),
            ],
            scratch_shapes=[
                pltpu.VMEM((rows * SUBLANES, LANES), F32),
                pltpu.VMEM((targets * SUBLANES, LANES), F32),
            ],
        ),
        out_shape=[
            jax.ShapeDtypeStruct((rows, width), BF16),
            jax.ShapeDtypeStruct((devices * targets, width), F32),
        ],
        compiler_params=pltpu.CompilerParams(vmem_limit_bytes=VMEM_BYTES),
        cost_estimate=pl.CostEstimate(
            flops=2 * rows * width * width, bytes_accessed=4 * rows * width, transcendentals=0
        ),
        name="owner_forward",
    )(bounds, table, query, bias.reshape(1, width), codes, shares)


def backward_kernel(
    requesters, place, bounds, codes, shares, grads, hidden, table, grad_pre, weight_grad, bias_grad, total, rows_here
):
    step = pl.program_id(0)
    targets, width = grads.shape
    chunks = width // LANES
    tile = SUBLANES * SUBLANES

    @pl.when(step == 0)
    def _():
        clear_rows(total, total.shape[0] // SUBLANES)

    @pl.when(step < requesters)
    def _():
        def spread(g, carry):
            both = grads[pl.ds(pl.multiple_of(g * 16, 16), 16), :].astype(F32)
            for h in range(2):
                for c in range(chunks):
                    rows_here[pl.ds((g * 2 + h) * tile + c, SUBLANES, stride=SUBLANES), :] = both[
                        h * SUBLANES : (h + 1) * SUBLANES, c * LANES : (c + 1) * LANES
                    ]
            return carry

        lax.fori_loop(0, targets // 16, spread, 0)

        def entry(k):
            code = codes[0, 0, k]
            node = lax.shift_right_logical(code, 8)
            target = code & (SHIFT - 1)
            put_row(total, node, row_at(total, node) + shares[0, 0, k] * row_at(rows_here, target))

        walk(bounds[step, 0], bounds[step, 1], entry)

    @pl.when(step == requesters)
    def _():
        weight_grad[...] = jnp.zeros_like(weight_grad)
        bias_grad[...] = jnp.zeros_like(bias_grad)

    @pl.when(step >= requesters)
    def _():
        base = (step - requesters) * ROW_BLOCK // SUBLANES

        def part(g, carry):
            where = pl.ds(pl.multiple_of(g * 16, 16), 16)
            for c in range(chunks):
                lane = slice(c * LANES, (c + 1) * LANES)
                halves = [
                    total[pl.ds((base + g * 2 + h) * tile + c, SUBLANES, stride=SUBLANES), :] for h in range(2)
                ]
                both = jnp.where(
                    hidden[where, lane].astype(F32) > 0, jnp.concatenate(halves, axis=0), 0.0
                )
                grad_pre[where, lane] = both.astype(BF16)
                bias_grad[:, lane] += both[:SUBLANES] + both[SUBLANES:]
            return carry

        lax.fori_loop(0, ROW_BLOCK // 16, part, 0)
        weight_grad[...] += lax.dot_general(
            table[...], grad_pre[...], (((0,), (0,)), ((), ())), preferred_element_type=F32
        )


def owner_backward(table, hidden, grads, codes, shares, bounds, place, groups, targets):
    rows, width = table.shape
    blocks = rows // ROW_BLOCK
    requesters, _, length = codes.shape
    owners = requesters // groups
    part = width // groups

    def node_block(i, place, bounds):
        return (jnp.maximum(i - requesters, 0), 0)

    def list_block(i, place, bounds):
        return (jnp.minimum(i, requesters - 1), 0, 0)

    def grad_block(i, place, bounds):
        k = jnp.minimum(i, requesters - 1)
        return (lax.rem(k, owners) * groups + lax.div(k, owners), 0)

    return pl.pallas_call(
        functools.partial(backward_kernel, requesters),
        grid_spec=pltpu.PrefetchScalarGridSpec(
            num_scalar_prefetch=2,
            grid=(requesters + blocks,),
            in_specs=[
                pl.BlockSpec((1, 1, length), list_block, memory_space=pltpu.SMEM),
                pl.BlockSpec((1, 1, length), list_block, memory_space=pltpu.SMEM),
                pl.BlockSpec((targets, width), grad_block),
                pl.BlockSpec((ROW_BLOCK, width), node_block),
                pl.BlockSpec(
                    (ROW_BLOCK, part), lambda i, place, bounds: (jnp.maximum(i - requesters, 0), place[0])
                ),
            ],
            out_specs=[
                pl.BlockSpec((ROW_BLOCK, width), node_block),
                pl.BlockSpec((part, width), lambda i, place, bounds: (0, 0)),
                pl.BlockSpec((SUBLANES, width), lambda i, place, bounds: (0, 0)),
            ],
            scratch_shapes=[
                pltpu.VMEM((rows * SUBLANES, LANES), F32),
                pltpu.VMEM((targets * SUBLANES, LANES), F32),
            ],
        ),
        out_shape=[
            jax.ShapeDtypeStruct((rows, width), BF16),
            jax.ShapeDtypeStruct((part, width), F32),
            jax.ShapeDtypeStruct((SUBLANES, width), F32),
        ],
        compiler_params=pltpu.CompilerParams(vmem_limit_bytes=VMEM_BYTES),
        cost_estimate=pl.CostEstimate(
            flops=2 * rows * width * width * 2, bytes_accessed=6 * rows * width, transcendentals=0
        ),
        name="owner_backward",
    )(place, bounds, codes, shares, grads, hidden, table)


def table_kernel(requesters, place, bounds, codes, grad_mixed, mix, grad_pre, query, out, bias_grad, self_total, here):
    step = pl.program_id(0)
    targets = grad_mixed.shape[0]

    @pl.when(step == 0)
    def _():
        self_total[...] = jnp.zeros_like(self_total)
        bias_grad[...] = jnp.zeros_like(bias_grad)

    @pl.when(step < requesters)
    def _():
        here[...] = lax.dot_general(
            grad_mixed[...], mix[...], (((1,), (1,)), ((), ())), preferred_element_type=F32
        )
        sums = grad_mixed[...].astype(F32).reshape(targets // SUBLANES, SUBLANES, grad_mixed.shape[1])
        bias_grad[...] += jnp.sum(sums, axis=0)

        def entry(k):
            code = codes[0, 0, k]
            node = lax.shift_right_logical(code, 8)
            target = code & (SHIFT - 1)
            self_total[pl.ds(node, 1), :] += here[pl.ds(target, 1), :]

        walk(bounds[step, 2], bounds[step, 3], entry)

    @pl.when(step >= requesters)
    def _():
        start = pl.multiple_of((step - requesters) * ROW_BLOCK, ROW_BLOCK)
        out[...] = self_total[pl.ds(start, ROW_BLOCK), :] + lax.dot_general(
            grad_pre[...], query[...], (((1,), (1,)), ((), ())), preferred_element_type=F32
        )


def owner_table_grad(grad_mixed, mix, grad_pre, query, codes, bounds, place, groups, targets):
    rows, width = grad_pre.shape
    blocks = rows // ROW_BLOCK
    requesters, _, length = codes.shape
    owners = requesters // groups
    part = width // groups

    def grad_block(i, place, bounds):
        k = jnp.minimum(i, requesters - 1)
        return (lax.rem(k, owners) * groups + lax.div(k, owners), 0)

    return pl.pallas_call(
        functools.partial(table_kernel, requesters),
        grid_spec=pltpu.PrefetchScalarGridSpec(
            num_scalar_prefetch=2,
            grid=(requesters + blocks,),
            in_specs=[
                pl.BlockSpec(
                    (1, 1, length),
                    lambda i, place, bounds: (jnp.minimum(i, requesters - 1), 0, 0),
                    memory_space=pltpu.SMEM,
                ),
                pl.BlockSpec((targets, width), grad_block),
                pl.BlockSpec((part, width), lambda i, place, bounds: (place[0], 0)),
                pl.BlockSpec((ROW_BLOCK, width), lambda i, place, bounds: (jnp.maximum(i - requesters, 0), 0)),
                pl.BlockSpec((part, width), lambda i, place, bounds: (place[0], 0)),
            ],
            out_specs=[
                pl.BlockSpec((ROW_BLOCK, part), lambda i, place, bounds: (jnp.maximum(i - requesters, 0), 0)),
                pl.BlockSpec((SUBLANES, width), lambda i, place, bounds: (0, 0)),
            ],
            scratch_shapes=[pltpu.VMEM((rows, part), F32), pltpu.VMEM((targets, part), F32)],
        ),
        out_shape=[
            jax.ShapeDtypeStruct((rows, part), F32),
            jax.ShapeDtypeStruct((SUBLANES, width), F32),
        ],
        compiler_params=pltpu.CompilerParams(vmem_limit_bytes=VMEM_BYTES),
        cost_estimate=pl.CostEstimate(
            flops=2 * rows * width * part, bytes_accessed=8 * rows * part, transcendentals=0
        ),
        name="owner_table_grad",
    )(place, bounds, codes, grad_mixed, mix, grad_pre, query)


def padded(values, length):
    return jnp.pad(values, (0, length - values.shape[0]))


def local(
    feature_table,
    neighbour_query_weight,
    query_bias,
    mix_weight,
    mix_bias,
    lookup_ids,
    present_counts,
    importance,
    embed_cot,
):
    owners = lax.axis_size("table")
    groups = lax.axis_size("rep")
    devices = owners * groups
    rows_owned, width = feature_table.shape
    batch_rows, slot_count = lookup_ids.shape
    near = slot_count - 1
    owner = lax.axis_index("table").astype(I32)
    group = lax.axis_index("rep").astype(I32)

    own_ids = lax.all_gather(lookup_ids[:, 0], "table", axis=0, tiled=True)
    wanted = own_ids - owner * rows_owned
    mine = (wanted >= 0) & (wanted < rows_owned)
    found = feature_table[jnp.clip(wanted, 0, rows_owned - 1)]
    found = jnp.where(mine[:, None], found, jnp.zeros((), BF16))
    self_rows = lax.psum_scatter(found, "table", scatter_dimension=0, tiled=True)

    present = (jnp.arange(near, dtype=I32)[None, :] < present_counts[:, None]).astype(F32)
    masked_weight = importance * present
    shares = lax.reduce_precision(masked_weight / jnp.sum(masked_weight, axis=1, keepdims=True), 8, 7)
    live_most = batch_rows // 2 * (near + 5)
    length = -(-live_most // LANES) * LANES
    target = jnp.arange(batch_rows, dtype=I32)
    keys = jnp.where(present > 0, lookup_ids[:, 1:] * SHIFT + target[:, None], jnp.iinfo(I32).max)
    keys, sorted_shares = lax.sort((keys.reshape(-1), shares.reshape(-1)), num_keys=1, is_stable=False)
    keys = keys[:live_most]
    sorted_shares = sorted_shares[:live_most]
    own_keys = lax.sort(lookup_ids[:, 0] * SHIFT + target)
    edges = jnp.arange(owners + 1, dtype=I32) * (rows_owned * SHIFT)
    starts = jnp.sum((keys[None, :] < edges[:, None]).astype(I32), axis=1)
    own_starts = jnp.sum((own_keys[None, :] < edges[:, None]).astype(I32), axis=1)
    own_length = SHIFT
    meta = jnp.concatenate(
        [
            starts.astype(F32),
            own_starts.astype(F32),
            jnp.stack([jnp.sum(present), jnp.sum(masked_weight)]),
        ]
    )
    meta_length = -(-meta.shape[0] // LANES) * LANES

    def as_code(key):
        return (key % (rows_owned * SHIFT)).astype(F32)

    request = jnp.concatenate(
        [
            padded(as_code(keys), length),
            padded(sorted_shares, length),
            padded(as_code(own_keys), own_length),
            padded(meta, meta_length),
        ]
    )
    request, _ = lax.optimization_barrier((request, found))
    plane = lax.all_gather(request, "table", axis=0)
    every = lax.all_gather(plane, "rep", axis=0).reshape(devices, -1)

    def unpack(lists):
        count = lists.shape[0]
        at = 2 * length
        codes = lists[:, :length].astype(I32).reshape(count, 1, length)
        parts = lists[:, length:at].reshape(count, 1, length)
        own_codes = lists[:, at : at + own_length].astype(I32).reshape(count, 1, own_length)
        notes = lists[:, at + own_length :]
        first = lax.dynamic_slice(notes, (0, owner), (count, 2))
        own_first = lax.dynamic_slice(notes, (0, owner + owners + 1), (count, 2))
        bounds = jnp.concatenate([first, own_first], axis=1).astype(I32)
        sums = jnp.sum(notes[:, 2 * (owners + 1) : 2 * (owners + 1) + 2], axis=0)
        return codes, parts, own_codes, bounds, sums

    codes, parts, _, bounds, _ = unpack(plane)
    hidden, pooled_parts = owner_forward(
        feature_table, neighbour_query_weight, query_bias, codes, parts, bounds, batch_rows
    )
    pooled_parts, self_rows = lax.optimization_barrier((pooled_parts, self_rows))
    pooled = lax.psum_scatter(pooled_parts, "table", scatter_dimension=0, tiled=True)
    pooled = lax.reduce_precision(pooled, 8, 7).astype(BF16)

    joined = jnp.concatenate([self_rows, pooled], axis=1)
    mixed = jnp.dot(joined, mix_weight, preferred_element_type=F32) + mix_bias
    activation = jax.nn.relu(mixed)
    inverse = lax.rsqrt(jnp.mean(activation * activation, axis=1, keepdims=True) + 1e-06)
    embed = (activation * inverse).astype(BF16)
    cotangent = embed_cot.astype(F32)
    grad_act = inverse * cotangent - activation * (inverse * inverse * inverse) * jnp.mean(
        activation * cotangent, axis=1, keepdims=True
    )
    grad_mixed = jnp.where(mixed > 0, grad_act, 0.0).astype(BF16)
    grad_pooled = lax.dot_general(
        grad_mixed, mix_weight[width:], (((1,), (1,)), ((), ())), preferred_element_type=F32
    ).astype(BF16)
    all_pooled = lax.all_gather(grad_pooled, ("table", "rep"), axis=0, tiled=True)
    all_mixed = lax.all_gather(grad_mixed, ("table", "rep"), axis=0, tiled=True)
    mix_part = 2 * width // devices
    columns = lax.all_to_all(
        joined.reshape(batch_rows, devices, mix_part).transpose(1, 0, 2),
        ("table", "rep"),
        split_axis=0,
        concat_axis=0,
        tiled=True,
    ).reshape(devices * batch_rows, mix_part)

    all_codes, all_parts, all_own_codes, all_bounds, sums = unpack(every)
    place = group.reshape(1)
    grad_pre, query_part, query_bias_part = owner_backward(
        feature_table, hidden, all_pooled, all_codes, all_parts, all_bounds, place, groups, batch_rows
    )
    table_grad, mix_bias_part = owner_table_grad(
        all_mixed, mix_weight, grad_pre, neighbour_query_weight, all_own_codes, all_bounds, place, groups, batch_rows
    )

    query_rows = width // devices
    bias_rows = 16
    outgoing = jnp.concatenate(
        [
            query_part.reshape(owners, query_rows, width),
            jnp.broadcast_to(
                jnp.pad(jnp.sum(query_bias_part, axis=0, keepdims=True), ((0, bias_rows - 1), (0, 0)))[None],
                (owners, bias_rows, width),
            ),
        ],
        axis=1,
    ).astype(BF16)
    summed = jnp.sum(
        lax.all_to_all(outgoing, "table", split_axis=0, concat_axis=0, tiled=True).astype(F32), axis=0
    )
    query_bias_grad = summed[query_rows]
    mix_rows = lax.dot_general(
        columns, all_mixed, (((0,), (0,)), ((), ())), preferred_element_type=F32
    )
    gathered = lax.all_gather(
        jnp.concatenate([summed[:query_rows], mix_rows], axis=0).astype(BF16), ("table", "rep"), axis=0
    ).reshape(owners, groups, query_rows + mix_part, width)
    query_weight_grad = (
        gathered[:, :, :query_rows].transpose(1, 0, 2, 3).reshape(width, width).astype(F32)
    )
    mix_weight_grad = gathered[:, :, query_rows:].reshape(2 * width, width).astype(F32)
    mix_bias_grad = jnp.sum(mix_bias_part, axis=0)
    statistics = sums / (batch_rows * devices)
    return (
        embed,
        table_grad,
        query_weight_grad,
        query_bias_grad,
        mix_weight_grad,
        mix_bias_grad,
        statistics,
    )


def solution(mesh):
    in_specs = (
        P("table", None),
        P(),
        P(),
        P(),
        P(),
        P(("table", "rep"), None),
        P(("table", "rep")),
        P(("table", "rep"), None),
        P(("table", "rep"), None),
    )
    out_specs = (P(("table", "rep"), None), P("table", "rep"), P(), P(), P(), P(), P())
    return jax.shard_map(local, mesh=mesh, in_specs=in_specs, out_specs=out_specs, check_vma=False)
```

time: 2430 us -> 566 us (0.23)
  waiting for transfers between devices: 1290 us -> 180 us
  local copies, waits for them, and re-layouts: 609 us -> 32.9 us
  Pallas kernels: 0 us -> 240 us
  other arithmetic: 262 us -> 33.8 us
  matrix products: 168 us -> 13.7 us
  blocking collectives: 54.8 us -> 18.5 us
    all_to_all x1, waiting for transfers between devices: 433 us -> 5.26 us  [local(): lax.all_to_all(outgoing, 'table', split_axis=0, concat_axis=0, tiled=True)]
    all_to_all x1, waiting for transfers between devices: 423 us -> 28 us  [local(): lax.all_to_all(joined.reshape(batch_rows, devices, mix_part).transpose(1,...]
    gather x2 -> x1, local copies, waits for them, and re-layouts: 268 us -> 15.9 us  [local(): found = feature_table[jnp.clip(wanted, 0, rows_owned - 1)]]
    pallas_call x0 -> x3, Pallas kernels: none -> 240 us  [the longest x1 126 us: owner_backward(): pl.pallas_call(functools.partial(backward_kernel, requesters), grid_spec=...]
    unnamed x42 -> x25, local copies, waits for them, and re-layouts: 227 us -> 2.37 us
    reduce_scatter x1 -> x2, waiting for transfers between devices: 265 us -> 64.7 us  [the longest x1 64.7 us: local(): lax.psum_scatter(pooled_parts, 'table', scatter_dimension=0, tiled=True)]
    scatter-add x1 -> x0, other arithmetic: 180 us -> none  [local(): owned_grad = jnp.zeros((rows_owned, width), jnp.float32).at[wanted.reshap...]
    psum x1 -> x0, waiting for transfers between devices: 173 us -> none  [local(): lax.psum((query_weight_grad, query_bias_grad, mix_weight_grad, mix_bias_g...]
  transfers between devices with their start and end apart: 4 -> 8, of which waited for: 4 -> 5; matrix products, arithmetic and copies ran while one was open for 3% -> 8% of each run, Pallas kernels for 0% -> 43%
where the time goes in v1:
time: 566 us; the launch traced here: 560 us
  Pallas kernels  240 us (42%)
  waiting for transfers between devices  180 us (32%)
  other arithmetic  33.8 us (6%)
  local copies, waits for them, and re-layouts  32.9 us (6%)
  starting transfers between devices  23.8 us (4%)
  blocking collectives  18.5 us (3%)
  between operations  16.7 us (3%)
  matrix products  13.7 us (2%)
    pallas_call x1, Pallas kernels, owner_backward(): pl.pallas_call(functools.partial(backward_kernel, requesters), grid_spec=...  126 us
    pallas_call x1, Pallas kernels, owner_forward(): pl.pallas_call(functools.partial(forward_kernel, blocks), grid_spec=pltpu...  67.1 us
    reduce_scatter x1, waiting for transfers between devices, local(): lax.psum_scatter(pooled_parts, 'table', scatter_dimension=0, tiled=True)  64.7 us
    all_gather x1, waiting for transfers between devices, local(): lax.all_gather(grad_pooled, ('table', 'rep'), axis=0, tiled=True)  64.4 us
    pallas_call x1, Pallas kernels, owner_table_grad(): pl.pallas_call(functools.partial(table_kernel, requesters), grid_spec=plt...  46.5 us
    all_to_all x1, waiting for transfers between devices, local(): lax.all_to_all(joined.reshape(batch_rows, devices, mix_part).transpose(1,...  28 us
    all_to_all x1, starting transfers between devices, local(): lax.all_to_all(outgoing, 'table', split_axis=0, concat_axis=0, tiled=True)  18.6 us
    all_gather x1, waiting for transfers between devices, local(): lax.all_gather(jnp.concatenate([summed[:query_rows], mix_rows], axis=0).a...  17.2 us
  transfers between devices with their start and end apart: 8, of which 5 were waited for; matrix products, arithmetic and copies ran while one was open for 8% of the time, Pallas kernels for 43%

profile of v1, /device:TPU:0, one launch (start us, length us, event | category | flops | bytes accessed | tf_op | source)
XLA Modules:
  0.0 559.7 jit_solution(18087900799021353551)
XLA Ops:
  8.1 0.7 fusion.20
  8.8 1.2 dynamic-slice
  10.7 0.3 dynamic-update-slice
  10.9 9.6 %all-reduce.4 = s32[1536]{0:T(1024)S(1)} all-reduce(s32[1536]{0:T(1024)S(1)} %dynamic-update-slice), channel_id=2, replica_groups=mesh['table'=8,'rep'=4] {'table'}, use_global_device_ids=true, to_apply=%add.4 | all-reduce | flops 1536 | bytes 12288
  20.6 15.9 %gather_fusion = bf16[1536,1024]{1,0:T(8,128)(2,1)S(1)} fusion(bf16[9216,1024]{1,0:T(8,128)(2,1)} %table.3, s32[2048]{0:T(1024)S(1)} %pad_clamp_fusion), kind=kCustom, calls=%fused_computation | custom fusion | bytes 6297600 | tf_op jit(solution)/shard_map/gather | solution.py:375
  36.5 2.1 broadcast_select_fusion
  38.6 0.7 copy-done.6
  39.4 0.6 fusion.16
  40.1 0.1 copy.43
  40.2 0.1 reshape.124
  40.3 0.1 copy.42
  40.4 0.1 reshape.123
  40.6 7.5 %sort.29 = (s32[9600]{0:T(1024)S(1)}, f32[9600]{0:T(1024)S(1)}) sort(s32[9600]{0:T(1024)S(1)} %reshape.123, f32[9600]{0:T(1024)S(1)} %reshape.124), dimensions={0}, to_apply=%region_1.2 | sort | flops 134400 | bytes 153600 | tf_op jit(solution)/shard_map/sort | solution.py:386
  48.1 0.2 convert_reduce_fusion.1
  48.4 3.2 sort.30
  51.6 0.2 convert_reduce_fusion.3
  51.7 1.4 select_maximum_fusion.2
  53.2 8.9 %all-gather.3 = f32[8,1,11136]{2,1,0:T(1,128)S(1)} all-gather(f32[1,1,11136]{2,1,0:T(1,128)S(1)} %reshape.167), channel_id=3, replica_groups=mesh['table'=8,'rep'=4] {'table'}, dimensions={0}, use_global_device_ids=true | all-gather | bytes 400896 | tf_op jit(solution)/shard_map/all_gather | solution.py:415
  62.2 0.8 copy.44.codes
  63.0 0.9 copy.45.shares
  63.9 0.1 constant_dynamic-slice_fusion.3
  64.0 0.7 maximum_convert_fusion.1.bounds
  64.7 67.1 %owner_forward.1 = (bf16[9216,1024]{1,0:T(8,128)(2,1)}, f32[1536,1024]{1,0:T(8,128)}) custom-call(s32[8,4]{1,0:T(8,128)} %maximum_convert_fusion.1.bounds, bf16[9216,1024]{1,0:T(8,128)(2,1)} %table.3, bf16[1024,1024]{1,0:T(8,128)(2,1)} %query.3, f32[1,1024]{1,0:T(1,128)} %bitcast.52, s32[8,1,5376]{2,1,0:T(1,128)} %copy.44.codes, f32[8,1,5376]{2,1,0:T(1,128)} %copy.45.shares), custom_call_target="tpu_custom_call" | custom-call | flops 19327352832 | bytes 37748736 | tf_op jit(solution)/shard_map/owner_forward/pallas_call | solution.py:113
  131.8 0.2 all-gather.15.cloned.1.call-start
  132.0 0.3 all-gather.15.cloned.1.call-update
  132.4 64.7 %reduce-scatter.5.cloned.1.call-done = f32[192,1024]{1,0:T(8,128)} async-done(((f32[1536,1024]{1,0:T(8,128)}), f32[192,1024]{1,0:T(8,128)}) %reduce-scatter.5.cloned.1.call-update) | async-done | bytes 786448 | tf_op jit(solution)/shard_map/reduce_scatter | solution.py:436
  197.1 1.2 reduce-precision_convert_fusion
  198.3 3.4 fusion.9
  201.7 1.1 fusion.8
  202.8 3.3 fusion.2
  206.2 0.5 all-gather.9.cloned.1.call-update
  206.8 0.1 pad_maximum_fusion
  206.8 1.3 copy.48
  208.1 4.6 all-to-all-start.1
  212.8 1.5 slice_bitcast_fusion
  214.2 1.6 copy.46.codes
  215.8 1.6 copy.47.shares
  217.4 0.1 constant_dynamic-slice_fusion.1
  217.4 0.7 maximum_convert_fusion.bounds
  218.1 28.0 %all-to-all-done.1 = bf16[32,192,64]{1,2,0:T(8,128)(2,1)S(1)} async-done(((bf16[32,192,64]{1,2,0:T(8,128)(2,1)}), bf16[32,192,64]{1,2,0:T(8,128)(2,1)S(1)}, u32[]{:S(2)}, u32[]{:S(2)}) %all-to-all-start.1) | async-done | bytes 786464 | tf_op jit(solution)/shard_map/all_to_all | solution.py:455
  246.1 0.6 copy.49
  246.7 1.1 reshape.135
  247.8 64.4 %all-gather.11.cloned.1.call-done.grads = bf16[6144,1024]{1,0:T(8,128)(2,1)} async-done(((bf16[192,1024]{1,0:T(8,128)(2,1)}), bf16[6144,1024]{1,0:T(8,128)(2,1)}) %all-gather.11.cloned.1.call-update) | async-done | bytes 12582928 | tf_op jit(solution)/shard_map/all_gather | solution.py:452
  312.2 126.2 %owner_backward.1 = (bf16[9216,1024]{1,0:T(8,128)(2,1)}, f32[256,1024]{1,0:T(8,128)}, f32[8,1024]{1,0:T(8,128)}) custom-call(s32[1]{0:T(128)} %bitcast.8.place, s32[32,4]{1,0:T(8,128)} %maximum_convert_fusion.bounds, s32[32,1,5376]{2,1,0:T(1,128)} %copy.46.codes, f32[32,1,5376]{2,1,0:T(1,128)} %copy.47.shares, ...), custom_call_target="tpu_custom_call" | custom-call | flops 38654705664 | bytes 56623104 | tf_op jit(solution)/shard_map/owner_backward/pallas_call | solution.py:233
  438.4 1.3 convert.20
  439.7 0.8 reduce_sum.106
  440.5 1.0 pad_maximum_fusion.1
  441.4 18.6 %all-to-all-start = ((bf16[8,48,1024]{2,1,0:T(8,128)(2,1)}), bf16[8,48,1024]{2,1,0:T(8,128)(2,1)S(1)}, u32[]{:S(2)}, u32[]{:S(2)}) async-start(bf16[8,48,1024]{2,1,0:T(8,128)(2,1)} %pad_maximum_fusion.1), calls=%async_computation.2 | async-start | bytes 1572864 | tf_op jit(solution)/shard_map/all_to_all | solution.py:485
  460.0 0.3 all-gather.13.cloned.1.call-start
  460.3 7.0 %fusion.5 = bf16[1,64,1024]{2,1,0:T(8,128)(2,1)S(1)} fusion(bf16[6144,64]{0,1:T(8,128)(2,1)S(1)} %reshape.135, bf16[6144,1024]{1,0:T(8,128)(2,1)} %all-gather.9.cloned.1.call-done.grad_mixed), kind=kOutput, calls=%fused_computation.10 | convolution fusion | flops 805371904 | bytes 13500416 | tf_op jit(solution)/shard_map/dot_general | solution.py:488
  467.3 5.3 all-to-all-done
  472.6 0.1 convert_reduce_fusion
  472.7 0.7 pad_maximum_fusion.2
  473.4 0.6 reshape.130.codes
  474.1 0.1 slice_reduce_fusion
  474.2 0.5 broadcast_multiply_fusion.2
  474.7 46.5 %owner_table_grad.1 = (f32[9216,256]{1,0:T(8,128)}, f32[8,1024]{1,0:T(8,128)}) custom-call(s32[1]{0:T(128)} %bitcast.8.place, s32[32,4]{1,0:T(8,128)} %maximum_convert_fusion.bounds, s32[32,1,256]{2,1,0:T(1,128)} %reshape.130.codes, bf16[6144,1024]{1,0:T(8,128)(2,1)} %all-gather.9.cloned.1.call-done.grad_mixed, bf16[2048,1024]{1,0:T(8,128)(2,1)} %mix.1, ...), custom_call_target="tpu_custom_call" | custom-call | flops 4831838208 | bytes 18874368 | tf_op jit(solution)/shard_map/owner_table_grad/pallas_call | solution.py:314
  521.2 1.4 reduce_sum.108
  522.6 0.6 slice.83
  523.2 17.2 %all-gather.13.cloned.1.call-done = bf16[32,96,1024]{2,1,0:T(8,128)(2,1)} async-done(((bf16[1,96,1024]{2,1,0:T(8,128)(2,1)}), bf16[32,96,1024]{2,1,0:T(8,128)(2,1)}) %all-gather.13.cloned.1.call-update) | async-done | bytes 6291472 | tf_op jit(solution)/shard_map/all_gather | solution.py:491
  540.3 2.6 slice.84
  543.0 2.1 convert_bitcast_fusion
  545.0 4.7 bitcast_convert_fusion
  549.8 2.3 copy.50
  (56 shorter events, 0.6 us)
Async XLA Ops:
  8.0 123.7 %reduce-scatter.3.cloned.1.call-start = ((), (), s32[]{:S(2)}) async-start(), calls=%async_computation.4 | async-start | bytes 3538944 | tf_op jit(solution)/shard_map/reduce_scatter | solution.py:377
  38.6 0.8 copy-start.6
  38.6 0.8 copy-start.7
  38.6 0.9 copy-start.5
  38.6 14.6 %copy-start.8 = (pred[5376]{0:T(1024)(128)(4,1)S(1)}, pred[5376]{0:T(1024)(128)(4,1)}, u32[]{:S(2)}) copy-start(pred[5376]{0:T(1024)(128)(4,1)} %constant.29.clone.1) | copy-start | bytes 16132
  38.6 158.5 %reduce-scatter.5.cloned.1.call-start = ((), (), s32[]{:S(2)}) async-start(), calls=%async_computation.5 | async-start | bytes 7077888 | tf_op jit(solution)/shard_map/reduce_scatter | solution.py:436
  62.1 69.6 %copy-start = (f32[8,1,11136]{2,0,1:T(8,128)}, f32[8,1,11136]{2,0,1:T(8,128)S(1)}, u32[]{:S(2)}) copy-start(f32[8,1,11136]{2,0,1:T(8,128)S(1)} %copy.53) | copy-start | bytes 1069060
  131.7 66.6 %copy-start.3 = (bf16[192,1024]{1,0:T(8,128)(2,1)S(1)}, bf16[192,1024]{1,0:T(8,128)(2,1)}, u32[]{:S(2)}) copy-start(bf16[192,1024]{1,0:T(8,128)(2,1)} %param.17) | copy-start | bytes 1179652
  131.8 66.5 %copy-start.4 = (bf16[192,1024]{1,0:T(8,128)(2,1)S(1)}, bf16[192,1024]{1,0:T(8,128)(2,1)}, u32[]{:S(2)}) copy-start(bf16[192,1024]{1,0:T(8,128)(2,1)} %reduce-scatter.3.cloned.1.call-done) | copy-start | bytes 1179652
  131.8 66.5 %copy-start.9 = (f32[1024]{0:T(1024)S(1)}, f32[1024]{0:T(1024)}, u32[]{:S(2)}) copy-start(f32[1024]{0:T(1024)} %param.13) | copy-start | bytes 12292
  131.8 81.0 %all-gather.15.cloned.1.call-start = ((), (), s32[]{:S(2)}) async-start(), calls=%async_computation.9 | async-start | bytes 1781760 | tf_op jit(solution)/shard_map/all_gather | solution.py:416
  132.4 179.8 %all-gather.11.cloned.1.call-start = ((), (), s32[]{:S(2)}) async-start(), calls=%async_computation.7 | async-start | bytes 12976128 | tf_op jit(solution)/shard_map/all_gather | solution.py:452
  202.8 3.4 copy-start.1
  206.2 254.1 %all-gather.9.cloned.1.call-start = ((), (), s32[]{:S(2)}) async-start(), calls=%async_computation.6 | async-start | bytes 12976128 | tf_op jit(solution)/shard_map/all_gather | solution.py:453
  208.1 38.0 %all-to-all-start.1 = ((bf16[32,192,64]{1,2,0:T(8,128)(2,1)}), bf16[32,192,64]{1,2,0:T(8,128)(2,1)S(1)}, u32[]{:S(2)}, u32[]{:S(2)}) async-start(bf16[32,192,64]{1,2,0:T(8,128)(2,1)} %bitcast.15), calls=%async_computation.3 | async-start | bytes 2097152 | tf_op jit(solution)/shard_map/all_to_all | solution.py:455
  212.8 4.6 slice-start
  441.4 31.1 %all-to-all-start = ((bf16[8,48,1024]{2,1,0:T(8,128)(2,1)}), bf16[8,48,1024]{2,1,0:T(8,128)(2,1)S(1)}, u32[]{:S(2)}, u32[]{:S(2)}) async-start(bf16[8,48,1024]{2,1,0:T(8,128)(2,1)} %pad_maximum_fusion.1), calls=%async_computation.2 | async-start | bytes 1572864 | tf_op jit(solution)/shard_map/all_to_all | solution.py:485
  460.0 13.4 %copy-start.2 = (f32[32,11136]{1,0:T(8,128)S(1)}, f32[32,11136]{1,0:T(8,128)}, u32[]{:S(2)}) copy-start(f32[32,11136]{1,0:T(8,128)} %all-gather.15.cloned.1.call-done) | copy-start | bytes 4276228
  460.0 80.3 %all-gather.13.cloned.1.call-start = ((), (), s32[]{:S(2)}) async-start(), calls=%async_computation.8 | async-start | bytes 6488064 | tf_op jit(solution)/shard_map/all_gather | solution.py:491
Sparse Core Ops, SparseCore 0:
  38.7 45.8 reduce-scatter.2
  131.9 65.1 reduce-scatter.4
Sparse Core Ops, SparseCore 1:
  134.4 37.7 all-gather.14
  206.3 105.9 all-gather.10
  315.0 93.6 all-gather.8
  473.5 66.8 all-gather.12

commit v2 on v1

v2 whole, which is shorter than its diff:
```python
import functools

import jax
import jax.numpy as jnp
from jax import lax
from jax.experimental import pallas as pl
from jax.experimental.pallas import tpu as pltpu
from jax.sharding import PartitionSpec as P

F32 = jnp.float32
BF16 = jnp.bfloat16
I32 = jnp.int32
LANES = 128
SUBLANES = 8
ROW_BLOCK = 512
SHIFT = 256
PART_BLOCK = 384
WINDOW = 1536
UNROLL = 4
VMEM_BYTES = 60 << 20


def row_at(ref, row):
    return ref[pl.ds(pl.multiple_of(row * SUBLANES, SUBLANES), SUBLANES), :]


def put_row(ref, row, value):
    ref[pl.ds(pl.multiple_of(row * SUBLANES, SUBLANES), SUBLANES), :] = value


def clear_rows(ref, rows):
    zero = jnp.zeros((SUBLANES * SUBLANES, LANES), F32)

    def step(i, carry):
        ref[pl.ds(pl.multiple_of(i * SUBLANES * SUBLANES, SUBLANES), SUBLANES * SUBLANES), :] = zero
        return carry

    lax.fori_loop(0, rows // SUBLANES, step, 0)


def walk(first, last, entry):
    count = last - first
    groups = count // UNROLL

    def group(i, carry):
        for u in range(UNROLL):
            entry(first + i * UNROLL + u)
        return carry

    def single(k, carry):
        entry(k)
        return carry

    lax.fori_loop(0, groups, group, 0)
    lax.fori_loop(first + groups * UNROLL, last, single, 0)


def window_start(first, length):
    return pl.multiple_of(jnp.minimum(lax.div(first, LANES) * LANES, length - WINDOW), LANES)


def forward_kernel(blocks, length, bounds, table, query, bias, codes, shares, hidden, pooled, hidden_rows, pooled_rows):
    step = pl.program_id(0)
    width = table.shape[1]
    chunks = width // LANES
    sub = 128

    @pl.when(step < blocks)
    def _():
        def part(j, carry):
            start = pl.multiple_of(j * sub, sub)
            pre = jnp.dot(table[pl.ds(start, sub), :], query[...], preferred_element_type=F32) + bias[...]
            tiny = jnp.finfo(BF16).tiny
            kept = jnp.where(pre > 0, jnp.maximum(pre, tiny), 0.0).astype(BF16)
            hidden[pl.ds(start, sub), :] = kept
            wide = kept.astype(F32)
            base = (step * ROW_BLOCK + start) * SUBLANES
            for g in range(sub // SUBLANES):
                for c in range(chunks):
                    hidden_rows[pl.ds(base + g * SUBLANES * SUBLANES + c, SUBLANES, stride=SUBLANES), :] = wide[
                        g * SUBLANES : (g + 1) * SUBLANES, c * LANES : (c + 1) * LANES
                    ]
            return carry

        lax.fori_loop(0, ROW_BLOCK // sub, part, 0)

    @pl.when(step >= blocks)
    def _():
        device = step - blocks
        targets = pooled.shape[0]
        clear_rows(pooled_rows, targets)

        def entry(k):
            code = codes[0, 0, k]
            node = lax.shift_right_logical(code, 8)
            target = code & (SHIFT - 1)
            put_row(
                pooled_rows,
                target,
                row_at(pooled_rows, target) + shares[0, 0, k] * row_at(hidden_rows, node),
            )

        base = window_start(bounds[device, 0], length)
        walk(bounds[device, 0] - base, bounds[device, 1] - base, entry)

        def part(g, carry):
            for c in range(chunks):
                pooled[
                    pl.ds(pl.multiple_of(g * SUBLANES, SUBLANES), SUBLANES), c * LANES : (c + 1) * LANES
                ] = pooled_rows[pl.ds(g * SUBLANES * SUBLANES + c, SUBLANES, stride=SUBLANES), :]
            return carry

        lax.fori_loop(0, targets // SUBLANES, part, 0)


def owner_forward(table, query, bias, codes, shares, bounds, targets):
    rows, width = table.shape
    blocks = rows // ROW_BLOCK
    devices, _, length = codes.shape

    def list_block(i, bounds):
        k = jnp.maximum(i - blocks, 0)
        return (k, 0, window_start(bounds[k, 0], length))

    window = (pl.Element(1), pl.Element(1), pl.Element(WINDOW))
    return pl.pallas_call(
        functools.partial(forward_kernel, blocks, length),
        grid_spec=pltpu.PrefetchScalarGridSpec(
            num_scalar_prefetch=1,
            grid=(blocks + devices,),
            in_specs=[
                pl.BlockSpec((ROW_BLOCK, width), lambda i, b: (jnp.minimum(i, blocks - 1), 0)),
                pl.BlockSpec((width, width), lambda i, b: (0, 0)),
                pl.BlockSpec((1, width), lambda i, b: (0, 0)),
                pl.BlockSpec(window, list_block, memory_space=pltpu.SMEM),
                pl.BlockSpec(window, list_block, memory_space=pltpu.SMEM),
            ],
            out_specs=[
                pl.BlockSpec((ROW_BLOCK, width), lambda i, b: (jnp.minimum(i, blocks - 1), 0)),
                pl.BlockSpec((targets, width), lambda i, b: (jnp.maximum(i - blocks, 0), 0)),
            ],
            scratch_shapes=[
                pltpu.VMEM((rows * SUBLANES, LANES), F32),
                pltpu.VMEM((targets * SUBLANES, LANES), F32),
            ],
        ),
        out_shape=[
            jax.ShapeDtypeStruct((rows, width), BF16),
            jax.ShapeDtypeStruct((devices * targets, width), F32),
        ],
        compiler_params=pltpu.CompilerParams(vmem_limit_bytes=VMEM_BYTES),
        cost_estimate=pl.CostEstimate(
            flops=2 * rows * width * width, bytes_accessed=4 * rows * width, transcendentals=0
        ),
        name="owner_forward",
    )(bounds, table, query, bias.reshape(1, width), codes, shares)


def spread_rows(source, rows_here):
    targets, width = source.shape
    chunks = width // LANES
    tile = SUBLANES * SUBLANES

    def part(g, sums):
        both = source[pl.ds(pl.multiple_of(g * 16, 16), 16), :].astype(F32)
        for h in range(2):
            for c in range(chunks):
                rows_here[pl.ds((g * 2 + h) * tile + c, SUBLANES, stride=SUBLANES), :] = both[
                    h * SUBLANES : (h + 1) * SUBLANES, c * LANES : (c + 1) * LANES
                ]
        return sums + both[:SUBLANES] + both[SUBLANES:]

    return lax.fori_loop(0, targets // 16, part, jnp.zeros((SUBLANES, width), F32))


def backward_kernel(
    requesters,
    length,
    place,
    bounds,
    codes,
    shares,
    self_codes,
    grads,
    hidden,
    table,
    mix_self,
    mix_pooled,
    query,
    table_grad,
    weight_grad,
    query_bias_grad,
    mix_bias_grad,
    near_total,
    self_total,
    rows_here,
    near_sums,
    self_sums,
    weight_sum,
):
    step = pl.program_id(0)
    block, width = hidden.shape
    rows = near_total.shape[0] // SUBLANES
    chunks = width // LANES
    tile = SUBLANES * SUBLANES
    groups, _, part_width = table_grad.shape

    @pl.when(step == 0)
    def _():
        clear_rows(near_total, rows)
        clear_rows(self_total, rows)
        mix_bias_grad[...] = jnp.zeros_like(mix_bias_grad)
        query_bias_grad[...] = jnp.zeros_like(query_bias_grad)
        weight_sum[...] = jnp.zeros_like(weight_sum)

    @pl.when(step < requesters)
    def _():
        mix_bias_grad[...] += spread_rows(grads, rows_here)
        first_row = place[0] * rows

        def parts_of(code):
            return lax.shift_right_logical(code, 8) - first_row, code & (SHIFT - 1)

        base = window_start(bounds[step, 0], length)

        def entry(k):
            node, target = parts_of(codes[0, 0, k])
            put_row(near_total, node, row_at(near_total, node) + shares[0, 0, k] * row_at(rows_here, target))

        walk(bounds[step, 0] - base, bounds[step, 1] - base, entry)

        def self_entry(k):
            node, target = parts_of(self_codes[0, 0, k])
            put_row(self_total, node, row_at(self_total, node) + row_at(rows_here, target))

        walk(bounds[step, 2], bounds[step, 3], self_entry)

    @pl.when(step >= requesters)
    def _():
        base = (step - requesters) * (block // SUBLANES)

        def part(g, carry):
            where = pl.ds(pl.multiple_of(g * 16, 16), 16)
            for total, sums in ((near_total, near_sums), (self_total, self_sums)):
                for c in range(chunks):
                    halves = [
                        total[pl.ds((base + g * 2 + h) * tile + c, SUBLANES, stride=SUBLANES), :] for h in range(2)
                    ]
                    sums[where, c * LANES : (c + 1) * LANES] = jnp.concatenate(halves, axis=0).astype(BF16)
            return carry

        lax.fori_loop(0, block // 16, part, 0)
        turned = (((1,), (1,)), ((), ()))
        raw = lax.dot_general(near_sums[...], mix_pooled[...], turned, preferred_element_type=F32)
        grad_pre = jnp.where(hidden[...].astype(F32) > 0, raw, 0.0)
        query_bias_grad[...] += jnp.sum(grad_pre.reshape(block // SUBLANES, SUBLANES, width), axis=0)
        grad_pre = grad_pre.astype(BF16)
        weight_sum[...] += lax.dot_general(
            table[...], grad_pre, (((0,), (0,)), ((), ())), preferred_element_type=F32
        )
        grad = lax.dot_general(grad_pre, query[...], turned, preferred_element_type=F32) + lax.dot_general(
            self_sums[...], mix_self[...], turned, preferred_element_type=F32
        )
        for q in range(groups):
            table_grad[q] = grad[:, q * part_width : (q + 1) * part_width].astype(BF16)

    @pl.when(step == pl.num_programs(0) - 1)
    def _():
        weight_grad[...] = weight_sum[...].astype(BF16)


def owner_backward(table, hidden, grads, mix, query, codes, shares, self_codes, bounds, place, owners, groups, targets):
    rows_owned, width = table.shape
    rows = rows_owned // groups
    blocks = rows // PART_BLOCK
    requesters, _, length = codes.shape
    self_length = self_codes.shape[2]

    def requester(i):
        return jnp.minimum(i, requesters - 1)

    def node_block(i, place, bounds):
        return (place[0] * blocks + jnp.maximum(i - requesters, 0), 0)

    def list_block(i, place, bounds):
        k = requester(i)
        return (k, 0, window_start(bounds[k, 0], length))

    def grad_block(i, place, bounds):
        k = requester(i)
        return (lax.rem(k, owners) * groups + lax.div(k, owners), 0)

    def whole(shape, row=0):
        return pl.BlockSpec(shape, lambda i, place, bounds: (row, 0), pipeline_mode=pl.Buffered(1))

    window = (pl.Element(1), pl.Element(1), pl.Element(WINDOW))
    return pl.pallas_call(
        functools.partial(backward_kernel, requesters, length),
        grid_spec=pltpu.PrefetchScalarGridSpec(
            num_scalar_prefetch=2,
            grid=(requesters + blocks,),
            in_specs=[
                pl.BlockSpec(window, list_block, memory_space=pltpu.SMEM),
                pl.BlockSpec(window, list_block, memory_space=pltpu.SMEM),
                pl.BlockSpec(
                    (1, 1, self_length), lambda i, place, bounds: (requester(i), 0, 0), memory_space=pltpu.SMEM
                ),
                pl.BlockSpec((targets, width), grad_block),
                pl.BlockSpec((PART_BLOCK, width), node_block),
                pl.BlockSpec((PART_BLOCK, width), node_block),
                whole((width, width), 0),
                whole((width, width), 1),
                whole((width, width)),
            ],
            out_specs=[
                pl.BlockSpec(
                    (groups, PART_BLOCK, width // groups),
                    lambda i, place, bounds: (0, jnp.maximum(i - requesters, 0), 0),
                ),
                pl.BlockSpec((width, width), lambda i, place, bounds: (0, 0)),
                pl.BlockSpec((SUBLANES, width), lambda i, place, bounds: (0, 0)),
                pl.BlockSpec((SUBLANES, width), lambda i, place, bounds: (0, 0)),
            ],
            scratch_shapes=[
                pltpu.VMEM((rows * SUBLANES, LANES), F32),
                pltpu.VMEM((rows * SUBLANES, LANES), F32),
                pltpu.VMEM((targets * SUBLANES, LANES), F32),
                pltpu.VMEM((PART_BLOCK, width), BF16),
                pltpu.VMEM((PART_BLOCK, width), BF16),
                pltpu.VMEM((width, width), F32),
            ],
        ),
        out_shape=[
            jax.ShapeDtypeStruct((groups, rows, width // groups), BF16),
            jax.ShapeDtypeStruct((width, width), BF16),
            jax.ShapeDtypeStruct((SUBLANES, width), F32),
            jax.ShapeDtypeStruct((SUBLANES, width), F32),
        ],
        compiler_params=pltpu.CompilerParams(vmem_limit_bytes=VMEM_BYTES),
        cost_estimate=pl.CostEstimate(
            flops=8 * rows * width * width, bytes_accessed=4 * requesters * targets * width, transcendentals=0
        ),
        name="owner_backward",
    )(place, bounds, codes, shares, self_codes, grads, hidden, table, mix, mix, query)


def padded(values, length):
    return jnp.pad(values, (0, length - values.shape[0]))


def local(
    feature_table,
    neighbour_query_weight,
    query_bias,
    mix_weight,
    mix_bias,
    lookup_ids,
    present_counts,
    importance,
    embed_cot,
):
    owners = lax.axis_size("table")
    groups = lax.axis_size("rep")
    devices = owners * groups
    rows_owned, width = feature_table.shape
    batch_rows, slot_count = lookup_ids.shape
    near = slot_count - 1
    owner = lax.axis_index("table").astype(I32)
    group = lax.axis_index("rep").astype(I32)

    own_ids = lax.all_gather(lookup_ids[:, 0], "table", axis=0, tiled=True)
    wanted = own_ids - owner * rows_owned
    mine = (wanted >= 0) & (wanted < rows_owned)
    found = feature_table[jnp.clip(wanted, 0, rows_owned - 1)]
    found = jnp.where(mine[:, None], found, jnp.zeros((), BF16))
    self_rows = lax.psum_scatter(found, "table", scatter_dimension=0, tiled=True)

    present = (jnp.arange(near, dtype=I32)[None, :] < present_counts[:, None]).astype(F32)
    masked_weight = importance * present
    shares = lax.reduce_precision(masked_weight / jnp.sum(masked_weight, axis=1, keepdims=True), 8, 7)
    live_most = batch_rows // 2 * (near + 5)
    length = -(-live_most // LANES) * LANES
    target = jnp.arange(batch_rows, dtype=I32)
    keys = jnp.where(present > 0, lookup_ids[:, 1:] * SHIFT + target[:, None], jnp.iinfo(I32).max)
    keys, sorted_shares = lax.sort((keys.reshape(-1), shares.reshape(-1)), num_keys=1, is_stable=False)
    keys = keys[:live_most]
    sorted_shares = sorted_shares[:live_most]
    own_keys = lax.sort(lookup_ids[:, 0] * SHIFT + target)
    edges = jnp.arange(devices + 1, dtype=I32) * (rows_owned // groups * SHIFT)
    starts = jnp.sum((keys[None, :] < edges[:, None]).astype(I32), axis=1)
    own_starts = jnp.sum((own_keys[None, :] < edges[:, None]).astype(I32), axis=1)
    own_length = SHIFT
    meta = jnp.concatenate(
        [
            starts.astype(F32),
            own_starts.astype(F32),
            jnp.stack([jnp.sum(present), jnp.sum(masked_weight)]),
        ]
    )
    meta_length = -(-meta.shape[0] // LANES) * LANES

    def as_code(key):
        return (key % (rows_owned * SHIFT)).astype(F32)

    request = jnp.concatenate(
        [
            padded(as_code(keys), length),
            padded(sorted_shares, length),
            padded(as_code(own_keys), own_length),
            padded(meta, meta_length),
        ]
    )
    request, _ = lax.optimization_barrier((request, found))
    plane = lax.all_gather(request, "table", axis=0)
    every = lax.all_gather(plane, "rep", axis=0).reshape(devices, -1)

    def unpack(lists, start, stride):
        count = lists.shape[0]
        at = 2 * length
        codes = lists[:, :length].astype(I32).reshape(count, 1, length)
        parts = lists[:, length:at].reshape(count, 1, length)
        own_codes = lists[:, at : at + own_length].astype(I32).reshape(count, 1, own_length)
        notes = lists[:, at + own_length :]
        first = lax.dynamic_slice(notes, (0, start), (count, stride + 1))[:, ::stride]
        own_first = lax.dynamic_slice(notes, (0, start + devices + 1), (count, stride + 1))[:, ::stride]
        bounds = jnp.concatenate([first, own_first], axis=1).astype(I32)
        sums = jnp.sum(notes[:, 2 * (devices + 1) : 2 * (devices + 1) + 2], axis=0)
        return codes, parts, own_codes, bounds, sums

    codes, parts, _, bounds, _ = unpack(plane, owner * groups, groups)
    hidden, pooled_parts = owner_forward(
        feature_table, neighbour_query_weight, query_bias, codes, parts, bounds, batch_rows
    )
    pooled_parts, self_rows = lax.optimization_barrier((pooled_parts, self_rows))
    pooled = lax.psum_scatter(pooled_parts, "table", scatter_dimension=0, tiled=True)
    pooled = lax.reduce_precision(pooled, 8, 7).astype(BF16)

    joined = jnp.concatenate([self_rows, pooled], axis=1)
    mixed = jnp.dot(joined, mix_weight, preferred_element_type=F32) + mix_bias
    activation = jax.nn.relu(mixed)
    inverse = lax.rsqrt(jnp.mean(activation * activation, axis=1, keepdims=True) + 1e-06)
    embed = (activation * inverse).astype(BF16)
    cotangent = embed_cot.astype(F32)
    grad_act = inverse * cotangent - activation * (inverse * inverse * inverse) * jnp.mean(
        activation * cotangent, axis=1, keepdims=True
    )
    grad_mixed = jnp.where(mixed > 0, grad_act, 0.0).astype(BF16)
    all_mixed = lax.all_gather(grad_mixed, ("table", "rep"), axis=0, tiled=True)
    mix_part = 2 * width // devices
    columns = lax.all_to_all(
        joined.reshape(batch_rows, devices, mix_part).transpose(1, 0, 2),
        ("table", "rep"),
        split_axis=0,
        concat_axis=0,
        tiled=True,
    ).reshape(devices * batch_rows, mix_part)

    mix_rows = lax.dot_general(
        columns, all_mixed, (((0,), (0,)), ((), ())), preferred_element_type=F32
    ).astype(BF16)
    mix_weight_grad = lax.all_gather(mix_rows, ("table", "rep"), axis=0, tiled=True).astype(F32)

    all_codes, all_parts, all_own_codes, all_bounds, sums = unpack(every, owner * groups + group, 1)
    place = group.reshape(1)
    table_part, query_part, query_bias_part, mix_bias_part = owner_backward(
        feature_table,
        hidden,
        all_mixed,
        mix_weight,
        neighbour_query_weight,
        all_codes,
        all_parts,
        all_own_codes,
        all_bounds,
        place,
        owners,
        groups,
        batch_rows,
    )
    mix_bias_grad = jnp.sum(mix_bias_part, axis=0)

    query_rows = width // devices
    bias_rows = 16
    incoming = lax.all_to_all(
        query_part.reshape(devices, query_rows, width), ("table", "rep"), split_axis=0, concat_axis=0, tiled=True
    )
    summed = jnp.sum(incoming.astype(F32), axis=0)
    bias_part = jnp.pad(jnp.sum(query_bias_part, axis=0, keepdims=True), ((0, bias_rows - 1), (0, 0)))
    gathered = lax.all_gather(
        jnp.concatenate([summed, bias_part], axis=0).astype(BF16), ("table", "rep"), axis=0
    ).astype(F32)
    query_weight_grad = gathered[:, :query_rows].reshape(width, width)
    query_bias_grad = jnp.sum(gathered[:, query_rows], axis=0)
    table_grad = lax.all_to_all(table_part, "rep", split_axis=0, concat_axis=0, tiled=True)
    table_grad = table_grad.reshape(rows_owned, width // groups).astype(F32)
    statistics = sums / (batch_rows * devices)
    return (
        embed,
        table_grad,
        query_weight_grad,
        query_bias_grad,
        mix_weight_grad,
        mix_bias_grad,
        statistics,
    )


def solution(mesh):
    in_specs = (
        P("table", None),
        P(),
        P(),
        P(),
        P(),
        P(("table", "rep"), None),
        P(("table", "rep")),
        P(("table", "rep"), None),
        P(("table", "rep"), None),
    )
    out_specs = (P(("table", "rep"), None), P("table", "rep"), P(), P(), P(), P(), P())
    return jax.shard_map(local, mesh=mesh, in_specs=in_specs, out_specs=out_specs, check_vma=False)
```

time: 566 us -> 604 us (1.067)
  Pallas kernels: 240 us -> 135 us
  waiting for transfers between devices: 180 us -> 281 us
  blocking collectives: 18.5 us -> 73.7 us
  starting transfers between devices: 23.8 us -> 10.1 us
  other arithmetic: 33.8 us -> 42.4 us
    all_to_all x1, waiting for transfers between devices: 5.26 us -> 114 us  [local(): lax.all_to_all(table_part, 'rep', split_axis=0, concat_axis=0, tiled=True)]
    pallas_call x3 -> x2, Pallas kernels: 240 us -> 135 us  [the longest x1 72.2 us: owner_backward(): pl.pallas_call(functools.partial(backward_kernel, requesters, length), gr...]
    all_gather x2, waiting for transfers between devices: 81.5 us -> 0.01 us  [the longest x1 0.01 us: local(): lax.all_gather(mix_rows, ('table', 'rep'), axis=0, tiled=True).astype(F32)]
    all_gather x1, waiting for transfers between devices: 0.03 us -> 65.2 us  [local(): all_mixed = lax.all_gather(grad_mixed, ('table', 'rep'), axis=0, tiled=True)]
    all_to_all x0 -> x1, blocking collectives: none -> 55.1 us  [local(): lax.all_to_all(query_part.reshape(devices, query_rows, width), ('table',...]
    all_to_all x1, starting transfers between devices: 18.6 us -> 5.06 us  [local(): lax.all_to_all(table_part, 'rep', split_axis=0, concat_axis=0, tiled=True)]
    reduce_scatter x1, waiting for transfers between devices: 64.7 us -> 74.3 us  [local(): lax.psum_scatter(pooled_parts, 'table', scatter_dimension=0, tiled=True)]
    convert_element_type x2 -> x3, other arithmetic: 6.79 us -> 15.2 us  [the longest x1 6.63 us: local(): lax.all_gather(mix_rows, ('table', 'rep'), axis=0, tiled=True).astype(F32)]
  transfers between devices with their start and end apart: 8 -> 8, of which waited for: 5 -> 4; matrix products, arithmetic and copies ran while one was open for 8% -> 8% of each run, Pallas kernels for 43% -> 22%
where the time goes in v2:
time: 604 us; the launch traced here: 601 us
  waiting for transfers between devices  281 us (47%)
  Pallas kernels  135 us (22%)
  blocking collectives  73.7 us (12%)
  other arithmetic  42.4 us (7%)
  local copies, waits for them, and re-layouts  30.7 us (5%)
  between operations  16.7 us (3%)
  matrix products  10.9 us (2%)
  starting transfers between devices  10.1 us (2%)
    all_to_all x1, waiting for transfers between devices, local(): lax.all_to_all(table_part, 'rep', split_axis=0, concat_axis=0, tiled=True)  114 us
    reduce_scatter x1, waiting for transfers between devices, local(): lax.psum_scatter(pooled_parts, 'table', scatter_dimension=0, tiled=True)  74.3 us
    pallas_call x1, Pallas kernels, owner_backward(): pl.pallas_call(functools.partial(backward_kernel, requesters, length), gr...  72.2 us
    all_gather x1, waiting for transfers between devices, local(): all_mixed = lax.all_gather(grad_mixed, ('table', 'rep'), axis=0, tiled=True)  65.2 us
    pallas_call x1, Pallas kernels, owner_forward(): pl.pallas_call(functools.partial(forward_kernel, blocks, length), grid_sp...  62.6 us
    all_to_all x1, blocking collectives, local(): lax.all_to_all(query_part.reshape(devices, query_rows, width), ('table',...  55.1 us
    all_to_all x1, waiting for transfers between devices, local(): lax.all_to_all(joined.reshape(batch_rows, devices, mix_part).transpose(1,...  27.2 us
    gather x1, local copies, waits for them, and re-layouts, local(): found = feature_table[jnp.clip(wanted, 0, rows_owned - 1)]  15.9 us
  transfers between devices with their start and end apart: 8, of which 4 were waited for; matrix products, arithmetic and copies ran while one was open for 8% of the time, Pallas kernels for 22%

profile of v2, /device:TPU:0, one launch (start us, length us, event | category | flops | bytes accessed | tf_op | source)
XLA Modules:
  0.0 600.6 jit_solution(3803010001291508443)
XLA Ops:
  8.1 0.7 fusion.13
  8.8 1.2 dynamic-slice
  10.7 0.3 dynamic-update-slice
  10.9 9.6 %all-reduce.4 = s32[1536]{0:T(1024)S(1)} all-reduce(s32[1536]{0:T(1024)S(1)} %dynamic-update-slice), channel_id=2, replica_groups=mesh['table'=8,'rep'=4] {'table'}, use_global_device_ids=true, to_apply=%add.4 | all-reduce | flops 1536 | bytes 12288
  20.6 15.9 %gather_fusion = bf16[1536,1024]{1,0:T(8,128)(2,1)S(1)} fusion(bf16[9216,1024]{1,0:T(8,128)(2,1)} %table.3, s32[2048]{0:T(1024)S(1)} %pad_clamp_fusion), kind=kCustom, calls=%fused_computation | custom fusion | bytes 6297600 | tf_op jit(solution)/shard_map/gather | solution.py:374
  36.5 2.1 broadcast_select_fusion
  38.6 0.0 reduce-scatter.5.cloned.1.call-start
  38.7 0.7 copy-done.7
  39.4 0.6 fusion.9
  40.1 3.2 sort.30
  43.3 0.2 convert_reduce_fusion.2
  43.4 0.1 copy.40
  43.5 0.1 reshape.119
  43.7 0.1 copy.39
  43.8 0.1 reshape.118
  43.9 7.5 %sort.29 = (s32[9600]{0:T(1024)S(1)}, f32[9600]{0:T(1024)S(1)}) sort(s32[9600]{0:T(1024)S(1)} %reshape.118, f32[9600]{0:T(1024)S(1)} %reshape.119), dimensions={0}, to_apply=%region_1.2 | sort | flops 134400 | bytes 153600 | tf_op jit(solution)/shard_map/sort | solution.py:385
  51.5 0.3 convert_reduce_fusion
  51.8 1.4 select_maximum_fusion.2
  53.3 9.1 %all-gather.3 = f32[8,1,11136]{2,1,0:T(1,128)S(1)} all-gather(f32[1,1,11136]{2,1,0:T(1,128)S(1)} %reshape.161), channel_id=3, replica_groups=mesh['table'=8,'rep'=4] {'table'}, dimensions={0}, use_global_device_ids=true | all-gather | bytes 400896 | tf_op jit(solution)/shard_map/all_gather | solution.py:414
  62.4 0.9 copy.42.shares
  63.3 0.1 constant_dynamic-slice_fusion.3
  63.3 0.1 slice.56
  63.4 0.1 slice.57
  63.5 0.8 copy.41.codes
  64.3 0.7 maximum_convert_fusion.1.bounds
  65.0 62.6 %owner_forward.1 = (bf16[9216,1024]{1,0:T(8,128)(2,1)}, f32[1536,1024]{1,0:T(8,128)}) custom-call(s32[8,4]{1,0:T(8,128)} %maximum_convert_fusion.1.bounds, bf16[9216,1024]{1,0:T(8,128)(2,1)} %table.3, bf16[1024,1024]{1,0:T(8,128)(2,1)} %query.3, f32[1,1024]{1,0:T(1,128)} %bitcast.42, s32[8,1,5376]{2,1,0:T(1,128)} %copy.41.codes, f32[8,1,5376]{2,1,0:T(1,128)} %copy.42.shares), custom_call_target="tpu_custom_call" | custom-call | flops 19327352832 | bytes 37748736 | tf_op jit(solution)/shard_map/owner_forward/pallas_call | solution.py:126
  127.7 0.0 all-gather.15.cloned.1.call-start
  127.7 0.5 all-gather.15.cloned.1.call-update
  128.3 74.3 %reduce-scatter.5.cloned.1.call-done = f32[192,1024]{1,0:T(8,128)} async-done(((f32[1536,1024]{1,0:T(8,128)}), f32[192,1024]{1,0:T(8,128)}) %reduce-scatter.5.cloned.1.call-update) | async-done | bytes 786448 | tf_op jit(solution)/shard_map/reduce_scatter | solution.py:435
  202.6 1.2 reduce-precision_convert_fusion
  203.8 3.4 fusion.3
  207.2 1.3 fusion.2
  208.5 0.1 pad_maximum_fusion
  208.5 1.3 copy.45
  209.8 4.6 all-to-all-start.2
  214.4 0.0 all-gather.13.cloned.1.call-start
  214.6 1.5 slice_bitcast_fusion
  216.1 1.6 copy.44.shares
  217.7 0.6 reshape.127.self_codes
  218.3 1.6 copy.43.codes
  219.8 0.1 constant_dynamic-slice_fusion.1
  219.9 0.7 maximum_convert_fusion.bounds
  220.6 27.2 %all-to-all-done.2 = bf16[32,192,64]{1,2,0:T(8,128)(2,1)S(1)} async-done(((bf16[32,192,64]{1,2,0:T(8,128)(2,1)}), bf16[32,192,64]{1,2,0:T(8,128)(2,1)S(1)}, u32[]{:S(2)}, u32[]{:S(2)}) %all-to-all-start.2) | async-done | bytes 786464 | tf_op jit(solution)/shard_map/all_to_all | solution.py:450
  247.8 0.6 copy.46
  248.4 1.1 reshape.131
  249.5 65.2 %all-gather.9.cloned.1.call-done.grads = bf16[6144,1024]{1,0:T(8,128)(2,1)} async-done(((bf16[192,1024]{1,0:T(8,128)(2,1)}), bf16[6144,1024]{1,0:T(8,128)(2,1)}) %all-gather.9.cloned.1.call-update) | async-done | bytes 12582928 | tf_op jit(solution)/shard_map/all_gather | solution.py:448
  314.7 7.5 %convolution_convert_fusion = bf16[64,1024]{1,0:T(8,128)(2,1)} fusion(bf16[6144,64]{0,1:T(8,128)(2,1)S(1)} %reshape.131, bf16[6144,1024]{1,0:T(8,128)(2,1)} %all-gather.9.cloned.1.call-done.grads), kind=kOutput, calls=%fused_computation.4 | convolution fusion | flops 805371904 | bytes 13500416 | tf_op jit(solution)/shard_map/dot_general | solution.py:458
  322.3 72.2 %owner_backward.1 = (bf16[4,2304,256]{2,1,0:T(8,128)(2,1)}, bf16[1024,1024]{1,0:T(8,128)(2,1)}, f32[8,1024]{1,0:T(8,128)}, f32[8,1024]{1,0:T(8,128)}) custom-call(s32[1]{0:T(128)} %bitcast.8.place, s32[32,4]{1,0:T(8,128)} %maximum_convert_fusion.bounds, s32[32,1,5376]{2,1,0:T(1,128)} %copy.43.codes, f32[32,1,5376]{2,1,0:T(1,128)} %copy.44.shares, ...), custom_call_target="tpu_custom_call" | custom-call | flops 19327352832 | bytes 25165824 | tf_op jit(solution)/shard_map/owner_backward/pallas_call | solution.py:297
  394.5 55.1 %all_to_all.15 = bf16[32,32,1024]{2,1,0:T(8,128)(2,1)S(1)} all-to-all(bf16[32,32,1024]{2,1,0:T(8,128)(2,1)} %bitcast.38), channel_id=1, replica_groups=mesh['table'=8,'rep'=4] {'table','rep'}, dimensions={0} | all-to-all | bytes 4194304 | tf_op jit(solution)/shard_map/all_to_all | solution.py:484
  449.6 5.1 all-to-all-start
  454.6 0.3 all-gather.11.cloned.1.call-start
  454.9 0.6 reduce_sum.116
  455.5 0.7 broadcast_in_dim.41
  456.2 1.0 reduce.1
  457.2 1.5 pad_maximum_fusion.1
  458.8 0.1 slice_reduce_fusion.1
  458.8 0.5 broadcast_multiply_fusion.2
  459.4 1.4 reduce_sum.118
  460.7 113.9 %all-to-all-done = bf16[4,2304,256]{2,1,0:T(8,128)(2,1)} async-done(((bf16[4,2304,256]{2,1,0:T(8,128)(2,1)}), bf16[4,2304,256]{2,1,0:T(8,128)(2,1)}, u32[]{:S(2)}, u32[]{:S(2)}) %all-to-all-start) | async-done | bytes 4718624 | tf_op jit(solution)/shard_map/all_to_all | solution.py:494
  574.6 5.8 bitcast_convert_fusion
  580.4 6.6 %convert_element_type.104 = f32[2048,1024]{1,0:T(8,128)} convert(bf16[2048,1024]{1,0:T(8,128)(2,1)} %all-gather.13.cloned.1.call-done) | non-fusion elementwise | flops 2097152 | bytes 12582912 | tf_op jit(solution)/shard_map/convert_element_type | solution.py:461
  587.0 2.8 convert_element_type.102
  589.8 0.7 slice_reduce_fusion
  590.5 2.5 slice.76
  (58 shorter events, 0.5 us)
Async XLA Ops:
  8.0 119.6 %reduce-scatter.3.cloned.1.call-start = ((), (), s32[]{:S(2)}) async-start(), calls=%async_computation.5 | async-start | bytes 3538944 | tf_op jit(solution)/shard_map/reduce_scatter | solution.py:376
  38.6 0.8 copy-start.7
  38.6 0.8 copy-start.9
  38.6 0.9 copy-start.6
  38.6 14.6 %copy-start.10 = (pred[5376]{0:T(1024)(128)(4,1)S(1)}, pred[5376]{0:T(1024)(128)(4,1)}, u32[]{:S(2)}) copy-start(pred[5376]{0:T(1024)(128)(4,1)} %constant.32.clone.1) | copy-start | bytes 16132
  38.6 164.0 %reduce-scatter.5.cloned.1.call-start = ((), (), s32[]{:S(2)}) async-start(), calls=%async_computation.6 | async-start | bytes 7077888 | tf_op jit(solution)/shard_map/reduce_scatter | solution.py:435
  62.4 65.2 %copy-start.1 = (f32[8,1,11136]{2,0,1:T(8,128)}, f32[8,1,11136]{2,0,1:T(8,128)S(1)}, u32[]{:S(2)}) copy-start(f32[8,1,11136]{2,0,1:T(8,128)S(1)} %copy.49) | copy-start | bytes 1069060
  127.6 76.2 %copy-start.4 = (bf16[192,1024]{1,0:T(8,128)(2,1)S(1)}, bf16[192,1024]{1,0:T(8,128)(2,1)}, u32[]{:S(2)}) copy-start(bf16[192,1024]{1,0:T(8,128)(2,1)} %param.17) | copy-start | bytes 1179652
  127.6 76.2 %copy-start.5 = (bf16[192,1024]{1,0:T(8,128)(2,1)S(1)}, bf16[192,1024]{1,0:T(8,128)(2,1)}, u32[]{:S(2)}) copy-start(bf16[192,1024]{1,0:T(8,128)(2,1)} %reduce-scatter.3.cloned.1.call-done) | copy-start | bytes 1179652
  127.6 76.2 %copy-start.11 = (f32[1024]{0:T(1024)S(1)}, f32[1024]{0:T(1024)}, u32[]{:S(2)}) copy-start(f32[1024]{0:T(1024)} %param.13) | copy-start | bytes 12292
  127.7 86.8 %all-gather.15.cloned.1.call-start = ((), (), s32[]{:S(2)}) async-start(), calls=%async_computation.10 | async-start | bytes 1781760 | tf_op jit(solution)/shard_map/all_gather | solution.py:415
  128.3 186.4 %all-gather.9.cloned.1.call-start = ((), (), s32[]{:S(2)}) async-start(), calls=%async_computation.7 | async-start | bytes 12976128 | tf_op jit(solution)/shard_map/all_gather | solution.py:448
  209.8 38.0 %all-to-all-start.2 = ((bf16[32,192,64]{1,2,0:T(8,128)(2,1)}), bf16[32,192,64]{1,2,0:T(8,128)(2,1)S(1)}, u32[]{:S(2)}, u32[]{:S(2)}) async-start(bf16[32,192,64]{1,2,0:T(8,128)(2,1)} %bitcast.17), calls=%async_computation.4 | async-start | bytes 2097152 | tf_op jit(solution)/shard_map/all_to_all | solution.py:450
  214.4 365.9 %all-gather.13.cloned.1.call-start = ((), (), s32[]{:S(2)}) async-start(), calls=%async_computation.9 | async-start | bytes 4325376 | tf_op jit(solution)/shard_map/all_gather | solution.py:461
  214.5 3.1 copy-start.2
  214.5 5.3 slice-start
  449.6 5.4 copy-start.8
  449.6 9.2 %copy-start.3 = (f32[32,11136]{1,0:T(8,128)S(1)}, f32[32,11136]{1,0:T(8,128)}, u32[]{:S(2)}) copy-start(f32[32,11136]{1,0:T(8,128)} %all-gather.15.cloned.1.call-done) | copy-start | bytes 4276228
  449.6 125.0 %all-to-all-start = ((bf16[4,2304,256]{2,1,0:T(8,128)(2,1)}), bf16[4,2304,256]{2,1,0:T(8,128)(2,1)}, u32[]{:S(2)}, u32[]{:S(2)}) async-start(bf16[4,2304,256]{2,1,0:T(8,128)(2,1)} %get-tuple-element.28), calls=%async_computation.2 | async-start | bytes 9437184 | tf_op jit(solution)/shard_map/all_to_all | solution.py:494
  454.6 132.4 %all-gather.11.cloned.1.call-start = ((), (), s32[]{:S(2)}) async-start(), calls=%async_computation.8 | async-start | bytes 3244032 | tf_op jit(solution)/shard_map/all_gather | solution.py:489
  587.0 3.5 copy-start
Sparse Core Ops, SparseCore 0:
  38.7 45.8 reduce-scatter.2
  127.8 74.7 reduce-scatter.4
Sparse Core Ops, SparseCore 1:
  130.3 47.2 all-gather.14
  208.6 106.1 all-gather.8
  322.3 60.3 all-gather.12
  458.9 108.5 all-gather.10

commit v3 on v2

--- a/solution.py
+++ b/solution.py
@@ -14,7 +14,7 @@
 SUBLANES = 8
 ROW_BLOCK = 512
 SHIFT = 256
-PART_BLOCK = 384
+SPLIT = 2
 WINDOW = 1536
 UNROLL = 4
 VMEM_BYTES = 60 << 20
@@ -183,12 +183,17 @@
     self_codes,
     grads,
     hidden,
-    table,
-    mix_self,
+    table_own,
+    table_other,
+    self_own,
+    self_other,
     mix_pooled,
-    query,
+    query_own,
+    query_other,
     table_grad,
+    table_send,
     weight_grad,
+    weight_send,
     query_bias_grad,
     mix_bias_grad,
     near_total,
@@ -203,7 +208,6 @@
     rows = near_total.shape[0] // SUBLANES
     chunks = width // LANES
     tile = SUBLANES * SUBLANES
-    groups, _, part_width = table_grad.shape
 
     @pl.when(step == 0)
     def _():
@@ -211,12 +215,13 @@
         clear_rows(self_total, rows)
         mix_bias_grad[...] = jnp.zeros_like(mix_bias_grad)
         query_bias_grad[...] = jnp.zeros_like(query_bias_grad)
+        weight_grad[...] = jnp.zeros_like(weight_grad)
         weight_sum[...] = jnp.zeros_like(weight_sum)
 
     @pl.when(step < requesters)
     def _():
         mix_bias_grad[...] += spread_rows(grads, rows_here)
-        first_row = place[0] * rows
+        first_row = lax.rem(place[0], SPLIT) * rows
 
         def parts_of(code):
             return lax.shift_right_logical(code, 8) - first_row, code & (SHIFT - 1)
@@ -255,32 +260,35 @@
         grad_pre = jnp.where(hidden[...].astype(F32) > 0, raw, 0.0)
         query_bias_grad[...] += jnp.sum(grad_pre.reshape(block // SUBLANES, SUBLANES, width), axis=0)
         grad_pre = grad_pre.astype(BF16)
-        weight_sum[...] += lax.dot_general(
-            table[...], grad_pre, (((0,), (0,)), ((), ())), preferred_element_type=F32
-        )
-        grad = lax.dot_general(grad_pre, query[...], turned, preferred_element_type=F32) + lax.dot_general(
-            self_sums[...], mix_self[...], turned, preferred_element_type=F32
-        )
-        for q in range(groups):
-            table_grad[q] = grad[:, q * part_width : (q + 1) * part_width].astype(BF16)
+        down = (((0,), (0,)), ((), ()))
+        weight_grad[...] += lax.dot_general(table_own[...], grad_pre, down, preferred_element_type=F32)
+        weight_sum[...] += lax.dot_general(table_other[...], grad_pre, down, preferred_element_type=F32)
+        table_grad[...] = lax.dot_general(
+            grad_pre, query_own[...], turned, preferred_element_type=F32
+        ) + lax.dot_general(self_sums[...], self_own[...], turned, preferred_element_type=F32)
+        table_send[...] = (
+            lax.dot_general(grad_pre, query_other[...], turned, preferred_element_type=F32)
+            + lax.dot_general(self_sums[...], self_other[...], turned, preferred_element_type=F32)
+        ).astype(BF16)
 
     @pl.when(step == pl.num_programs(0) - 1)
     def _():
-        weight_grad[...] = weight_sum[...].astype(BF16)
+        weight_send[...] = weight_sum[...].astype(BF16)
 
 
 def owner_backward(table, hidden, grads, mix, query, codes, shares, self_codes, bounds, place, owners, groups, targets):
     rows_owned, width = table.shape
-    rows = rows_owned // groups
-    blocks = rows // PART_BLOCK
+    rows = rows_owned // SPLIT
+    blocks = rows // ROW_BLOCK
     requesters, _, length = codes.shape
     self_length = self_codes.shape[2]
+    part = width // groups
 
     def requester(i):
         return jnp.minimum(i, requesters - 1)
 
-    def node_block(i, place, bounds):
-        return (place[0] * blocks + jnp.maximum(i - requesters, 0), 0)
+    def node_row(i, place):
+        return lax.rem(place[0], SPLIT) * blocks + jnp.maximum(i - requesters, 0)
 
     def list_block(i, place, bounds):
         k = requester(i)
@@ -290,8 +298,16 @@
         k = requester(i)
         return (lax.rem(k, owners) * groups + lax.div(k, owners), 0)
 
-    def whole(shape, row=0):
-        return pl.BlockSpec(shape, lambda i, place, bounds: (row, 0), pipeline_mode=pl.Buffered(1))
+    def weights(which):
+        return pl.BlockSpec(
+            (part, width), lambda i, place, bounds: (place[which], 0), pipeline_mode=pl.Buffered(1)
+        )
+
+    def table_columns(which):
+        return pl.BlockSpec((ROW_BLOCK, part), lambda i, place, bounds: (node_row(i, place), place[which]))
+
+    def fixed(shape):
+        return pl.BlockSpec(shape, lambda i, place, bounds: (0, 0))
 
     window = (pl.Element(1), pl.Element(1), pl.Element(WINDOW))
     return pl.pallas_call(
@@ -306,33 +322,37 @@
                     (1, 1, self_length), lambda i, place, bounds: (requester(i), 0, 0), memory_space=pltpu.SMEM
                 ),
                 pl.BlockSpec((targets, width), grad_block),
-                pl.BlockSpec((PART_BLOCK, width), node_block),
-                pl.BlockSpec((PART_BLOCK, width), node_block),
-                whole((width, width), 0),
-                whole((width, width), 1),
-                whole((width, width)),
+                pl.BlockSpec((ROW_BLOCK, width), lambda i, place, bounds: (node_row(i, place), 0)),
+                table_columns(0),
+                table_columns(1),
+                weights(0),
+                weights(1),
+                pl.BlockSpec((width, width), lambda i, place, bounds: (1, 0), pipeline_mode=pl.Buffered(1)),
+                weights(0),
+                weights(1),
             ],
             out_specs=[
-                pl.BlockSpec(
-                    (groups, PART_BLOCK, width // groups),
-                    lambda i, place, bounds: (0, jnp.maximum(i - requesters, 0), 0),
-                ),
-                pl.BlockSpec((width, width), lambda i, place, bounds: (0, 0)),
-                pl.BlockSpec((SUBLANES, width), lambda i, place, bounds: (0, 0)),
-                pl.BlockSpec((SUBLANES, width), lambda i, place, bounds: (0, 0)),
+                pl.BlockSpec((ROW_BLOCK, part), lambda i, place, bounds: (node_row(i, place), 0)),
+                pl.BlockSpec((ROW_BLOCK, part), lambda i, place, bounds: (jnp.maximum(i - requesters, 0), 0)),
+                fixed((part, width)),
+                fixed((part, width)),
+                fixed((SUBLANES, width)),
+                fixed((SUBLANES, width)),
             ],
             scratch_shapes=[
                 pltpu.VMEM((rows * SUBLANES, LANES), F32),
                 pltpu.VMEM((rows * SUBLANES, LANES), F32),
                 pltpu.VMEM((targets * SUBLANES, LANES), F32),
-                pltpu.VMEM((PART_BLOCK, width), BF16),
-                pltpu.VMEM((PART_BLOCK, width), BF16),
-                pltpu.VMEM((width, width), F32),
+                pltpu.VMEM((ROW_BLOCK, width), BF16),
+                pltpu.VMEM((ROW_BLOCK, width), BF16),
+                pltpu.VMEM((part, width), F32),
             ],
         ),
         out_shape=[
-            jax.ShapeDtypeStruct((groups, rows, width // groups), BF16),
-            jax.ShapeDtypeStruct((width, width), BF16),
+            jax.ShapeDtypeStruct((rows_owned, part), F32),
+            jax.ShapeDtypeStruct((rows, part), BF16),
+            jax.ShapeDtypeStruct((part, width), F32),
+            jax.ShapeDtypeStruct((part, width), BF16),
             jax.ShapeDtypeStruct((SUBLANES, width), F32),
             jax.ShapeDtypeStruct((SUBLANES, width), F32),
         ],
@@ -341,7 +361,22 @@
             flops=8 * rows * width * width, bytes_accessed=4 * requesters * targets * width, transcendentals=0
         ),
         name="owner_backward",
-    )(place, bounds, codes, shares, self_codes, grads, hidden, table, mix, mix, query)
+    )(
+        place,
+        bounds,
+        codes,
+        shares,
+        self_codes,
+        grads,
+        hidden,
+        table,
+        table,
+        mix,
+        mix,
+        mix,
+        query,
+        query,
+    )
 
 
 def padded(values, length):
@@ -386,7 +421,7 @@
     keys = keys[:live_most]
     sorted_shares = sorted_shares[:live_most]
     own_keys = lax.sort(lookup_ids[:, 0] * SHIFT + target)
-    edges = jnp.arange(devices + 1, dtype=I32) * (rows_owned // groups * SHIFT)
+    edges = jnp.arange(owners * SPLIT + 1, dtype=I32) * (rows_owned // SPLIT * SHIFT)
     starts = jnp.sum((keys[None, :] < edges[:, None]).astype(I32), axis=1)
     own_starts = jnp.sum((own_keys[None, :] < edges[:, None]).astype(I32), axis=1)
     own_length = SHIFT
@@ -422,12 +457,12 @@
         own_codes = lists[:, at : at + own_length].astype(I32).reshape(count, 1, own_length)
         notes = lists[:, at + own_length :]
         first = lax.dynamic_slice(notes, (0, start), (count, stride + 1))[:, ::stride]
-        own_first = lax.dynamic_slice(notes, (0, start + devices + 1), (count, stride + 1))[:, ::stride]
+        own_first = lax.dynamic_slice(notes, (0, start + owners * SPLIT + 1), (count, stride + 1))[:, ::stride]
         bounds = jnp.concatenate([first, own_first], axis=1).astype(I32)
-        sums = jnp.sum(notes[:, 2 * (devices + 1) : 2 * (devices + 1) + 2], axis=0)
+        sums = jnp.sum(notes[:, 2 * (owners * SPLIT + 1) : 2 * (owners * SPLIT + 2)], axis=0)
         return codes, parts, own_codes, bounds, sums
 
-    codes, parts, _, bounds, _ = unpack(plane, owner * groups, groups)
+    codes, parts, _, bounds, _ = unpack(plane, owner * SPLIT, SPLIT)
     hidden, pooled_parts = owner_forward(
         feature_table, neighbour_query_weight, query_bias, codes, parts, bounds, batch_rows
     )
@@ -460,9 +495,11 @@
     ).astype(BF16)
     mix_weight_grad = lax.all_gather(mix_rows, ("table", "rep"), axis=0, tiled=True).astype(F32)
 
-    all_codes, all_parts, all_own_codes, all_bounds, sums = unpack(every, owner * groups + group, 1)
-    place = group.reshape(1)
-    table_part, query_part, query_bias_part, mix_bias_part = owner_backward(
+    half = lax.rem(group, SPLIT)
+    partner = group + 1 - 2 * half
+    swap = [(i, i + 1 - 2 * (i % SPLIT)) for i in range(groups)]
+    all_codes, all_parts, all_own_codes, all_bounds, sums = unpack(every, owner * SPLIT + half, 1)
+    table_grad, table_send, query_part, query_send, query_bias_part, mix_bias_part = owner_backward(
         feature_table,
         hidden,
         all_mixed,
@@ -472,7 +509,7 @@
         all_parts,
         all_own_codes,
         all_bounds,
-        place,
+        jnp.stack([group, partner]),
         owners,
         groups,
         batch_rows,
@@ -481,18 +518,23 @@
 
     query_rows = width // devices
     bias_rows = 16
+    query_part = query_part + lax.ppermute(query_send, "rep", swap).astype(F32)
+    table_got = lax.ppermute(table_send, "rep", swap)
     incoming = lax.all_to_all(
-        query_part.reshape(devices, query_rows, width), ("table", "rep"), split_axis=0, concat_axis=0, tiled=True
+        query_part.astype(BF16).reshape(owners, query_rows, width), "table", split_axis=0, concat_axis=0, tiled=True
     )
     summed = jnp.sum(incoming.astype(F32), axis=0)
     bias_part = jnp.pad(jnp.sum(query_bias_part, axis=0, keepdims=True), ((0, bias_rows - 1), (0, 0)))
     gathered = lax.all_gather(
         jnp.concatenate([summed, bias_part], axis=0).astype(BF16), ("table", "rep"), axis=0
-    ).astype(F32)
-    query_weight_grad = gathered[:, :query_rows].reshape(width, width)
-    query_bias_grad = jnp.sum(gathered[:, query_rows], axis=0)
-    table_grad = lax.all_to_all(table_part, "rep", split_axis=0, concat_axis=0, tiled=True)
-    table_grad = table_grad.reshape(rows_owned, width // groups).astype(F32)
+    ).reshape(owners, groups, query_rows + bias_rows, width)
+    query_weight_grad = (
+        gathered[:, :, :query_rows].transpose(1, 0, 2, 3).reshape(width, width).astype(F32)
+    )
+    query_bias_grad = jnp.sum(gathered[:, :SPLIT, query_rows].astype(F32), axis=(0, 1))
+    table_grad = lax.dynamic_update_slice(
+        table_grad, table_got.astype(F32), ((1 - half) * (rows_owned // SPLIT), 0)
+    )
     statistics = sums / (batch_rows * devices)
     return (
         embed,

time: 604 us -> 594 us (0.983)
  Pallas kernels: 135 us -> 181 us
  blocking collectives: 73.7 us -> 49.2 us
  waiting for transfers between devices: 281 us -> 258 us
    all_to_all x2 -> x1, waiting for transfers between devices: 141 us -> 9.54 us  [local(): lax.all_to_all(query_part.astype(BF16).reshape(owners, query_rows, width)...]
    ppermute x0 -> x2, waiting for transfers between devices: none -> 75.6 us  [the longest x1 66.9 us: local(): table_got = lax.ppermute(table_send, 'rep', swap)]
    pallas_call x1, Pallas kernels: 72.2 us -> 116 us  [owner_backward(): pl.pallas_call(functools.partial(backward_kernel, requesters, length), gr...]
    all_to_all x1, blocking collectives: 55.1 us -> 30.5 us  [local(): lax.all_to_all(joined.reshape(batch_rows, devices, mix_part).transpose(1,...]
    all_gather x1, waiting for transfers between devices: 65.2 us -> 88.5 us  [local(): all_mixed = lax.all_gather(grad_mixed, ('table', 'rep'), axis=0, tiled=True)]
    all_gather x1, waiting for transfers between devices: 0.01 us -> 11 us  [local(): lax.all_gather(mix_rows, ('table', 'rep'), axis=0, tiled=True).astype(F32)]
    all_to_all x2 -> x1, starting transfers between devices: 9.66 us -> 3.49 us  [local(): lax.all_to_all(query_part.astype(BF16).reshape(owners, query_rows, width)...]
  transfers between devices with their start and end apart: 8 -> 9, of which waited for: 4 -> 6; matrix products, arithmetic and copies ran while one was open for 8% -> 8% of each run, Pallas kernels for 22% -> 11%
where the time goes in v3:
time: 594 us; the launch traced here: 592 us
  waiting for transfers between devices  258 us (43%)
  Pallas kernels  181 us (30%)
  blocking collectives  49.2 us (8%)
  other arithmetic  39.7 us (7%)
  local copies, waits for them, and re-layouts  29.1 us (5%)
  between operations  16.7 us (3%)
  matrix products  10.9 us (2%)
  starting transfers between devices  7.79 us (1%)
    pallas_call x1, Pallas kernels, owner_backward(): pl.pallas_call(functools.partial(backward_kernel, requesters, length), gr...  116 us
    all_gather x1, waiting for transfers between devices, local(): all_mixed = lax.all_gather(grad_mixed, ('table', 'rep'), axis=0, tiled=True)  88.5 us
    reduce_scatter x1, waiting for transfers between devices, local(): lax.psum_scatter(pooled_parts, 'table', scatter_dimension=0, tiled=True)  72.7 us
    ppermute x1, waiting for transfers between devices, local(): table_got = lax.ppermute(table_send, 'rep', swap)  66.9 us
    pallas_call x1, Pallas kernels, owner_forward(): pl.pallas_call(functools.partial(forward_kernel, blocks, length), grid_sp...  64.6 us
    all_to_all x1, blocking collectives, local(): lax.all_to_all(joined.reshape(batch_rows, devices, mix_part).transpose(1,...  30.5 us
    gather x1, local copies, waits for them, and re-layouts, local(): found = feature_table[jnp.clip(wanted, 0, rows_owned - 1)]  15.9 us
  transfers between devices with their start and end apart: 9, of which 6 were waited for; matrix products, arithmetic and copies ran while one was open for 8% of the time, Pallas kernels for 11%

profile of v3, /device:TPU:0, one launch (start us, length us, event | category | flops | bytes accessed | tf_op | source)
XLA Modules:
  0.0 592.3 jit_solution(2047895081071190401)
XLA Ops:
  8.1 0.7 fusion.14
  8.8 1.2 dynamic-slice
  10.7 0.3 dynamic-update-slice
  10.9 9.6 %all-reduce.4 = s32[1536]{0:T(1024)S(1)} all-reduce(s32[1536]{0:T(1024)S(1)} %dynamic-update-slice), channel_id=2, replica_groups=mesh['table'=8,'rep'=4] {'table'}, use_global_device_ids=true, to_apply=%add.4 | all-reduce | flops 1536 | bytes 12288
  20.6 15.9 %gather_fusion = bf16[1536,1024]{1,0:T(8,128)(2,1)S(1)} fusion(bf16[9216,1024]{1,0:T(8,128)(2,1)} %table_other.1, s32[2048]{0:T(1024)S(1)} %pad_clamp_fusion), kind=kCustom, calls=%fused_computation | custom fusion | bytes 6297600 | tf_op jit(solution)/shard_map/gather | solution.py:409
  36.5 2.1 broadcast_select_fusion
  38.7 0.7 copy-done.5
  39.4 0.6 fusion.10
  40.1 3.2 sort.30
  43.3 0.2 convert_reduce_fusion.2
  43.4 0.1 copy.50
  43.5 0.1 reshape.117
  43.7 0.1 copy.49
  43.8 0.1 reshape.116
  43.9 7.5 %sort.29 = (s32[9600]{0:T(1024)S(1)}, f32[9600]{0:T(1024)S(1)}) sort(s32[9600]{0:T(1024)S(1)} %reshape.116, f32[9600]{0:T(1024)S(1)} %reshape.117), dimensions={0}, to_apply=%region_1.2 | sort | flops 134400 | bytes 153600 | tf_op jit(solution)/shard_map/sort | solution.py:420
  51.5 0.2 convert_reduce_fusion
  51.8 1.4 select_maximum_fusion.2
  53.2 9.1 %all-gather.3 = f32[8,1,11136]{2,1,0:T(1,128)S(1)} all-gather(f32[1,1,11136]{2,1,0:T(1,128)S(1)} %reshape.158), channel_id=3, replica_groups=mesh['table'=8,'rep'=4] {'table'}, dimensions={0}, use_global_device_ids=true | all-gather | bytes 400896 | tf_op jit(solution)/shard_map/all_gather | solution.py:449
  62.4 0.9 copy.52.shares
  63.2 0.1 constant_dynamic-slice_fusion.3
  63.3 0.1 slice.56
  63.4 0.1 slice.57
  63.5 0.8 copy.51.codes
  64.3 0.7 maximum_convert_fusion.1.bounds
  65.0 64.6 %owner_forward.1 = (bf16[9216,1024]{1,0:T(8,128)(2,1)}, f32[1536,1024]{1,0:T(8,128)}) custom-call(s32[8,4]{1,0:T(8,128)} %maximum_convert_fusion.1.bounds, bf16[9216,1024]{1,0:T(8,128)(2,1)} %table_other.1, bf16[1024,1024]{1,0:T(8,128)(2,1)} %query_other.1, f32[1,1024]{1,0:T(1,128)} %bitcast.45, s32[8,1,5376]{2,1,0:T(1,128)} %copy.51.codes, ...), custom_call_target="tpu_custom_call" | custom-call | flops 19327352832 | bytes 37748736 | tf_op jit(solution)/shard_map/owner_forward/pallas_call | solution.py:126
  129.7 0.5 all-gather.15.cloned.1.call-update
  130.3 72.7 %reduce-scatter.5.cloned.1.call-done = f32[192,1024]{1,0:T(8,128)} async-done(((f32[1536,1024]{1,0:T(8,128)}), f32[192,1024]{1,0:T(8,128)}) %reduce-scatter.5.cloned.1.call-update) | async-done | bytes 786448 | tf_op jit(solution)/shard_map/reduce_scatter | solution.py:470
  203.0 1.2 reduce-precision_convert_fusion
  204.2 3.4 fusion.3
  207.6 1.3 fusion.2
  208.9 0.6 pad_add_fusion.place
  209.5 1.5 slice_bitcast_fusion
  211.0 1.6 copy.54.shares
  212.6 0.6 reshape.124.self_codes
  213.2 1.6 copy.53.codes
  214.8 0.1 constant_dynamic-slice_fusion.1
  214.9 0.7 maximum_convert_fusion.bounds
  215.5 88.5 %all-gather.9.cloned.1.call-done.grads = bf16[6144,1024]{1,0:T(8,128)(2,1)} async-done(((bf16[192,1024]{1,0:T(8,128)(2,1)}), bf16[6144,1024]{1,0:T(8,128)(2,1)}) %all-gather.9.cloned.1.call-update) | async-done | bytes 12582928 | tf_op jit(solution)/shard_map/all_gather | solution.py:483
  304.0 116.3 %owner_backward.1 = (f32[9216,256]{1,0:T(8,128)}, bf16[4608,256]{1,0:T(8,128)(2,1)}, f32[256,1024]{1,0:T(8,128)}, bf16[256,1024]{1,0:T(8,128)(2,1)}, f32[8,1024]{1,0:T(8,128)}, /*index=5*/f32[8,1024]{1,0:T(8,128)}) custom-call(s32[2]{0:T(128)} %pad_add_fusion.place, s32[32,4]{1,0:T(8,128)} %maximum_convert_fusion.bounds, s32[32,1,5376]{2,1,0:T(1,128)} %copy.53.codes, ...), custom_call_target="tpu_custom_call" | custom-call | flops 38654705664 | bytes 25165824 | tf_op jit(solution)/shard_map/owner_backward/pallas_call | solution.py:313
  420.3 0.7 collective-permute-start.1
  421.1 8.7 %collective-permute-done.1 = bf16[256,1024]{1,0:T(8,128)(2,1)S(1)} collective-permute-done((bf16[256,1024]{1,0:T(8,128)(2,1)}, bf16[256,1024]{1,0:T(8,128)(2,1)S(1)}, u32[]{:S(2)}, u32[]{:S(2)}) %collective-permute-start.1) | collective-permute-done | bytes 524320 | tf_op jit(solution)/shard_map/ppermute | solution.py:521
  429.8 2.2 add_convert_fusion
  432.0 3.5 all-to-all-start
  435.5 0.0 all-gather.11.cloned.1.call-start
  435.6 9.5 %all-to-all-done = bf16[8,32,1024]{2,1,0:T(8,128)(2,1)S(1)} async-done(((bf16[8,32,1024]{2,1,0:T(8,128)(2,1)}), bf16[8,32,1024]{2,1,0:T(8,128)(2,1)S(1)}, u32[]{:S(2)}, u32[]{:S(2)}) %all-to-all-start) | async-done | bytes 524320 | tf_op jit(solution)/shard_map/all_to_all | solution.py:523
  445.1 0.1 reduce.1
  445.2 0.6 pad_maximum_fusion.1
  445.9 0.1 pad_maximum_fusion
  446.0 0.5 copy.56
  446.5 30.5 %all_to_all.10 = bf16[32,192,64]{1,2,0:T(8,128)(2,1)S(1)} all-to-all(bf16[32,192,64]{1,2,0:T(8,128)(2,1)S(1)} %bitcast.35), channel_id=1, replica_groups=mesh['table'=8,'rep'=4] {'table','rep'}, dimensions={0} | all-to-all | bytes 1572864 | tf_op jit(solution)/shard_map/all_to_all | solution.py:485
  477.0 0.6 copy.57
  477.6 1.1 reshape.128
  478.7 7.6 %convolution_convert_fusion = bf16[64,1024]{1,0:T(8,128)(2,1)} fusion(bf16[6144,64]{0,1:T(8,128)(2,1)S(1)} %reshape.128, bf16[6144,1024]{1,0:T(8,128)(2,1)} %all-gather.9.cloned.1.call-done.grads), kind=kOutput, calls=%fused_computation.5 | convolution fusion | flops 805371904 | bytes 13500416 | tf_op jit(solution)/shard_map/dot_general | solution.py:493
  486.3 3.3 collective-permute-start
  489.6 0.8 slice_reduce_fusion
  490.4 0.5 broadcast_multiply_fusion.2
  491.0 0.6 reduce_sum.118
  491.6 66.9 %collective-permute-done = bf16[4608,256]{1,0:T(8,128)(2,1)S(1)} collective-permute-done((bf16[4608,256]{1,0:T(8,128)(2,1)}, bf16[4608,256]{1,0:T(8,128)(2,1)S(1)}, u32[]{:S(2)}, u32[]{:S(2)}) %collective-permute-start) | collective-permute-done | bytes 2359328 | tf_op jit(solution)/shard_map/ppermute | solution.py:522
  558.5 2.6 convert_dynamic-update-slice_fusion
  561.0 2.1 convert_bitcast_fusion
  563.1 2.3 copy.55
  565.4 1.6 fusion.6
  567.0 11.0 %all-gather.13.cloned.1.call-done = bf16[2048,1024]{1,0:T(8,128)(2,1)} async-done(((bf16[64,1024]{1,0:T(8,128)(2,1)}), bf16[2048,1024]{1,0:T(8,128)(2,1)}) %all-gather.13.cloned.1.call-update) | async-done | bytes 4194320 | tf_op jit(solution)/shard_map/all_gather | solution.py:496
  578.0 6.6 %convert_element_type.121 = f32[2048,1024]{1,0:T(8,128)} convert(bf16[2048,1024]{1,0:T(8,128)(2,1)} %all-gather.13.cloned.1.call-done) | non-fusion elementwise | flops 2097152 | bytes 12582912 | tf_op jit(solution)/shard_map/convert_element_type | solution.py:496
  (60 shorter events, 0.7 us)
Async XLA Ops:
  8.0 121.6 %reduce-scatter.3.cloned.1.call-start = ((), (), s32[]{:S(2)}) async-start(), calls=%async_computation.4 | async-start | bytes 3538944 | tf_op jit(solution)/shard_map/reduce_scatter | solution.py:411
  38.6 0.8 copy-start.5
  38.6 0.8 copy-start.8
  38.6 0.9 copy-start.4
  38.6 14.6 %copy-start.9 = (pred[5376]{0:T(1024)(128)(4,1)S(1)}, pred[5376]{0:T(1024)(128)(4,1)}, u32[]{:S(2)}) copy-start(pred[5376]{0:T(1024)(128)(4,1)} %constant.37.clone.1) | copy-start | bytes 16132
  38.6 164.4 %reduce-scatter.5.cloned.1.call-start = ((), (), s32[]{:S(2)}) async-start(), calls=%async_computation.5 | async-start | bytes 7077888 | tf_op jit(solution)/shard_map/reduce_scatter | solution.py:470
  62.3 67.2 %copy-start = (f32[8,1,11136]{2,0,1:T(8,128)}, f32[8,1,11136]{2,0,1:T(8,128)S(1)}, u32[]{:S(2)}) copy-start(f32[8,1,11136]{2,0,1:T(8,128)S(1)} %copy.60) | copy-start | bytes 1069060
  129.6 74.6 %copy-start.2 = (bf16[192,1024]{1,0:T(8,128)(2,1)S(1)}, bf16[192,1024]{1,0:T(8,128)(2,1)}, u32[]{:S(2)}) copy-start(bf16[192,1024]{1,0:T(8,128)(2,1)} %param.17) | copy-start | bytes 1179652
  129.6 74.6 %copy-start.3 = (bf16[192,1024]{1,0:T(8,128)(2,1)S(1)}, bf16[192,1024]{1,0:T(8,128)(2,1)}, u32[]{:S(2)}) copy-start(bf16[192,1024]{1,0:T(8,128)(2,1)} %reduce-scatter.3.cloned.1.call-done) | copy-start | bytes 1179652
  129.6 74.6 %copy-start.10 = (f32[1024]{0:T(1024)S(1)}, f32[1024]{0:T(1024)}, u32[]{:S(2)}) copy-start(f32[1024]{0:T(1024)} %param.13) | copy-start | bytes 12292
  129.6 79.8 %all-gather.15.cloned.1.call-start = ((), (), s32[]{:S(2)}) async-start(), calls=%async_computation.9 | async-start | bytes 1781760 | tf_op jit(solution)/shard_map/all_gather | solution.py:450
  130.2 173.8 %all-gather.9.cloned.1.call-start = ((), (), s32[]{:S(2)}) async-start(), calls=%async_computation.6 | async-start | bytes 12976128 | tf_op jit(solution)/shard_map/all_gather | solution.py:483
  209.5 3.1 copy-start.1
  209.5 5.3 slice-start
  420.3 15.2 %copy-start.7 = (f32[8,1024]{1,0:T(8,128)S(1)}, f32[8,1024]{1,0:T(8,128)}, u32[]{:S(2)}) copy-start(f32[8,1024]{1,0:T(8,128)} %get-tuple-element.34) | copy-start | bytes 98308
  420.3 9.5 %collective-permute-start.1 = (bf16[256,1024]{1,0:T(8,128)(2,1)}, bf16[256,1024]{1,0:T(8,128)(2,1)S(1)}, u32[]{:S(2)}, u32[]{:S(2)}) collective-permute-start(bf16[256,1024]{1,0:T(8,128)(2,1)} %get-tuple-element.33), channel_id=1, source_target_pairs={{0,1},{1,0},{2,3},{3,2},{4,5},{5,4},{6,7},{7,6},{8,9},{9,8},{10,11... | collective-permute-start | bytes 1572872 | tf_op jit(solution)/shard_map/ppermute | solution.py:521
  432.0 13.1 %all-to-all-start = ((bf16[8,32,1024]{2,1,0:T(8,128)(2,1)}), bf16[8,32,1024]{2,1,0:T(8,128)(2,1)S(1)}, u32[]{:S(2)}, u32[]{:S(2)}) async-start(bf16[8,32,1024]{2,1,0:T(8,128)(2,1)} %bitcast.12), calls=%async_computation.2 | async-start | bytes 1048576 | tf_op jit(solution)/shard_map/all_to_all | solution.py:523
  435.5 125.6 %all-gather.11.cloned.1.call-start = ((), (), s32[]{:S(2)}) async-start(), calls=%async_computation.7 | async-start | bytes 3244032 | tf_op jit(solution)/shard_map/all_gather | solution.py:528
  445.9 132.2 %all-gather.13.cloned.1.call-start = ((), (), s32[]{:S(2)}) async-start(), calls=%async_computation.8 | async-start | bytes 4325376 | tf_op jit(solution)/shard_map/all_gather | solution.py:496
  478.7 12.2 %copy-start.6 = (f32[8,1024]{1,0:T(8,128)S(1)}, f32[8,1024]{1,0:T(8,128)}, u32[]{:S(2)}) copy-start(f32[8,1024]{1,0:T(8,128)} %get-tuple-element.35) | copy-start | bytes 98308
  486.3 72.2 %collective-permute-start = (bf16[4608,256]{1,0:T(8,128)(2,1)}, bf16[4608,256]{1,0:T(8,128)(2,1)S(1)}, u32[]{:S(2)}, u32[]{:S(2)}) collective-permute-start(bf16[4608,256]{1,0:T(8,128)(2,1)} %get-tuple-element.31), channel_id=1, source_target_pairs={{0,1},{1,0},{2,3},{3,2},{4,5},{5,4},{6,7},{7,6},{8,9},{9,8},{10,11... | collective-permute-start | bytes 7077896 | tf_op jit(solution)/shard_map/ppermute | solution.py:522
Sparse Core Ops, SparseCore 0:
  38.7 45.7 reduce-scatter.2
  129.8 73.1 reduce-scatter.4
Sparse Core Ops, SparseCore 1:
  132.3 45.7 all-gather.14
  209.0 95.0 all-gather.8
  445.9 63.4 all-gather.10
  513.0 65.0 all-gather.12

commit v4 on v3

--- a/solution.py
+++ b/solution.py
@@ -191,7 +191,8 @@
     query_own,
     query_other,
     table_grad,
-    table_send,
+    send_first,
+    send_last,
     weight_grad,
     weight_send,
     query_bias_grad,
@@ -266,10 +267,12 @@
         table_grad[...] = lax.dot_general(
             grad_pre, query_own[...], turned, preferred_element_type=F32
         ) + lax.dot_general(self_sums[...], self_own[...], turned, preferred_element_type=F32)
-        table_send[...] = (
+        send = (
             lax.dot_general(grad_pre, query_other[...], turned, preferred_element_type=F32)
             + lax.dot_general(self_sums[...], self_other[...], turned, preferred_element_type=F32)
         ).astype(BF16)
+        send_first[...] = send[:, : send_first.shape[1]]
+        send_last[...] = send[:, send_first.shape[1] :]
 
     @pl.when(step == pl.num_programs(0) - 1)
     def _():
@@ -333,7 +336,8 @@
             ],
             out_specs=[
                 pl.BlockSpec((ROW_BLOCK, part), lambda i, place, bounds: (node_row(i, place), 0)),
-                pl.BlockSpec((ROW_BLOCK, part), lambda i, place, bounds: (jnp.maximum(i - requesters, 0), 0)),
+                pl.BlockSpec((ROW_BLOCK, part // 2), lambda i, place, bounds: (jnp.maximum(i - requesters, 0), 0)),
+                pl.BlockSpec((ROW_BLOCK, part // 2), lambda i, place, bounds: (jnp.maximum(i - requesters, 0), 0)),
                 fixed((part, width)),
                 fixed((part, width)),
                 fixed((SUBLANES, width)),
@@ -350,7 +354,8 @@
         ),
         out_shape=[
             jax.ShapeDtypeStruct((rows_owned, part), F32),
-            jax.ShapeDtypeStruct((rows, part), BF16),
+            jax.ShapeDtypeStruct((rows, part // 2), BF16),
+            jax.ShapeDtypeStruct((rows, part // 2), BF16),
             jax.ShapeDtypeStruct((part, width), F32),
             jax.ShapeDtypeStruct((part, width), BF16),
             jax.ShapeDtypeStruct((SUBLANES, width), F32),
@@ -403,13 +408,6 @@
     owner = lax.axis_index("table").astype(I32)
     group = lax.axis_index("rep").astype(I32)
 
-    own_ids = lax.all_gather(lookup_ids[:, 0], "table", axis=0, tiled=True)
-    wanted = own_ids - owner * rows_owned
-    mine = (wanted >= 0) & (wanted < rows_owned)
-    found = feature_table[jnp.clip(wanted, 0, rows_owned - 1)]
-    found = jnp.where(mine[:, None], found, jnp.zeros((), BF16))
-    self_rows = lax.psum_scatter(found, "table", scatter_dimension=0, tiled=True)
-
     present = (jnp.arange(near, dtype=I32)[None, :] < present_counts[:, None]).astype(F32)
     masked_weight = importance * present
     shares = lax.reduce_precision(masked_weight / jnp.sum(masked_weight, axis=1, keepdims=True), 8, 7)
@@ -443,10 +441,17 @@
             padded(sorted_shares, length),
             padded(as_code(own_keys), own_length),
             padded(meta, meta_length),
+            padded(lookup_ids[:, 0].astype(F32), own_length),
         ]
     )
-    request, _ = lax.optimization_barrier((request, found))
     plane = lax.all_gather(request, "table", axis=0)
+
+    own_ids = plane[:, -own_length:][:, :batch_rows].astype(I32).reshape(-1)
+    wanted = own_ids - owner * rows_owned
+    mine = (wanted >= 0) & (wanted < rows_owned)
+    found = feature_table[jnp.clip(wanted, 0, rows_owned - 1)]
+    found = jnp.where(mine[:, None], found, jnp.zeros((), BF16))
+    self_rows = lax.psum_scatter(found, "table", scatter_dimension=0, tiled=True)
     every = lax.all_gather(plane, "rep", axis=0).reshape(devices, -1)
 
     def unpack(lists, start, stride):
@@ -463,11 +468,15 @@
         return codes, parts, own_codes, bounds, sums
 
     codes, parts, _, bounds, _ = unpack(plane, owner * SPLIT, SPLIT)
+    bounds, _ = lax.optimization_barrier((bounds, found))
     hidden, pooled_parts = owner_forward(
         feature_table, neighbour_query_weight, query_bias, codes, parts, bounds, batch_rows
     )
     pooled_parts, self_rows = lax.optimization_barrier((pooled_parts, self_rows))
     pooled = lax.psum_scatter(pooled_parts, "table", scatter_dimension=0, tiled=True)
+    half = lax.rem(group, SPLIT)
+    pooled, lists = lax.optimization_barrier((pooled, unpack(every, owner * SPLIT + half, 1)))
+    all_codes, all_parts, all_own_codes, all_bounds, sums = lists
     pooled = lax.reduce_precision(pooled, 8, 7).astype(BF16)
 
     joined = jnp.concatenate([self_rows, pooled], axis=1)
@@ -493,13 +502,12 @@
     mix_rows = lax.dot_general(
         columns, all_mixed, (((0,), (0,)), ((), ())), preferred_element_type=F32
     ).astype(BF16)
-    mix_weight_grad = lax.all_gather(mix_rows, ("table", "rep"), axis=0, tiled=True).astype(F32)
-
-    half = lax.rem(group, SPLIT)
+    all_mixed, mix_rows = lax.optimization_barrier((all_mixed, mix_rows))
+    mix_gathered = lax.all_gather(mix_rows, ("table", "rep"), axis=0, tiled=True)
+
     partner = group + 1 - 2 * half
     swap = [(i, i + 1 - 2 * (i % SPLIT)) for i in range(groups)]
-    all_codes, all_parts, all_own_codes, all_bounds, sums = unpack(every, owner * SPLIT + half, 1)
-    table_grad, table_send, query_part, query_send, query_bias_part, mix_bias_part = owner_backward(
+    table_grad, send_first, send_last, query_part, query_send, query_bias_part, mix_bias_part = owner_backward(
         feature_table,
         hidden,
         all_mixed,
@@ -519,12 +527,17 @@
     query_rows = width // devices
     bias_rows = 16
     query_part = query_part + lax.ppermute(query_send, "rep", swap).astype(F32)
-    table_got = lax.ppermute(table_send, "rep", swap)
+    send_first, mix_gathered = lax.optimization_barrier((send_first, mix_gathered))
+    mix_weight_grad = mix_gathered.astype(F32)
+    got_first = lax.ppermute(send_first, "rep", swap)
     incoming = lax.all_to_all(
         query_part.astype(BF16).reshape(owners, query_rows, width), "table", split_axis=0, concat_axis=0, tiled=True
     )
     summed = jnp.sum(incoming.astype(F32), axis=0)
     bias_part = jnp.pad(jnp.sum(query_bias_part, axis=0, keepdims=True), ((0, bias_rows - 1), (0, 0)))
+    summed, got_first = lax.optimization_barrier((summed, got_first))
+    got_last = lax.ppermute(send_last, "rep", swap)
+    table_got = jnp.concatenate([got_first, got_last], axis=1)
     gathered = lax.all_gather(
         jnp.concatenate([summed, bias_part], axis=0).astype(BF16), ("table", "rep"), axis=0
     ).reshape(owners, groups, query_rows + bias_rows, width)

time: 594 us -> 549 us (0.924)
  waiting for transfers between devices: 258 us -> 205 us
    ppermute x1 -> x2, waiting for transfers between devices: 66.9 us -> 25.6 us  [the longest x1 22.4 us: local(): got_last = lax.ppermute(send_last, 'rep', swap)]
    all_gather x1, waiting for transfers between devices: 0.01 us -> 24 us  [local(): lax.all_gather(jnp.concatenate([summed, bias_part], axis=0).astype(BF16),...]
    all_gather x1, waiting for transfers between devices: 88.5 us -> 65.1 us  [local(): all_mixed = lax.all_gather(grad_mixed, ('table', 'rep'), axis=0, tiled=True)]
    all_gather x1, waiting for transfers between devices: 11 us -> 0.01 us  [local(): lax.all_gather(mix_rows, ('table', 'rep'), axis=0, tiled=True)]
    unnamed x1 -> x0, blocking collectives: 9.58 us -> none
    all_to_all x1, blocking collectives: 30.5 us -> 37.8 us  [local(): lax.all_to_all(joined.reshape(batch_rows, devices, mix_part).transpose(1,...]
  transfers between devices with their start and end apart: 9 -> 10, of which waited for: 6 -> 7; matrix products, arithmetic and copies ran while one was open for 8% -> 5% of each run, Pallas kernels for 11% -> 33%
where the time goes in v4:
time: 549 us; the launch traced here: 543 us
  waiting for transfers between devices  205 us (37%)
  Pallas kernels  177 us (32%)
  blocking collectives  48.8 us (9%)
  other arithmetic  44.5 us (8%)
  local copies, waits for them, and re-layouts  28.1 us (5%)
  between operations  16 us (3%)
  starting transfers between devices  11.9 us (2%)
  matrix products  10.9 us (2%)
    pallas_call x1, Pallas kernels, owner_backward(): pl.pallas_call(functools.partial(backward_kernel, requesters, length), gr...  111 us
    reduce_scatter x1, waiting for transfers between devices, local(): lax.psum_scatter(pooled_parts, 'table', scatter_dimension=0, tiled=True)  67.2 us
    pallas_call x1, Pallas kernels, owner_forward(): pl.pallas_call(functools.partial(forward_kernel, blocks, length), grid_sp...  66.1 us
    all_gather x1, waiting for transfers between devices, local(): all_mixed = lax.all_gather(grad_mixed, ('table', 'rep'), axis=0, tiled=True)  65.1 us
    all_to_all x1, blocking collectives, local(): lax.all_to_all(joined.reshape(batch_rows, devices, mix_part).transpose(1,...  37.8 us
    all_gather x1, waiting for transfers between devices, local(): lax.all_gather(jnp.concatenate([summed, bias_part], axis=0).astype(BF16),...  24 us
    ppermute x1, waiting for transfers between devices, local(): got_last = lax.ppermute(send_last, 'rep', swap)  22.4 us
    gather x1, local copies, waits for them, and re-layouts, local(): found = feature_table[jnp.clip(wanted, 0, rows_owned - 1)]  15.9 us
  transfers between devices with their start and end apart: 10, of which 7 were waited for; matrix products, arithmetic and copies ran while one was open for 5% of the time, Pallas kernels for 33%

profile of v4, /device:TPU:0, one launch (start us, length us, event | category | flops | bytes accessed | tf_op | source)
XLA Modules:
  0.0 542.5 jit_solution(15160924677637382718)
XLA Ops:
  8.1 0.7 slice_convert_fusion.5
  8.8 0.8 add_select_fusion
  9.6 1.5 fusion.8
  11.1 3.2 sort.30
  14.3 0.2 convert_reduce_fusion.3
  14.4 0.8 divide_reduce-precision_fusion
  15.3 0.1 copy.50
  15.4 0.1 reshape.160
  15.5 0.1 copy.49
  15.6 0.1 reshape.159
  15.8 7.5 %sort.29 = (s32[9600]{0:T(1024)S(1)}, f32[9600]{0:T(1024)S(1)}) sort(s32[9600]{0:T(1024)S(1)} %reshape.159, f32[9600]{0:T(1024)S(1)} %reshape.160), dimensions={0}, to_apply=%region_1.2 | sort | flops 134400 | bytes 153600 | tf_op jit(solution)/shard_map/sort | solution.py:418
  23.3 0.2 convert_reduce_fusion.1
  23.6 0.7 select_dynamic-update-slice_fusion
  24.3 1.4 constant_dynamic-update-slice_fusion.1
  25.8 11.1 %all-gather.2 = f32[8,1,11392]{2,1,0:T(1,128)S(1)} all-gather(f32[1,1,11392]{2,1,0:T(1,128)S(1)} %reshape.184), channel_id=2, replica_groups=mesh['table'=8,'rep'=4] {'table'}, dimensions={0}, use_global_device_ids=true | all-gather | bytes 410112 | tf_op jit(solution)/shard_map/all_gather | solution.py:447
  36.9 0.1 and.24
  37.1 15.9 %gather_fusion = bf16[1536,1024]{1,0:T(8,128)(2,1)S(1)} fusion(bf16[9216,1024]{1,0:T(8,128)(2,1)} %table_other.1, s32[2048]{0:T(1024)S(1)} %pad_clamp_fusion), kind=kCustom, calls=%fused_computation | custom fusion | bytes 6297600 | tf_op jit(solution)/shard_map/gather | solution.py:452
  53.0 2.1 broadcast_select_fusion
  55.2 0.5 all-gather.14.cloned.1.call-update
  55.8 0.3 copy-done.1
  56.3 0.8 copy.52.shares
  57.2 0.8 copy.51.codes
  58.1 0.7 maximum_convert_fusion.1.bounds
  58.7 66.1 %owner_forward.1 = (bf16[9216,1024]{1,0:T(8,128)(2,1)}, f32[1536,1024]{1,0:T(8,128)}) custom-call(s32[8,4]{1,0:T(8,128)} %maximum_convert_fusion.1.bounds, bf16[9216,1024]{1,0:T(8,128)(2,1)} %table_other.1, bf16[1024,1024]{1,0:T(8,128)(2,1)} %query_other.1, f32[1,1024]{1,0:T(1,128)} %bitcast.48, s32[8,1,5376]{2,1,0:T(1,128)} %copy.51.codes, ...), custom_call_target="tpu_custom_call" | custom-call | flops 19327352832 | bytes 37748736 | tf_op jit(solution)/shard_map/owner_forward/pallas_call | solution.py:126
  124.9 0.2 all-gather.8.cloned.1.call-start
  125.2 0.8 slice_convert_fusion.3
  125.9 0.6 reshape.167.self_codes
  126.6 0.8 slice.82
  127.5 0.7 maximum_convert_fusion.bounds
  128.1 0.8 slice_reduce_fusion
  128.9 1.4 slice_bitcast_fusion
  130.3 67.2 %reduce-scatter.5.cloned.1.call-done = f32[192,1024]{1,0:T(8,128)} async-done(((f32[1536,1024]{1,0:T(8,128)}), f32[192,1024]{1,0:T(8,128)}) %reduce-scatter.5.cloned.1.call-update) | async-done | bytes 786448 | tf_op jit(solution)/shard_map/reduce_scatter | solution.py:476
  197.5 1.2 reduce-precision_convert_fusion
  198.7 3.4 fusion.3
  202.1 1.3 fusion.2
  203.4 1.1 pad_maximum_fusion
  204.5 0.5 copy.53
  205.0 37.8 %all_to_all.10 = bf16[32,192,64]{1,2,0:T(8,128)(2,1)S(1)} all-to-all(bf16[32,192,64]{1,2,0:T(8,128)(2,1)S(1)} %bitcast.36), channel_id=1, replica_groups=mesh['table'=8,'rep'=4] {'table','rep'}, dimensions={0} | all-to-all | bytes 1572864 | tf_op jit(solution)/shard_map/all_to_all | solution.py:494
  242.8 0.6 copy.54
  243.4 1.1 reshape.169
  244.5 65.1 %all-gather.8.cloned.1.call-done.grads = bf16[6144,1024]{1,0:T(8,128)(2,1)} async-done(((bf16[192,1024]{1,0:T(8,128)(2,1)}), bf16[6144,1024]{1,0:T(8,128)(2,1)}) %all-gather.8.cloned.1.call-update) | async-done | bytes 12582928 | tf_op jit(solution)/shard_map/all_gather | solution.py:492
  309.6 7.5 %convolution_convert_fusion = bf16[64,1024]{1,0:T(8,128)(2,1)} fusion(bf16[6144,64]{0,1:T(8,128)(2,1)S(1)} %reshape.169, bf16[6144,1024]{1,0:T(8,128)(2,1)} %all-gather.8.cloned.1.call-done.grads), kind=kOutput, calls=%fused_computation.5 | convolution fusion | flops 805371904 | bytes 13500416 | tf_op jit(solution)/shard_map/dot_general | solution.py:502
  317.2 0.6 pad_add_fusion.place
  317.8 1.6 copy.55.codes
  319.4 1.6 copy.56.shares
  320.9 111.2 %owner_backward.1 = (f32[9216,256]{1,0:T(8,128)}, bf16[4608,128]{1,0:T(8,128)(2,1)}, bf16[4608,128]{1,0:T(8,128)(2,1)}, f32[256,1024]{1,0:T(8,128)}, bf16[256,10...) custom-call(s32[2]{0:T(128)} %pad_add_fusion.place, s32[32,4]{1,0:T(8,128)} %maximum_convert_fusion.bounds, ...), custom_call_target="tpu_custom_call" | custom-call | flops 38654705664 | bytes 25165824 | tf_op jit(solution)/shard_map/owner_backward/pallas_call | solution.py:316
  432.1 2.2 collective-permute-start
  434.3 0.1 collective-permute-start.1
  434.4 12.9 %collective-permute-done = bf16[256,1024]{1,0:T(8,128)(2,1)S(1)} collective-permute-done((bf16[256,1024]{1,0:T(8,128)(2,1)}, bf16[256,1024]{1,0:T(8,128)(2,1)S(1)}, u32[]{:S(2)}, u32[]{:S(2)}) %collective-permute-start) | collective-permute-done | bytes 524320 | tf_op jit(solution)/shard_map/ppermute | solution.py:529
  447.3 2.2 add_convert_fusion
  449.4 8.5 %all-to-all-start.1 = ((bf16[8,32,1024]{2,1,0:T(8,128)(2,1)}), bf16[8,32,1024]{2,1,0:T(8,128)(2,1)S(1)}, u32[]{:S(2)}, u32[]{:S(2)}) async-start(bf16[8,32,1024]{2,1,0:T(8,128)(2,1)} %bitcast.13), calls=%async_computation.3 | async-start | bytes 1048576 | tf_op jit(solution)/shard_map/all_to_all | solution.py:533
  458.0 9.6 %all-to-all-done.1 = bf16[8,32,1024]{2,1,0:T(8,128)(2,1)S(1)} async-done(((bf16[8,32,1024]{2,1,0:T(8,128)(2,1)}), bf16[8,32,1024]{2,1,0:T(8,128)(2,1)S(1)}, u32[]{:S(2)}, u32[]{:S(2)}) %all-to-all-start.1) | async-done | bytes 524320 | tf_op jit(solution)/shard_map/all_to_all | solution.py:533
  467.7 3.2 collective-permute-done.1
  470.9 0.6 pad_maximum_fusion.1
  471.6 0.8 collective-permute-start.2
  472.3 0.5 broadcast_multiply_fusion.1
  472.9 0.6 reduce_sum.119
  473.5 6.6 %convert_element_type.134 = f32[2048,1024]{1,0:T(8,128)} convert(bf16[2048,1024]{1,0:T(8,128)(2,1)} %all-gather.10.cloned.1.call-done) | non-fusion elementwise | flops 2097152 | bytes 12582912 | tf_op jit(solution)/shard_map/convert_element_type | solution.py:531
  480.1 22.4 %collective-permute-done.2 = bf16[4608,128]{1,0:T(8,128)(2,1)S(1)} collective-permute-done((bf16[4608,128]{1,0:T(8,128)(2,1)}, bf16[4608,128]{1,0:T(8,128)(2,1)S(1)}, u32[]{:S(2)}, u32[]{:S(2)}) %collective-permute-start.2) | collective-permute-done | bytes 1179680 | tf_op jit(solution)/shard_map/ppermute | solution.py:539
  502.5 2.5 convert_dynamic-update-slice_fusion
  505.0 24.0 %all-gather.12.cloned.1.call-done = bf16[32,48,1024]{2,1,0:T(8,128)(2,1)} async-done(((bf16[1,48,1024]{2,1,0:T(8,128)(2,1)}), bf16[32,48,1024]{2,1,0:T(8,128)(2,1)}) %all-gather.12.cloned.1.call-update) | async-done | bytes 3145744 | tf_op jit(solution)/shard_map/all_gather | solution.py:541
  528.9 1.6 fusion.6
  530.6 2.1 convert_bitcast_fusion
  532.6 2.3 copy.57
  (55 shorter events, 1.1 us)
Async XLA Ops:
  8.0 116.8 %reduce-scatter.3.cloned.1.call-start = ((), (), s32[]{:S(2)}) async-start(), calls=%async_computation.4 | async-start | bytes 3538944 | tf_op jit(solution)/shard_map/reduce_scatter | solution.py:454
  36.8 16.2 %copy-start = (f32[8,1,11392]{2,0,1:T(8,128)}, f32[8,1,11392]{2,0,1:T(8,128)S(1)}, u32[]{:S(2)}) copy-start(f32[8,1,11392]{2,0,1:T(8,128)S(1)} %copy.60) | copy-start | bytes 1093636
  55.1 1.0 copy-start.1
  55.1 70.0 %all-gather.14.cloned.1.call-start = ((), (), s32[]{:S(2)}) async-start(), calls=%async_computation.9 | async-start | bytes 1822720 | tf_op jit(solution)/shard_map/all_gather | solution.py:455
  55.7 141.8 %reduce-scatter.5.cloned.1.call-start = ((), (), s32[]{:S(2)}) async-start(), calls=%async_computation.5 | async-start | bytes 7077888 | tf_op jit(solution)/shard_map/reduce_scatter | solution.py:476
  124.9 73.8 %copy-start.2 = (bf16[192,1024]{1,0:T(8,128)(2,1)S(1)}, bf16[192,1024]{1,0:T(8,128)(2,1)}, u32[]{:S(2)}) copy-start(bf16[192,1024]{1,0:T(8,128)(2,1)} %param.17) | copy-start | bytes 1179652
  124.9 73.8 %copy-start.3 = (bf16[192,1024]{1,0:T(8,128)(2,1)S(1)}, bf16[192,1024]{1,0:T(8,128)(2,1)}, u32[]{:S(2)}) copy-start(bf16[192,1024]{1,0:T(8,128)(2,1)} %reduce-scatter.3.cloned.1.call-done) | copy-start | bytes 1179652
  124.9 73.8 %copy-start.6 = (f32[1024]{0:T(1024)S(1)}, f32[1024]{0:T(1024)}, u32[]{:S(2)}) copy-start(f32[1024]{0:T(1024)} %param.13) | copy-start | bytes 12292
  124.9 184.7 %all-gather.8.cloned.1.call-start = ((), (), s32[]{:S(2)}) async-start(), calls=%async_computation.6 | async-start | bytes 12976128 | tf_op jit(solution)/shard_map/all_gather | solution.py:492
  203.4 230.9 %all-gather.10.cloned.1.call-start = ((), (), s32[]{:S(2)}) async-start(), calls=%async_computation.7 | async-start | bytes 4325376 | tf_op jit(solution)/shard_map/all_gather | solution.py:506
  432.1 25.9 %copy-start.5 = (f32[8,1024]{1,0:T(8,128)S(1)}, f32[8,1024]{1,0:T(8,128)}, u32[]{:S(2)}) copy-start(f32[8,1024]{1,0:T(8,128)} %get-tuple-element.58) | copy-start | bytes 98308
  432.1 40.7 %copy-start.4 = (f32[8,1024]{1,0:T(8,128)S(1)}, f32[8,1024]{1,0:T(8,128)}, u32[]{:S(2)}) copy-start(f32[8,1024]{1,0:T(8,128)} %get-tuple-element.60) | copy-start | bytes 98308
  432.1 15.2 %collective-permute-start = (bf16[256,1024]{1,0:T(8,128)(2,1)}, bf16[256,1024]{1,0:T(8,128)(2,1)S(1)}, u32[]{:S(2)}, u32[]{:S(2)}) collective-permute-start(bf16[256,1024]{1,0:T(8,128)(2,1)} %get-tuple-element.51), channel_id=1, source_target_pairs={{0,1},{1,0},{2,3},{3,2},{4,5},{5,4},{6,7},{7,6},{8,9},{9,8},{10,11... | collective-permute-start | bytes 1572872 | tf_op jit(solution)/shard_map/ppermute | solution.py:529
  434.3 36.6 %collective-permute-start.1 = (bf16[4608,128]{1,0:T(8,128)(2,1)}, bf16[4608,128]{1,0:T(8,128)(2,1)S(1)}, u32[]{:S(2)}, u32[]{:S(2)}) collective-permute-start(bf16[4608,128]{1,0:T(8,128)(2,1)} %get-tuple-element.54), channel_id=1, source_target_pairs={{0,1},{1,0},{2,3},{3,2},{4,5},{5,4},{6,7},{7,6},{8,9},{9,8},{10,11... | collective-permute-start | bytes 3538952 | tf_op jit(solution)/shard_map/ppermute | solution.py:532
  449.4 18.2 %all-to-all-start.1 = ((bf16[8,32,1024]{2,1,0:T(8,128)(2,1)}), bf16[8,32,1024]{2,1,0:T(8,128)(2,1)S(1)}, u32[]{:S(2)}, u32[]{:S(2)}) async-start(bf16[8,32,1024]{2,1,0:T(8,128)(2,1)} %bitcast.13), calls=%async_computation.3 | async-start | bytes 1048576 | tf_op jit(solution)/shard_map/all_to_all | solution.py:533
  457.9 71.0 %all-gather.12.cloned.1.call-start = ((), (), s32[]{:S(2)}) async-start(), calls=%async_computation.8 | async-start | bytes 3244032 | tf_op jit(solution)/shard_map/all_gather | solution.py:541
  471.6 30.9 %collective-permute-start.2 = (bf16[4608,128]{1,0:T(8,128)(2,1)}, bf16[4608,128]{1,0:T(8,128)(2,1)S(1)}, u32[]{:S(2)}, u32[]{:S(2)}) collective-permute-start(bf16[4608,128]{1,0:T(8,128)(2,1)} %get-tuple-element.56), channel_id=1, source_target_pairs={{0,1},{1,0},{2,3},{3,2},{4,5},{5,4},{6,7},{7,6},{8,9},{9,8},{10,11... | collective-permute-start | bytes 3538952 | tf_op jit(solution)/shard_map/ppermute | solution.py:539
Sparse Core Ops, SparseCore 0:
  55.3 46.3 reduce-scatter.2
  125.0 72.4 reduce-scatter.4
Sparse Core Ops, SparseCore 1:
  57.8 35.2 all-gather.13
  203.5 106.1 all-gather.7
  317.3 60.3 all-gather.9
  471.7 57.2 all-gather.11

commit v5 on v4

--- a/solution.py
+++ b/solution.py
@@ -185,14 +185,9 @@
     hidden,
     table_own,
     table_other,
-    self_own,
-    self_other,
     mix_pooled,
-    query_own,
-    query_other,
-    table_grad,
-    send_first,
-    send_last,
+    grad_pre,
+    self_sums,
     weight_grad,
     weight_send,
     query_bias_grad,
@@ -201,7 +196,6 @@
     self_total,
     rows_here,
     near_sums,
-    self_sums,
     weight_sum,
 ):
     step = pl.program_id(0)
@@ -258,28 +252,20 @@
         lax.fori_loop(0, block // 16, part, 0)
         turned = (((1,), (1,)), ((), ()))
         raw = lax.dot_general(near_sums[...], mix_pooled[...], turned, preferred_element_type=F32)
-        grad_pre = jnp.where(hidden[...].astype(F32) > 0, raw, 0.0)
-        query_bias_grad[...] += jnp.sum(grad_pre.reshape(block // SUBLANES, SUBLANES, width), axis=0)
-        grad_pre = grad_pre.astype(BF16)
+        wide = jnp.where(hidden[...].astype(F32) > 0, raw, 0.0)
+        query_bias_grad[...] += jnp.sum(wide.reshape(block // SUBLANES, SUBLANES, width), axis=0)
+        kept = wide.astype(BF16)
+        grad_pre[...] = kept
         down = (((0,), (0,)), ((), ()))
-        weight_grad[...] += lax.dot_general(table_own[...], grad_pre, down, preferred_element_type=F32)
-        weight_sum[...] += lax.dot_general(table_other[...], grad_pre, down, preferred_element_type=F32)
-        table_grad[...] = lax.dot_general(
-            grad_pre, query_own[...], turned, preferred_element_type=F32
-        ) + lax.dot_general(self_sums[...], self_own[...], turned, preferred_element_type=F32)
-        send = (
-            lax.dot_general(grad_pre, query_other[...], turned, preferred_element_type=F32)
-            + lax.dot_general(self_sums[...], self_other[...], turned, preferred_element_type=F32)
-        ).astype(BF16)
-        send_first[...] = send[:, : send_first.shape[1]]
-        send_last[...] = send[:, send_first.shape[1] :]
+        weight_grad[...] += lax.dot_general(table_own[...], kept, down, preferred_element_type=F32)
+        weight_sum[...] += lax.dot_general(table_other[...], kept, down, preferred_element_type=F32)
 
     @pl.when(step == pl.num_programs(0) - 1)
     def _():
         weight_send[...] = weight_sum[...].astype(BF16)
 
 
-def owner_backward(table, hidden, grads, mix, query, codes, shares, self_codes, bounds, place, owners, groups, targets):
+def owner_backward(table, hidden, grads, mix, codes, shares, self_codes, bounds, place, owners, groups, targets):
     rows_owned, width = table.shape
     rows = rows_owned // SPLIT
     blocks = rows // ROW_BLOCK
@@ -300,11 +286,6 @@
     def grad_block(i, place, bounds):
         k = requester(i)
         return (lax.rem(k, owners) * groups + lax.div(k, owners), 0)
-
-    def weights(which):
-        return pl.BlockSpec(
-            (part, width), lambda i, place, bounds: (place[which], 0), pipeline_mode=pl.Buffered(1)
-        )
 
     def table_columns(which):
         return pl.BlockSpec((ROW_BLOCK, part), lambda i, place, bounds: (node_row(i, place), place[which]))
@@ -328,16 +309,11 @@
                 pl.BlockSpec((ROW_BLOCK, width), lambda i, place, bounds: (node_row(i, place), 0)),
                 table_columns(0),
                 table_columns(1),
-                weights(0),
-                weights(1),
                 pl.BlockSpec((width, width), lambda i, place, bounds: (1, 0), pipeline_mode=pl.Buffered(1)),
-                weights(0),
-                weights(1),
             ],
             out_specs=[
-                pl.BlockSpec((ROW_BLOCK, part), lambda i, place, bounds: (node_row(i, place), 0)),
-                pl.BlockSpec((ROW_BLOCK, part // 2), lambda i, place, bounds: (jnp.maximum(i - requesters, 0), 0)),
-                pl.BlockSpec((ROW_BLOCK, part // 2), lambda i, place, bounds: (jnp.maximum(i - requesters, 0), 0)),
+                pl.BlockSpec((ROW_BLOCK, width), lambda i, place, bounds: (jnp.maximum(i - requesters, 0), 0)),
+                pl.BlockSpec((ROW_BLOCK, width), lambda i, place, bounds: (jnp.maximum(i - requesters, 0), 0)),
                 fixed((part, width)),
                 fixed((part, width)),
                 fixed((SUBLANES, width)),
@@ -348,14 +324,12 @@
                 pltpu.VMEM((rows * SUBLANES, LANES), F32),
                 pltpu.VMEM((targets * SUBLANES, LANES), F32),
                 pltpu.VMEM((ROW_BLOCK, width), BF16),
-                pltpu.VMEM((ROW_BLOCK, width), BF16),
                 pltpu.VMEM((part, width), F32),
             ],
         ),
         out_shape=[
-            jax.ShapeDtypeStruct((rows_owned, part), F32),
-            jax.ShapeDtypeStruct((rows, part // 2), BF16),
-            jax.ShapeDtypeStruct((rows, part // 2), BF16),
+            jax.ShapeDtypeStruct((rows, width), BF16),
+            jax.ShapeDtypeStruct((rows, width), BF16),
             jax.ShapeDtypeStruct((part, width), F32),
             jax.ShapeDtypeStruct((part, width), BF16),
             jax.ShapeDtypeStruct((SUBLANES, width), F32),
@@ -377,11 +351,49 @@
         table,
         table,
         mix,
-        mix,
-        mix,
-        query,
-        query,
-    )
+    )
+
+
+def table_kernel(place, grad_pre, self_sums, query, mix_self, *outs):
+    turned = (((1,), (1,)), ((), ()))
+    grad = lax.dot_general(grad_pre[...], query[...], turned, preferred_element_type=F32) + lax.dot_general(
+        self_sums[...], mix_self[...], turned, preferred_element_type=F32
+    )
+    at = 0
+    for out in outs:
+        out[...] = grad[:, at : at + out.shape[1]].astype(out.dtype)
+        at += out.shape[1]
+
+
+def table_columns_grad(grad_pre, self_sums, query, mix, place, part, kept_rows=None):
+    rows, width = grad_pre.shape
+    blocks = rows // ROW_BLOCK
+
+    def node_block(i, place):
+        return (i, 0)
+
+    weights = pl.BlockSpec((part, width), lambda i, place: (place[0], 0), pipeline_mode=pl.Buffered(1))
+    if kept_rows is None:
+        out_specs = [pl.BlockSpec((ROW_BLOCK, part // 2), node_block)] * 2
+        out_shape = [jax.ShapeDtypeStruct((rows, part // 2), BF16)] * 2
+    else:
+        out_specs = [pl.BlockSpec((ROW_BLOCK, part), lambda i, place: (lax.rem(place[0], SPLIT) * blocks + i, 0))]
+        out_shape = [jax.ShapeDtypeStruct((kept_rows, part), F32)]
+    return pl.pallas_call(
+        table_kernel,
+        grid_spec=pltpu.PrefetchScalarGridSpec(
+            num_scalar_prefetch=1,
+            grid=(blocks,),
+            in_specs=[pl.BlockSpec((ROW_BLOCK, width), node_block)] * 2 + [weights] * 2,
+            out_specs=out_specs,
+        ),
+        out_shape=out_shape,
+        compiler_params=pltpu.CompilerParams(vmem_limit_bytes=VMEM_BYTES),
+        cost_estimate=pl.CostEstimate(
+            flops=4 * rows * width * part, bytes_accessed=4 * rows * width, transcendentals=0
+        ),
+        name="table_columns_grad",
+    )(place, grad_pre, self_sums, query, mix)
 
 
 def padded(values, length):
@@ -507,12 +519,11 @@
 
     partner = group + 1 - 2 * half
     swap = [(i, i + 1 - 2 * (i % SPLIT)) for i in range(groups)]
-    table_grad, send_first, send_last, query_part, query_send, query_bias_part, mix_bias_part = owner_backward(
+    grad_pre, self_sums, query_part, query_send, query_bias_part, mix_bias_part = owner_backward(
         feature_table,
         hidden,
         all_mixed,
         mix_weight,
-        neighbour_query_weight,
         all_codes,
         all_parts,
         all_own_codes,
@@ -522,10 +533,16 @@
         groups,
         batch_rows,
     )
+    part = width // groups
+    send_first, send_last = table_columns_grad(
+        grad_pre, self_sums, neighbour_query_weight, mix_weight, partner.reshape(1), part
+    )
+    (table_grad,) = table_columns_grad(
+        grad_pre, self_sums, neighbour_query_weight, mix_weight, group.reshape(1), part, rows_owned
+    )
     mix_bias_grad = jnp.sum(mix_bias_part, axis=0)
 
     query_rows = width // devices
-    bias_rows = 16
     query_part = query_part + lax.ppermute(query_send, "rep", swap).astype(F32)
     send_first, mix_gathered = lax.optimization_barrier((send_first, mix_gathered))
     mix_weight_grad = mix_gathered.astype(F32)
@@ -534,17 +551,15 @@
         query_part.astype(BF16).reshape(owners, query_rows, width), "table", split_axis=0, concat_axis=0, tiled=True
     )
     summed = jnp.sum(incoming.astype(F32), axis=0)
-    bias_part = jnp.pad(jnp.sum(query_bias_part, axis=0, keepdims=True), ((0, bias_rows - 1), (0, 0)))
     summed, got_first = lax.optimization_barrier((summed, got_first))
     got_last = lax.ppermute(send_last, "rep", swap)
     table_got = jnp.concatenate([got_first, got_last], axis=1)
-    gathered = lax.all_gather(
-        jnp.concatenate([summed, bias_part], axis=0).astype(BF16), ("table", "rep"), axis=0
-    ).reshape(owners, groups, query_rows + bias_rows, width)
-    query_weight_grad = (
-        gathered[:, :, :query_rows].transpose(1, 0, 2, 3).reshape(width, width).astype(F32)
-    )
-    query_bias_grad = jnp.sum(gathered[:, :SPLIT, query_rows].astype(F32), axis=(0, 1))
+    gathered = lax.all_gather(summed.astype(BF16), ("table", "rep"), axis=0).reshape(
+        owners, groups, query_rows, width
+    )
+    query_weight_grad = gathered.transpose(1, 0, 2, 3).reshape(width, width).astype(F32)
+    bias_parts = lax.all_gather(jnp.sum(query_bias_part, axis=0), ("table", "rep"), axis=0)
+    query_bias_grad = jnp.sum(bias_parts.reshape(owners, groups, width)[:, :SPLIT], axis=(0, 1))
     table_grad = lax.dynamic_update_slice(
         table_grad, table_got.astype(F32), ((1 - half) * (rows_owned // SPLIT), 0)
     )

time: 549 us -> 584 us (1.064)
  blocking collectives: 48.8 us -> 155 us
  waiting for transfers between devices: 205 us -> 134 us
  Pallas kernels: 177 us -> 188 us
  starting transfers between devices: 11.9 us -> 4.99 us
    all_gather x0 -> x1, blocking collectives: none -> 87.9 us  [local(): lax.all_gather(jnp.sum(query_bias_part, axis=0), ('table', 'rep'), axis=0)]
    pallas_call x0 -> x2, Pallas kernels: none -> 26.7 us  [table_columns_grad(): pl.pallas_call(table_kernel, grid_spec=pltpu.PrefetchScalarGridSpec(num_s...]
    all_gather x1, waiting for transfers between devices: 24 us -> 0.01 us  [local(): lax.all_gather(summed.astype(BF16), ('table', 'rep'), axis=0)]
    ppermute x1, waiting for transfers between devices: 22.4 us -> 0.01 us  [local(): got_last = lax.ppermute(send_last, 'rep', swap)]
    all_to_all x0 -> x1, blocking collectives: none -> 18.6 us  [local(): lax.all_to_all(query_part.astype(BF16).reshape(owners, query_rows, width)...]
    pallas_call x1, Pallas kernels: 111 us -> 96.4 us  [owner_backward(): pl.pallas_call(functools.partial(backward_kernel, requesters, length), gr...]
    ppermute x1, waiting for transfers between devices: 12.9 us -> 0.01 us  [local(): query_part = query_part + lax.ppermute(query_send, 'rep', swap).astype(F32)]
    all_to_all x1 -> x0, waiting for transfers between devices: 9.6 us -> none  [local(): lax.all_to_all(query_part.astype(BF16).reshape(owners, query_rows, width)...]
  transfers between devices with their start and end apart: 10 -> 9, of which waited for: 7 -> 3; matrix products, arithmetic and copies ran while one was open for 5% -> 5% of each run, Pallas kernels for 33% -> 33%
where the time goes in v5:
time: 584 us; the launch traced here: 579 us
  Pallas kernels  188 us (32%)
  blocking collectives  155 us (27%)
  waiting for transfers between devices  134 us (23%)
  other arithmetic  41.4 us (7%)
  local copies, waits for them, and re-layouts  28.1 us (5%)
  between operations  16 us (3%)
  matrix products  11 us (2%)
    pallas_call x1, Pallas kernels, owner_backward(): pl.pallas_call(functools.partial(backward_kernel, requesters, length), gr...  96.4 us
    all_gather x1, blocking collectives, local(): lax.all_gather(jnp.sum(query_bias_part, axis=0), ('table', 'rep'), axis=0)  87.9 us
    reduce_scatter x1, waiting for transfers between devices, local(): lax.psum_scatter(pooled_parts, 'table', scatter_dimension=0, tiled=True)  66.5 us
    pallas_call x1, Pallas kernels, owner_forward(): pl.pallas_call(functools.partial(forward_kernel, blocks, length), grid_sp...  65.1 us
    all_gather x1, waiting for transfers between devices, local(): all_mixed = lax.all_gather(grad_mixed, ('table', 'rep'), axis=0, tiled=True)  65.1 us
    all_to_all x1, blocking collectives, local(): lax.all_to_all(joined.reshape(batch_rows, devices, mix_part).transpose(1,...  37.8 us
    pallas_call x2, Pallas kernels, table_columns_grad(): pl.pallas_call(table_kernel, grid_spec=pltpu.PrefetchScalarGridSpec(num_s...  26.7 us
    all_to_all x1, blocking collectives, local(): lax.all_to_all(query_part.astype(BF16).reshape(owners, query_rows, width)...  18.6 us
  transfers between devices with their start and end apart: 9, of which 3 were waited for; matrix products, arithmetic and copies ran while one was open for 5% of the time, Pallas kernels for 33%

profile of v5, /device:TPU:0, one launch (start us, length us, event | category | flops | bytes accessed | tf_op | source)
XLA Modules:
  0.0 578.7 jit_solution(16516223091823161395)
XLA Ops:
  8.1 0.7 slice_convert_fusion.4
  8.8 0.8 add_select_fusion
  9.6 1.5 fusion.7
  11.1 3.2 sort.30
  14.3 0.2 convert_reduce_fusion.3
  14.4 0.8 divide_reduce-precision_fusion
  15.3 0.1 copy.59
  15.4 0.1 reshape.135
  15.5 0.1 copy.58
  15.6 0.1 reshape.134
  15.8 7.5 %sort.29 = (s32[9600]{0:T(1024)S(1)}, f32[9600]{0:T(1024)S(1)}) sort(s32[9600]{0:T(1024)S(1)} %reshape.134, f32[9600]{0:T(1024)S(1)} %reshape.135), dimensions={0}, to_apply=%region_1.2 | sort | flops 134400 | bytes 153600 | tf_op jit(solution)/shard_map/sort | solution.py:430
  23.3 0.2 convert_reduce_fusion.1
  23.6 0.7 select_dynamic-update-slice_fusion
  24.3 1.4 constant_dynamic-update-slice_fusion.1
  25.8 11.1 %all-gather.4 = f32[8,1,11392]{2,1,0:T(1,128)S(1)} all-gather(f32[1,1,11392]{2,1,0:T(1,128)S(1)} %reshape.166), channel_id=2, replica_groups=mesh['table'=8,'rep'=4] {'table'}, dimensions={0}, use_global_device_ids=true | all-gather | bytes 410112 | tf_op jit(solution)/shard_map/all_gather | solution.py:459
  36.9 0.1 and.24
  37.0 0.1 min.12
  37.1 15.9 %gather_fusion = bf16[1536,1024]{1,0:T(8,128)(2,1)S(1)} fusion(bf16[9216,1024]{1,0:T(8,128)(2,1)} %table_other.1, s32[2048]{0:T(1024)S(1)} %pad_clamp_fusion), kind=kCustom, calls=%fused_computation | custom fusion | bytes 6297600 | tf_op jit(solution)/shard_map/gather | solution.py:464
  53.0 2.1 broadcast_select_fusion
  55.2 0.5 all-gather.14.cloned.1.call-update
  55.8 0.3 copy-done.1
  56.1 0.1 constant_dynamic-slice_fusion.3
  56.3 0.8 copy.61.shares
  57.2 0.8 copy.60.codes
  58.1 0.7 maximum_convert_fusion.1.bounds
  58.7 65.1 %owner_forward.1 = (bf16[9216,1024]{1,0:T(8,128)(2,1)}, f32[1536,1024]{1,0:T(8,128)}) custom-call(s32[8,4]{1,0:T(8,128)} %maximum_convert_fusion.1.bounds, bf16[9216,1024]{1,0:T(8,128)(2,1)} %table_other.1, bf16[1024,1024]{1,0:T(8,128)(2,1)} %query.5, f32[1,1024]{1,0:T(1,128)} %bitcast.43, s32[8,1,5376]{2,1,0:T(1,128)} %copy.60.codes, f32[8,1,5376]{2,1,0:T(1,128)} %copy.61.shares), custom_call_target="tpu_custom_call" | custom-call | flops 19327352832 | bytes 37748736 | tf_op jit(solution)/shard_map/owner_forward/pallas_call | solution.py:126
  123.9 0.2 all-gather.10.cloned.1.call-start
  124.2 0.8 slice_convert_fusion.2
  125.0 0.6 reshape.142.self_codes
  125.6 0.8 slice.78
  126.5 0.7 maximum_convert_fusion.bounds
  127.1 0.8 slice_reduce_fusion.1
  128.0 1.4 slice_bitcast_fusion
  129.4 66.5 %reduce-scatter.5.cloned.1.call-done = f32[192,1024]{1,0:T(8,128)} async-done(((f32[1536,1024]{1,0:T(8,128)}), f32[192,1024]{1,0:T(8,128)}) %reduce-scatter.5.cloned.1.call-update) | async-done | bytes 786448 | tf_op jit(solution)/shard_map/reduce_scatter | solution.py:488
  195.9 1.2 reduce-precision_convert_fusion
  197.1 3.5 fusion.3
  200.6 1.2 fusion.2
  201.9 1.1 pad_maximum_fusion
  203.0 0.5 copy.62
  203.5 37.8 %all_to_all.10 = bf16[32,192,64]{1,2,0:T(8,128)(2,1)S(1)} all-to-all(bf16[32,192,64]{1,2,0:T(8,128)(2,1)S(1)} %bitcast.32), channel_id=1, replica_groups=mesh['table'=8,'rep'=4] {'table','rep'}, dimensions={0} | all-to-all | bytes 1572864 | tf_op jit(solution)/shard_map/all_to_all | solution.py:506
  241.3 0.6 copy.63
  241.9 1.1 reshape.145
  243.0 65.1 %all-gather.10.cloned.1.call-done.grads = bf16[6144,1024]{1,0:T(8,128)(2,1)} async-done(((bf16[192,1024]{1,0:T(8,128)(2,1)}), bf16[6144,1024]{1,0:T(8,128)(2,1)}) %all-gather.10.cloned.1.call-update) | async-done | bytes 12582928 | tf_op jit(solution)/shard_map/all_gather | solution.py:504
  308.1 7.5 %convolution_convert_fusion = bf16[64,1024]{1,0:T(8,128)(2,1)} fusion(bf16[6144,64]{0,1:T(8,128)(2,1)S(1)} %reshape.145, bf16[6144,1024]{1,0:T(8,128)(2,1)} %all-gather.10.cloned.1.call-done.grads), kind=kOutput, calls=%fused_computation.5 | convolution fusion | flops 805371904 | bytes 13500416 | tf_op jit(solution)/shard_map/dot_general | solution.py:514
  315.7 0.6 pad_add_fusion.place
  316.3 1.6 copy.64.codes
  317.9 1.6 copy.65.shares
  319.4 96.4 %owner_backward.1 = (bf16[4608,1024]{1,0:T(8,128)(2,1)}, bf16[4608,1024]{1,0:T(8,128)(2,1)}, f32[256,1024]{1,0:T(8,128)}, bf16[256,1024]{1,0:T(8,128)(2,1)}, f32[8,1024]{1,0:T(8,128)}, /*index=5*/f32[8,1024]{1,0:T(8,128)}) custom-call(s32[2]{0:T(128)} %pad_add_fusion.place, s32[32,4]{1,0:T(8,128)} %maximum_convert_fusion.bounds, s32[32,1,5376]{2,1,0:T(1,128)} %copy.64.codes, ...), custom_call_target="tpu_custom_call" | custom-call | flops 38654705664 | bytes 25165824 | tf_op jit(solution)/shard_map/owner_backward/pallas_call | solution.py:297
  415.9 13.2 %table_columns_grad.3 = (bf16[4608,128]{1,0:T(8,128)(2,1)}, bf16[4608,128]{1,0:T(8,128)(2,1)}) custom-call(s32[1]{0:T(128)} %bitcast.10.place, bf16[4608,1024]{1,0:T(8,128)(2,1)} %get-tuple-element.50.grad_pre, bf16[4608,1024]{1,0:T(8,128)(2,1)} %get-tuple-element.51.self_sums, bf16[1024,1024]{1,0:T(8,128)(2,1)} %query.5, bf16[2048,1024]{1,0:T(8,128)(2,1)} %mix_self.3), custom_call_target="tpu_custom_call" | custom-call | flops 4831838208 | bytes 18874368 | tf_op jit(solution)/shard_map/table_columns_grad/pallas_call | solution.py:382
  429.1 2.0 collective-permute-start.1
  431.2 0.1 add_convert_fusion
  431.3 18.6 %all_to_all.11 = bf16[8,32,1024]{2,1,0:T(8,128)(2,1)S(1)} all-to-all(bf16[8,32,1024]{2,1,0:T(8,128)(2,1)S(1)} %bitcast.40), channel_id=1, replica_groups=mesh['table'=8,'rep'=4] {'table'}, dimensions={0} | all-to-all | bytes 1048576 | tf_op jit(solution)/shard_map/all_to_all | solution.py:550
  449.9 0.7 convert_reduce_fusion
  450.6 1.3 collective-permute-done.1
  451.9 2.4 collective-permute-start.2
  454.4 0.5 broadcast_multiply_fusion.1
  454.9 0.6 reduce_sum.119
  455.5 87.9 %all-gather.3 = f32[32768]{0:T(1024)S(1)} all-gather(f32[1024]{0:T(1024)S(1)} %reduce_sum.117), channel_id=5, replica_groups=mesh['table'=8,'rep'=4] {'table','rep'}, dimensions={0}, use_global_device_ids=true | all-gather | bytes 135168 | tf_op jit(solution)/shard_map/all_gather | solution.py:561
  543.4 0.6 slice_reduce_fusion
  544.0 13.6 %table_columns_grad.2 = f32[9216,256]{1,0:T(8,128)} custom-call(s32[1]{0:T(128)} %bitcast.9.place, bf16[4608,1024]{1,0:T(8,128)(2,1)} %get-tuple-element.50.grad_pre, bf16[4608,1024]{1,0:T(8,128)(2,1)} %get-tuple-element.51.self_sums, bf16[1024,1024]{1,0:T(8,128)(2,1)} %query.5, bf16[2048,1024]{1,0:T(8,128)(2,1)} %mix_self.3), custom_call_target="tpu_custom_call" | custom-call | flops 4831838208 | bytes 18874368 | tf_op jit(solution)/shard_map/table_columns_grad/pallas_call | solution.py:382
  557.6 6.6 %convert_element_type.127 = f32[2048,1024]{1,0:T(8,128)} convert(bf16[2048,1024]{1,0:T(8,128)(2,1)} %all-gather.12.cloned.1.call-done) | non-fusion elementwise | flops 2097152 | bytes 12582912 | tf_op jit(solution)/shard_map/convert_element_type | solution.py:548
  564.3 2.5 convert_dynamic-update-slice_fusion
  566.8 2.1 convert_bitcast_fusion
  568.8 2.3 copy.66
  (55 shorter events, 1.0 us)
Async XLA Ops:
  8.0 115.9 %reduce-scatter.3.cloned.1.call-start = ((), (), s32[]{:S(2)}) async-start(), calls=%async_computation.4 | async-start | bytes 3538944 | tf_op jit(solution)/shard_map/reduce_scatter | solution.py:466
  36.8 16.2 %copy-start = (f32[8,1,11392]{2,0,1:T(8,128)}, f32[8,1,11392]{2,0,1:T(8,128)S(1)}, u32[]{:S(2)}) copy-start(f32[8,1,11392]{2,0,1:T(8,128)S(1)} %copy.71) | copy-start | bytes 1093636
  55.1 1.0 copy-start.1
  55.1 69.0 %all-gather.14.cloned.1.call-start = ((), (), s32[]{:S(2)}) async-start(), calls=%async_computation.8 | async-start | bytes 1822720 | tf_op jit(solution)/shard_map/all_gather | solution.py:467
  55.7 140.2 %reduce-scatter.5.cloned.1.call-start = ((), (), s32[]{:S(2)}) async-start(), calls=%async_computation.5 | async-start | bytes 7077888 | tf_op jit(solution)/shard_map/reduce_scatter | solution.py:488
  123.9 73.2 %copy-start.3 = (bf16[192,1024]{1,0:T(8,128)(2,1)S(1)}, bf16[192,1024]{1,0:T(8,128)(2,1)}, u32[]{:S(2)}) copy-start(bf16[192,1024]{1,0:T(8,128)(2,1)} %param.17) | copy-start | bytes 1179652
  123.9 73.2 %copy-start.6 = (f32[1024]{0:T(1024)S(1)}, f32[1024]{0:T(1024)}, u32[]{:S(2)}) copy-start(f32[1024]{0:T(1024)} %param.13) | copy-start | bytes 12292
  123.9 184.2 %all-gather.10.cloned.1.call-start = ((), (), s32[]{:S(2)}) async-start(), calls=%async_computation.6 | async-start | bytes 12976128 | tf_op jit(solution)/shard_map/all_gather | solution.py:504
  201.9 227.2 %all-gather.12.cloned.1.call-start = ((), (), s32[]{:S(2)}) async-start(), calls=%async_computation.7 | async-start | bytes 4325376 | tf_op jit(solution)/shard_map/all_gather | solution.py:518
  315.6 251.1 %all-gather.16.cloned.1.call-start = ((), (), s32[]{:S(2)}) async-start(), calls=%async_computation.9 | async-start | bytes 2162688 | tf_op jit(solution)/shard_map/all_gather | solution.py:557
  415.8 15.3 %collective-permute-start = (bf16[256,1024]{1,0:T(8,128)(2,1)}, bf16[256,1024]{1,0:T(8,128)(2,1)S(1)}, u32[]{:S(2)}, u32[]{:S(2)}) collective-permute-start(bf16[256,1024]{1,0:T(8,128)(2,1)} %get-tuple-element.53), channel_id=1, source_target_pairs={{0,1},{1,0},{2,3},{3,2},{4,5},{5,4},{6,7},{7,6},{8,9},{9,8},{10,11... | collective-permute-start | bytes 1572872 | tf_op jit(solution)/shard_map/ppermute | solution.py:546
  415.9 15.3 %copy-start.2 = (f32[256,1024]{1,0:T(8,128)S(1)}, f32[256,1024]{1,0:T(8,128)}, u32[]{:S(2)}) copy-start(f32[256,1024]{1,0:T(8,128)} %get-tuple-element.52) | copy-start | bytes 3145732
  429.1 25.8 %copy-start.5 = (f32[8,1024]{1,0:T(8,128)S(1)}, f32[8,1024]{1,0:T(8,128)}, u32[]{:S(2)}) copy-start(f32[8,1024]{1,0:T(8,128)} %get-tuple-element.60) | copy-start | bytes 98308
  429.1 25.8 %copy-start.4 = (f32[8,1024]{1,0:T(8,128)S(1)}, f32[8,1024]{1,0:T(8,128)}, u32[]{:S(2)}) copy-start(f32[8,1024]{1,0:T(8,128)} %get-tuple-element.62) | copy-start | bytes 98308
  429.1 22.8 %collective-permute-start.1 = (bf16[4608,128]{1,0:T(8,128)(2,1)}, bf16[4608,128]{1,0:T(8,128)(2,1)S(1)}, u32[]{:S(2)}, u32[]{:S(2)}) collective-permute-start(bf16[4608,128]{1,0:T(8,128)(2,1)} %get-tuple-element.56), channel_id=1, source_target_pairs={{0,1},{1,0},{2,3},{3,2},{4,5},{5,4},{6,7},{7,6},{8,9},{9,8},{10,11... | collective-permute-start | bytes 3538952 | tf_op jit(solution)/shard_map/ppermute | solution.py:549
  451.9 112.3 %collective-permute-start.2 = (bf16[4608,128]{1,0:T(8,128)(2,1)}, bf16[4608,128]{1,0:T(8,128)(2,1)S(1)}, u32[]{:S(2)}, u32[]{:S(2)}) collective-permute-start(bf16[4608,128]{1,0:T(8,128)(2,1)} %get-tuple-element.58), channel_id=1, source_target_pairs={{0,1},{1,0},{2,3},{3,2},{4,5},{5,4},{6,7},{7,6},{8,9},{9,8},{10,11... | collective-permute-start | bytes 3538952 | tf_op jit(solution)/shard_map/ppermute | solution.py:555
Sparse Core Ops, SparseCore 0:
  55.3 46.3 reduce-scatter.2
  124.0 71.8 reduce-scatter.4
Sparse Core Ops, SparseCore 1:
  57.8 35.2 all-gather.13
  202.0 106.1 all-gather.9
  315.7 60.3 all-gather.11
  452.0 66.2 all-gather.15

commit v6 on v5

--- a/solution.py
+++ b/solution.py
@@ -14,6 +14,7 @@
 SUBLANES = 8
 ROW_BLOCK = 512
 SHIFT = 256
+BIAS_ROWS = 16
 SPLIT = 2
 WINDOW = 1536
 UNROLL = 4
@@ -190,17 +191,18 @@
     self_sums,
     weight_grad,
     weight_send,
-    query_bias_grad,
     mix_bias_grad,
     near_total,
     self_total,
     rows_here,
     near_sums,
     weight_sum,
+    bias_sum,
 ):
     step = pl.program_id(0)
     block, width = hidden.shape
     rows = near_total.shape[0] // SUBLANES
+    part_rows = weight_sum.shape[0]
     chunks = width // LANES
     tile = SUBLANES * SUBLANES
 
@@ -209,7 +211,7 @@
         clear_rows(near_total, rows)
         clear_rows(self_total, rows)
         mix_bias_grad[...] = jnp.zeros_like(mix_bias_grad)
-        query_bias_grad[...] = jnp.zeros_like(query_bias_grad)
+        bias_sum[...] = jnp.zeros_like(bias_sum)
         weight_grad[...] = jnp.zeros_like(weight_grad)
         weight_sum[...] = jnp.zeros_like(weight_sum)
 
@@ -253,16 +255,19 @@
         turned = (((1,), (1,)), ((), ()))
         raw = lax.dot_general(near_sums[...], mix_pooled[...], turned, preferred_element_type=F32)
         wide = jnp.where(hidden[...].astype(F32) > 0, raw, 0.0)
-        query_bias_grad[...] += jnp.sum(wide.reshape(block // SUBLANES, SUBLANES, width), axis=0)
+        bias_sum[...] += jnp.sum(wide.reshape(block // SUBLANES, SUBLANES, width), axis=0)
         kept = wide.astype(BF16)
         grad_pre[...] = kept
         down = (((0,), (0,)), ((), ()))
-        weight_grad[...] += lax.dot_general(table_own[...], kept, down, preferred_element_type=F32)
+        weight_grad[:part_rows] += lax.dot_general(table_own[...], kept, down, preferred_element_type=F32)
         weight_sum[...] += lax.dot_general(table_other[...], kept, down, preferred_element_type=F32)
 
     @pl.when(step == pl.num_programs(0) - 1)
     def _():
-        weight_send[...] = weight_sum[...].astype(BF16)
+        bias = jnp.broadcast_to(jnp.sum(bias_sum[...], axis=0, keepdims=True), (BIAS_ROWS, width))
+        weight_grad[part_rows:] = bias
+        weight_send[:part_rows] = weight_sum[...].astype(BF16)
+        weight_send[part_rows:] = bias.astype(BF16)
 
 
 def owner_backward(table, hidden, grads, mix, codes, shares, self_codes, bounds, place, owners, groups, targets):
@@ -314,9 +319,8 @@
             out_specs=[
                 pl.BlockSpec((ROW_BLOCK, width), lambda i, place, bounds: (jnp.maximum(i - requesters, 0), 0)),
                 pl.BlockSpec((ROW_BLOCK, width), lambda i, place, bounds: (jnp.maximum(i - requesters, 0), 0)),
-                fixed((part, width)),
-                fixed((part, width)),
-                fixed((SUBLANES, width)),
+                fixed((part + BIAS_ROWS, width)),
+                fixed((part + BIAS_ROWS, width)),
                 fixed((SUBLANES, width)),
             ],
             scratch_shapes=[
@@ -325,14 +329,14 @@
                 pltpu.VMEM((targets * SUBLANES, LANES), F32),
                 pltpu.VMEM((ROW_BLOCK, width), BF16),
                 pltpu.VMEM((part, width), F32),
+                pltpu.VMEM((SUBLANES, width), F32),
             ],
         ),
         out_shape=[
             jax.ShapeDtypeStruct((rows, width), BF16),
             jax.ShapeDtypeStruct((rows, width), BF16),
-            jax.ShapeDtypeStruct((part, width), F32),
-            jax.ShapeDtypeStruct((part, width), BF16),
-            jax.ShapeDtypeStruct((SUBLANES, width), F32),
+            jax.ShapeDtypeStruct((part + BIAS_ROWS, width), F32),
+            jax.ShapeDtypeStruct((part + BIAS_ROWS, width), BF16),
             jax.ShapeDtypeStruct((SUBLANES, width), F32),
         ],
         compiler_params=pltpu.CompilerParams(vmem_limit_bytes=VMEM_BYTES),
@@ -519,7 +523,7 @@
 
     partner = group + 1 - 2 * half
     swap = [(i, i + 1 - 2 * (i % SPLIT)) for i in range(groups)]
-    grad_pre, self_sums, query_part, query_send, query_bias_part, mix_bias_part = owner_backward(
+    grad_pre, self_sums, query_part, query_send, mix_bias_part = owner_backward(
         feature_table,
         hidden,
         all_mixed,
@@ -547,19 +551,24 @@
     send_first, mix_gathered = lax.optimization_barrier((send_first, mix_gathered))
     mix_weight_grad = mix_gathered.astype(F32)
     got_first = lax.ppermute(send_first, "rep", swap)
-    incoming = lax.all_to_all(
-        query_part.astype(BF16).reshape(owners, query_rows, width), "table", split_axis=0, concat_axis=0, tiled=True
-    )
+    bias_rows = SUBLANES
+    outgoing = jnp.concatenate(
+        [
+            query_part[:part].reshape(owners, query_rows, width),
+            jnp.broadcast_to(query_part[part : part + bias_rows], (owners, bias_rows, width)),
+        ],
+        axis=1,
+    )
+    incoming = lax.all_to_all(outgoing.astype(BF16), "table", split_axis=0, concat_axis=0, tiled=True)
     summed = jnp.sum(incoming.astype(F32), axis=0)
+    query_bias_grad = summed[query_rows]
     summed, got_first = lax.optimization_barrier((summed, got_first))
     got_last = lax.ppermute(send_last, "rep", swap)
     table_got = jnp.concatenate([got_first, got_last], axis=1)
-    gathered = lax.all_gather(summed.astype(BF16), ("table", "rep"), axis=0).reshape(
+    gathered = lax.all_gather(summed[:query_rows].astype(BF16), ("table", "rep"), axis=0).reshape(
         owners, groups, query_rows, width
     )
     query_weight_grad = gathered.transpose(1, 0, 2, 3).reshape(width, width).astype(F32)
-    bias_parts = lax.all_gather(jnp.sum(query_bias_part, axis=0), ("table", "rep"), axis=0)
-    query_bias_grad = jnp.sum(bias_parts.reshape(owners, groups, width)[:, :SPLIT], axis=(0, 1))
     table_grad = lax.dynamic_update_slice(
         table_grad, table_got.astype(F32), ((1 - half) * (rows_owned // SPLIT), 0)
     )

time: 584 us -> 531 us (0.909); the launches traced: 579 us -> 532 us
  blocking collectives: 155 us -> 69 us
  waiting for transfers between devices: 134 us -> 174 us
    all_gather x1 -> x0, blocking collectives: 87.9 us -> none  [local(): lax.all_gather(jnp.sum(query_bias_part, axis=0), ('table', 'rep'), axis=0)]
    all_gather x1, waiting for transfers between devices: 0.01 us -> 26.6 us  [local(): lax.all_gather(summed[:query_rows].astype(BF16), ('table', 'rep'), axis=0)]
    reduce_scatter x1, waiting for transfers between devices: 66.5 us -> 72.8 us  [local(): lax.psum_scatter(pooled_parts, 'table', scatter_dimension=0, tiled=True)]
  transfers between devices with their start and end apart: 9 -> 9, of which waited for: 3 -> 5; matrix products, arithmetic and copies ran while one was open for 5% -> 5% of each run, Pallas kernels for 33% -> 35%
where the time goes in v6:
time: 531 us; the launch traced here: 532 us
  Pallas kernels  187 us (35%)
  waiting for transfers between devices  174 us (33%)
  blocking collectives  69 us (13%)
  other arithmetic  40.3 us (8%)
  local copies, waits for them, and re-layouts  29.3 us (6%)
  between operations  16 us (3%)
  matrix products  11 us (2%)
    pallas_call x1, Pallas kernels, owner_backward(): pl.pallas_call(functools.partial(backward_kernel, requesters, length), gr...  97.3 us
    reduce_scatter x1, waiting for transfers between devices, local(): lax.psum_scatter(pooled_parts, 'table', scatter_dimension=0, tiled=True)  72.8 us
    all_gather x1, waiting for transfers between devices, local(): all_mixed = lax.all_gather(grad_mixed, ('table', 'rep'), axis=0, tiled=True)  65.1 us
    pallas_call x1, Pallas kernels, owner_forward(): pl.pallas_call(functools.partial(forward_kernel, blocks, length), grid_sp...  63.2 us
    all_to_all x1, blocking collectives, local(): lax.all_to_all(joined.reshape(batch_rows, devices, mix_part).transpose(1,...  37.8 us
    pallas_call x2, Pallas kernels, table_columns_grad(): pl.pallas_call(table_kernel, grid_spec=pltpu.PrefetchScalarGridSpec(num_s...  26.8 us
    all_gather x1, waiting for transfers between devices, local(): lax.all_gather(summed[:query_rows].astype(BF16), ('table', 'rep'), axis=0)  26.6 us
    all_to_all x1, blocking collectives, local(): lax.all_to_all(outgoing.astype(BF16), 'table', split_axis=0, concat_axis=...  20.2 us
  transfers between devices with their start and end apart: 9, of which 5 were waited for; matrix products, arithmetic and copies ran while one was open for 5% of the time, Pallas kernels for 35%

profile of v6, /device:TPU:0, one launch (start us, length us, event | category | flops | bytes accessed | tf_op | source)
XLA Modules:
  0.0 532.3 jit_solution(2916581508391556081)
XLA Ops:
  8.1 0.7 slice_convert_fusion.7
  8.8 0.8 add_select_fusion
  9.6 1.5 fusion.7
  11.1 3.2 sort.30
  14.3 0.2 convert_reduce_fusion.3
  14.4 0.8 divide_reduce-precision_fusion
  15.3 0.1 copy.50
  15.4 0.1 reshape.133
  15.5 0.1 copy.49
  15.6 0.1 reshape.132
  15.8 7.5 %sort.29 = (s32[9600]{0:T(1024)S(1)}, f32[9600]{0:T(1024)S(1)}) sort(s32[9600]{0:T(1024)S(1)} %reshape.132, f32[9600]{0:T(1024)S(1)} %reshape.133), dimensions={0}, to_apply=%region_1.2 | sort | flops 134400 | bytes 153600 | tf_op jit(solution)/shard_map/sort | solution.py:434
  23.3 0.2 convert_reduce_fusion.1
  23.6 0.7 select_dynamic-update-slice_fusion
  24.3 1.4 constant_dynamic-update-slice_fusion.1
  25.8 11.1 %all-gather.3 = f32[8,1,11392]{2,1,0:T(1,128)S(1)} all-gather(f32[1,1,11392]{2,1,0:T(1,128)S(1)} %reshape.161), channel_id=2, replica_groups=mesh['table'=8,'rep'=4] {'table'}, dimensions={0}, use_global_device_ids=true | all-gather | bytes 410112 | tf_op jit(solution)/shard_map/all_gather | solution.py:463
  37.1 15.9 %gather_fusion = bf16[1536,1024]{1,0:T(8,128)(2,1)S(1)} fusion(bf16[9216,1024]{1,0:T(8,128)(2,1)} %table_other.1, s32[2048]{0:T(1024)S(1)} %pad_clamp_fusion), kind=kCustom, calls=%fused_computation | custom fusion | bytes 6297600 | tf_op jit(solution)/shard_map/gather | solution.py:468
  53.0 2.1 broadcast_select_fusion
  55.2 0.5 all-gather.13.cloned.1.call-update
  55.8 0.3 copy-done.1
  56.3 0.8 copy.52.shares
  57.2 0.8 copy.51.codes
  58.1 0.7 maximum_convert_fusion.1.bounds
  58.7 63.2 %owner_forward.1 = (bf16[9216,1024]{1,0:T(8,128)(2,1)}, f32[1536,1024]{1,0:T(8,128)}) custom-call(s32[8,4]{1,0:T(8,128)} %maximum_convert_fusion.1.bounds, bf16[9216,1024]{1,0:T(8,128)(2,1)} %table_other.1, bf16[1024,1024]{1,0:T(8,128)(2,1)} %query.5, f32[1,1024]{1,0:T(1,128)} %bitcast.45, s32[8,1,5376]{2,1,0:T(1,128)} %copy.51.codes, f32[8,1,5376]{2,1,0:T(1,128)} %copy.52.shares), custom_call_target="tpu_custom_call" | custom-call | flops 19327352832 | bytes 37748736 | tf_op jit(solution)/shard_map/owner_forward/pallas_call | solution.py:127
  122.0 0.2 all-gather.9.cloned.1.call-start
  122.3 0.8 slice_convert_fusion.5
  123.0 0.6 reshape.140.self_codes
  123.7 0.8 slice.92
  124.5 0.7 maximum_convert_fusion.bounds
  125.2 0.8 slice_reduce_fusion
  126.0 1.4 slice_bitcast_fusion
  127.4 72.8 %reduce-scatter.5.cloned.1.call-done = f32[192,1024]{1,0:T(8,128)} async-done(((f32[1536,1024]{1,0:T(8,128)}), f32[192,1024]{1,0:T(8,128)}) %reduce-scatter.5.cloned.1.call-update) | async-done | bytes 786448 | tf_op jit(solution)/shard_map/reduce_scatter | solution.py:492
  200.3 1.2 reduce-precision_convert_fusion
  201.5 3.5 fusion.3
  205.0 1.2 fusion.2
  206.3 1.1 pad_maximum_fusion
  207.4 0.5 copy.53
  207.9 37.8 %all_to_all.10 = bf16[32,192,64]{1,2,0:T(8,128)(2,1)S(1)} all-to-all(bf16[32,192,64]{1,2,0:T(8,128)(2,1)S(1)} %bitcast.33), channel_id=1, replica_groups=mesh['table'=8,'rep'=4] {'table','rep'}, dimensions={0} | all-to-all | bytes 1572864 | tf_op jit(solution)/shard_map/all_to_all | solution.py:510
  245.7 0.6 copy.54
  246.2 1.1 reshape.143
  247.4 65.1 %all-gather.9.cloned.1.call-done.grads = bf16[6144,1024]{1,0:T(8,128)(2,1)} async-done(((bf16[192,1024]{1,0:T(8,128)(2,1)}), bf16[6144,1024]{1,0:T(8,128)(2,1)}) %all-gather.9.cloned.1.call-update) | async-done | bytes 12582928 | tf_op jit(solution)/shard_map/all_gather | solution.py:508
  312.5 7.5 %convolution_convert_fusion = bf16[64,1024]{1,0:T(8,128)(2,1)} fusion(bf16[6144,64]{0,1:T(8,128)(2,1)S(1)} %reshape.143, bf16[6144,1024]{1,0:T(8,128)(2,1)} %all-gather.9.cloned.1.call-done.grads), kind=kOutput, calls=%fused_computation.6 | convolution fusion | flops 805371904 | bytes 13500416 | tf_op jit(solution)/shard_map/dot_general | solution.py:518
  320.1 0.6 pad_add_fusion.place
  320.7 1.6 copy.55.codes
  322.2 1.6 copy.56.shares
  323.8 97.3 %owner_backward.1 = (bf16[4608,1024]{1,0:T(8,128)(2,1)}, bf16[4608,1024]{1,0:T(8,128)(2,1)}, f32[272,1024]{1,0:T(8,128)}, bf16[272,1024]{1,0:T(8,128)(2,1)}, f32[8,1024]{1,0:T(8,128)}) custom-call(s32[2]{0:T(128)} %pad_add_fusion.place, s32[32,4]{1,0:T(8,128)} %maximum_convert_fusion.bounds, s32[32,1,5376]{2,1,0:T(1,128)} %copy.55.codes, ...), custom_call_target="tpu_custom_call" | custom-call | flops 38654705664 | bytes 25165824 | tf_op jit(solution)/shard_map/owner_backward/pallas_call | solution.py:302
  421.1 0.4 collective-permute-start
  421.5 13.1 %table_columns_grad.3 = (bf16[4608,128]{1,0:T(8,128)(2,1)}, bf16[4608,128]{1,0:T(8,128)(2,1)}) custom-call(s32[1]{0:T(128)} %bitcast.10.place, bf16[4608,1024]{1,0:T(8,128)(2,1)} %get-tuple-element.49.grad_pre, bf16[4608,1024]{1,0:T(8,128)(2,1)} %get-tuple-element.50.self_sums, bf16[1024,1024]{1,0:T(8,128)(2,1)} %query.5, bf16[2048,1024]{1,0:T(8,128)(2,1)} %mix_self.3), custom_call_target="tpu_custom_call" | custom-call | flops 4831838208 | bytes 18874368 | tf_op jit(solution)/shard_map/table_columns_grad/pallas_call | solution.py:386
  434.7 1.7 collective-permute-start.1
  436.4 0.2 convert_add_fusion
  436.7 20.2 %all_to_all.11 = bf16[8,40,1024]{2,1,0:T(8,128)(2,1)S(1)} all-to-all(bf16[8,40,1024]{2,1,0:T(8,128)(2,1)S(1)} %pad_maximum_fusion.1), channel_id=1, replica_groups=mesh['table'=8,'rep'=4] {'table'}, dimensions={0} | all-to-all | bytes 1310720 | tf_op jit(solution)/shard_map/all_to_all | solution.py:562
  456.9 0.1 convert_reduce_fusion
  457.0 3.6 collective-permute-done.1
  460.6 0.6 slice.124
  461.2 2.4 collective-permute-start.2
  463.6 0.5 broadcast_multiply_fusion.1
  464.2 0.6 reduce_sum.99
  464.8 13.6 %table_columns_grad.2 = f32[9216,256]{1,0:T(8,128)} custom-call(s32[1]{0:T(128)} %bitcast.9.place, bf16[4608,1024]{1,0:T(8,128)(2,1)} %get-tuple-element.49.grad_pre, bf16[4608,1024]{1,0:T(8,128)(2,1)} %get-tuple-element.50.self_sums, bf16[1024,1024]{1,0:T(8,128)(2,1)} %query.5, bf16[2048,1024]{1,0:T(8,128)(2,1)} %mix_self.3), custom_call_target="tpu_custom_call" | custom-call | flops 4831838208 | bytes 18874368 | tf_op jit(solution)/shard_map/table_columns_grad/pallas_call | solution.py:386
  478.4 0.6 slice.97
  479.0 6.6 %convert_element_type.121 = f32[2048,1024]{1,0:T(8,128)} convert(bf16[2048,1024]{1,0:T(8,128)(2,1)} %all-gather.11.cloned.1.call-done) | non-fusion elementwise | flops 2097152 | bytes 12582912 | tf_op jit(solution)/shard_map/convert_element_type | solution.py:552
  485.6 5.7 %collective-permute-done.2 = bf16[4608,128]{1,0:T(8,128)(2,1)S(1)} collective-permute-done((bf16[4608,128]{1,0:T(8,128)(2,1)}, bf16[4608,128]{1,0:T(8,128)(2,1)S(1)}, u32[]{:S(2)}, u32[]{:S(2)}) %collective-permute-start.2) | collective-permute-done | bytes 1179680 | tf_op jit(solution)/shard_map/ppermute | solution.py:566
  491.3 2.5 convert_dynamic-update-slice_fusion
  493.8 26.6 %all-gather.15.cloned.1.call-done = bf16[1024,1024]{1,0:T(8,128)(2,1)} async-done(((bf16[32,1024]{1,0:T(8,128)(2,1)}), bf16[1024,1024]{1,0:T(8,128)(2,1)}) %all-gather.15.cloned.1.call-update) | async-done | bytes 2097168 | tf_op jit(solution)/shard_map/all_gather | solution.py:568
  520.4 2.1 convert_bitcast_fusion
  522.4 2.3 copy.57
  (55 shorter events, 1.2 us)
Async XLA Ops:
  8.0 113.9 %reduce-scatter.3.cloned.1.call-start = ((), (), s32[]{:S(2)}) async-start(), calls=%async_computation.4 | async-start | bytes 3538944 | tf_op jit(solution)/shard_map/reduce_scatter | solution.py:470
  36.8 16.2 %copy-start = (f32[8,1,11392]{2,0,1:T(8,128)}, f32[8,1,11392]{2,0,1:T(8,128)S(1)}, u32[]{:S(2)}) copy-start(f32[8,1,11392]{2,0,1:T(8,128)S(1)} %copy.60) | copy-start | bytes 1093636
  55.1 1.0 copy-start.1
  55.1 67.1 %all-gather.13.cloned.1.call-start = ((), (), s32[]{:S(2)}) async-start(), calls=%async_computation.8 | async-start | bytes 1822720 | tf_op jit(solution)/shard_map/all_gather | solution.py:471
  55.7 144.5 %reduce-scatter.5.cloned.1.call-start = ((), (), s32[]{:S(2)}) async-start(), calls=%async_computation.5 | async-start | bytes 7077888 | tf_op jit(solution)/shard_map/reduce_scatter | solution.py:492
  122.0 79.5 %copy-start.3 = (bf16[192,1024]{1,0:T(8,128)(2,1)S(1)}, bf16[192,1024]{1,0:T(8,128)(2,1)}, u32[]{:S(2)}) copy-start(bf16[192,1024]{1,0:T(8,128)(2,1)} %param.17) | copy-start | bytes 1179652
  122.0 79.5 %copy-start.5 = (f32[1024]{0:T(1024)S(1)}, f32[1024]{0:T(1024)}, u32[]{:S(2)}) copy-start(f32[1024]{0:T(1024)} %param.13) | copy-start | bytes 12292
  122.0 190.5 %all-gather.9.cloned.1.call-start = ((), (), s32[]{:S(2)}) async-start(), calls=%async_computation.6 | async-start | bytes 12976128 | tf_op jit(solution)/shard_map/all_gather | solution.py:508
  206.3 228.4 %all-gather.11.cloned.1.call-start = ((), (), s32[]{:S(2)}) async-start(), calls=%async_computation.7 | async-start | bytes 4325376 | tf_op jit(solution)/shard_map/all_gather | solution.py:522
  320.0 200.3 %all-gather.15.cloned.1.call-start = ((), (), s32[]{:S(2)}) async-start(), calls=%async_computation.9 | async-start | bytes 2162688 | tf_op jit(solution)/shard_map/all_gather | solution.py:568
  421.1 15.3 %collective-permute-start = (bf16[272,1024]{1,0:T(8,128)(2,1)}, bf16[272,1024]{1,0:T(8,128)(2,1)S(1)}, u32[]{:S(2)}, u32[]{:S(2)}) collective-permute-start(bf16[272,1024]{1,0:T(8,128)(2,1)} %get-tuple-element.52), channel_id=1, source_target_pairs={{0,1},{1,0},{2,3},{3,2},{4,5},{5,4},{6,7},{7,6},{8,9},{9,8},{10,11... | collective-permute-start | bytes 1671176 | tf_op jit(solution)/shard_map/ppermute | solution.py:550
  421.5 14.9 %copy-start.2 = (f32[272,1024]{1,0:T(8,128)S(1)}, f32[272,1024]{1,0:T(8,128)}, u32[]{:S(2)}) copy-start(f32[272,1024]{1,0:T(8,128)} %get-tuple-element.51) | copy-start | bytes 3342340
  434.7 25.9 %collective-permute-start.1 = (bf16[4608,128]{1,0:T(8,128)(2,1)}, bf16[4608,128]{1,0:T(8,128)(2,1)S(1)}, u32[]{:S(2)}, u32[]{:S(2)}) collective-permute-start(bf16[4608,128]{1,0:T(8,128)(2,1)} %get-tuple-element.55), channel_id=1, source_target_pairs={{0,1},{1,0},{2,3},{3,2},{4,5},{5,4},{6,7},{7,6},{8,9},{9,8},{10,11... | collective-permute-start | bytes 3538952 | tf_op jit(solution)/shard_map/ppermute | solution.py:553
  436.4 27.8 %copy-start.4 = (f32[8,1024]{1,0:T(8,128)S(1)}, f32[8,1024]{1,0:T(8,128)}, u32[]{:S(2)}) copy-start(f32[8,1024]{1,0:T(8,128)} %get-tuple-element.60) | copy-start | bytes 98308
  461.2 30.0 %collective-permute-start.2 = (bf16[4608,128]{1,0:T(8,128)(2,1)}, bf16[4608,128]{1,0:T(8,128)(2,1)S(1)}, u32[]{:S(2)}, u32[]{:S(2)}) collective-permute-start(bf16[4608,128]{1,0:T(8,128)(2,1)} %get-tuple-element.57), channel_id=1, source_target_pairs={{0,1},{1,0},{2,3},{3,2},{4,5},{5,4},{6,7},{7,6},{8,9},{9,8},{10,11... | collective-permute-start | bytes 3538952 | tf_op jit(solution)/shard_map/ppermute | solution.py:566
Sparse Core Ops, SparseCore 0:
  55.3 46.3 reduce-scatter.2
  122.1 78.1 reduce-scatter.4
Sparse Core Ops, SparseCore 1:
  57.8 35.2 all-gather.12
  206.3 106.1 all-gather.8
  320.1 60.3 all-gather.10
  461.3 59.0 all-gather.14

commit v7 on v6

--- a/solution.py
+++ b/solution.py
@@ -565,8 +565,15 @@
     summed, got_first = lax.optimization_barrier((summed, got_first))
     got_last = lax.ppermute(send_last, "rep", swap)
     table_got = jnp.concatenate([got_first, got_last], axis=1)
-    gathered = lax.all_gather(summed[:query_rows].astype(BF16), ("table", "rep"), axis=0).reshape(
-        owners, groups, query_rows, width
+    column = lax.all_to_all(
+        jnp.broadcast_to(summed[:query_rows].astype(BF16), (groups, query_rows, width)),
+        "rep",
+        split_axis=0,
+        concat_axis=0,
+        tiled=True,
+    )
+    gathered = lax.all_to_all(
+        jnp.broadcast_to(column, (owners, groups, query_rows, width)), "table", split_axis=0, concat_axis=0, tiled=True
     )
     query_weight_grad = gathered.transpose(1, 0, 2, 3).reshape(width, width).astype(F32)
     table_grad = lax.dynamic_update_slice(

time: 531 us -> 522 us (0.983); the launches traced: 532 us -> 517 us
  waiting for transfers between devices: 174 us -> 140 us
  Pallas kernels: 187 us -> 201 us
  starting transfers between devices: 4.99 us -> 15.5 us
  blocking collectives: 69 us -> 62.3 us
    all_gather x1 -> x0, waiting for transfers between devices: 26.6 us -> none  [local(): lax.all_gather(summed[:query_rows].astype(BF16), ('table', 'rep'), axis=0)]
    all_to_all x0 -> x2, starting transfers between devices: none -> 11 us  [the longest x1 7.58 us: local(): lax.all_to_all(jnp.broadcast_to(column, (owners, groups, query_rows, widt...]
    reduce_scatter x1, waiting for transfers between devices: 72.8 us -> 62.6 us  [local(): lax.psum_scatter(pooled_parts, 'table', scatter_dimension=0, tiled=True)]
    pallas_call x1, Pallas kernels: 63.2 us -> 71.3 us  [owner_forward(): pl.pallas_call(functools.partial(forward_kernel, blocks, length), grid_sp...]
    all_to_all x1, blocking collectives: 20.2 us -> 13.5 us  [local(): lax.all_to_all(outgoing.astype(BF16), 'table', split_axis=0, concat_axis=...]
    all_to_all x0 -> x2, waiting for transfers between devices: none -> 5.84 us  [the longest x1 4.95 us: local(): lax.all_to_all(jnp.broadcast_to(summed[:query_rows].astype(BF16), (groups...]
    ppermute x1, waiting for transfers between devices: 5.67 us -> 0.01 us  [local(): got_last = lax.ppermute(send_last, 'rep', swap)]
    pallas_call x1, Pallas kernels: 97.3 us -> 103 us  [owner_backward(): pl.pallas_call(functools.partial(backward_kernel, requesters, length), gr...]
  transfers between devices with their start and end apart: 9 -> 10, of which waited for: 5 -> 5; matrix products, arithmetic and copies ran while one was open for 5% -> 6% of each run, Pallas kernels for 35% -> 39%
where the time goes in v7:
time: 522 us; the launch traced here: 517 us
  Pallas kernels  201 us (39%)
  waiting for transfers between devices  140 us (27%)
  blocking collectives  62.3 us (12%)
  other arithmetic  42 us (8%)
  local copies, waits for them, and re-layouts  28.7 us (5%)
  between operations  16 us (3%)
  starting transfers between devices  15.5 us (3%)
  matrix products  11 us (2%)
    pallas_call x1, Pallas kernels, owner_backward(): pl.pallas_call(functools.partial(backward_kernel, requesters, length), gr...  103 us
    pallas_call x1, Pallas kernels, owner_forward(): pl.pallas_call(functools.partial(forward_kernel, blocks, length), grid_sp...  71.3 us
    all_gather x1, waiting for transfers between devices, local(): all_mixed = lax.all_gather(grad_mixed, ('table', 'rep'), axis=0, tiled=True)  65.1 us
    reduce_scatter x1, waiting for transfers between devices, local(): lax.psum_scatter(pooled_parts, 'table', scatter_dimension=0, tiled=True)  62.6 us
    all_to_all x1, blocking collectives, local(): lax.all_to_all(joined.reshape(batch_rows, devices, mix_part).transpose(1,...  37.8 us
    pallas_call x2, Pallas kernels, table_columns_grad(): pl.pallas_call(table_kernel, grid_spec=pltpu.PrefetchScalarGridSpec(num_s...  26.8 us
    gather x1, local copies, waits for them, and re-layouts, local(): found = feature_table[jnp.clip(wanted, 0, rows_owned - 1)]  15.9 us
    all_to_all x1, blocking collectives, local(): lax.all_to_all(outgoing.astype(BF16), 'table', split_axis=0, concat_axis=...  13.5 us
  transfers between devices with their start and end apart: 10, of which 5 were waited for; matrix products, arithmetic and copies ran while one was open for 6% of the time, Pallas kernels for 39%

profile of v7, /device:TPU:0, one launch (start us, length us, event | category | flops | bytes accessed | tf_op | source)
XLA Modules:
  0.0 516.6 jit_solution(10753607906914068261)
XLA Ops:
  8.1 0.7 slice_convert_fusion.7
  8.8 0.8 add_select_fusion
  9.6 1.5 fusion.7
  11.1 3.2 sort.30
  14.3 0.2 convert_reduce_fusion.3
  14.4 0.8 divide_reduce-precision_fusion
  15.4 0.1 reshape.130
  15.5 0.1 copy.51
  15.6 0.1 reshape.129
  15.8 7.5 %sort.29 = (s32[9600]{0:T(1024)S(1)}, f32[9600]{0:T(1024)S(1)}) sort(s32[9600]{0:T(1024)S(1)} %reshape.129, f32[9600]{0:T(1024)S(1)} %reshape.130), dimensions={0}, to_apply=%region_1.2 | sort | flops 134400 | bytes 153600 | tf_op jit(solution)/shard_map/sort | solution.py:434
  23.3 0.2 convert_reduce_fusion.1
  23.6 0.7 select_dynamic-update-slice_fusion
  24.3 1.4 constant_dynamic-update-slice_fusion.1
  25.8 11.1 %all-gather.2 = f32[8,1,11392]{2,1,0:T(1,128)S(1)} all-gather(f32[1,1,11392]{2,1,0:T(1,128)S(1)} %reshape.154), channel_id=2, replica_groups=mesh['table'=8,'rep'=4] {'table'}, dimensions={0}, use_global_device_ids=true | all-gather | bytes 410112 | tf_op jit(solution)/shard_map/all_gather | solution.py:463
  37.1 15.9 %gather_fusion = bf16[1536,1024]{1,0:T(8,128)(2,1)S(1)} fusion(bf16[9216,1024]{1,0:T(8,128)(2,1)} %table_other.1, s32[2048]{0:T(1024)S(1)} %pad_clamp_fusion), kind=kCustom, calls=%fused_computation | custom fusion | bytes 6297600 | tf_op jit(solution)/shard_map/gather | solution.py:468
  53.0 2.1 broadcast_select_fusion
  55.2 0.5 all-gather.11.cloned.1.call-update
  55.8 0.3 copy-done.1
  56.3 0.8 copy.54.shares
  57.2 0.8 copy.53.codes
  58.1 0.7 maximum_convert_fusion.1.bounds
  58.7 71.3 %owner_forward.1 = (bf16[9216,1024]{1,0:T(8,128)(2,1)}, f32[1536,1024]{1,0:T(8,128)}) custom-call(s32[8,4]{1,0:T(8,128)} %maximum_convert_fusion.1.bounds, bf16[9216,1024]{1,0:T(8,128)(2,1)} %table_other.1, bf16[1024,1024]{1,0:T(8,128)(2,1)} %query.5, f32[1,1024]{1,0:T(1,128)} %bitcast.42, s32[8,1,5376]{2,1,0:T(1,128)} %copy.53.codes, f32[8,1,5376]{2,1,0:T(1,128)} %copy.54.shares), custom_call_target="tpu_custom_call" | custom-call | flops 19327352832 | bytes 37748736 | tf_op jit(solution)/shard_map/owner_forward/pallas_call | solution.py:127
  130.1 0.2 all-gather.7.cloned.1.call-start
  130.4 0.8 slice_convert_fusion.5
  131.2 0.6 reshape.137.self_codes
  131.8 0.8 slice.92
  132.7 0.7 maximum_convert_fusion.bounds
  133.3 0.8 slice_reduce_fusion
  134.1 1.4 slice_bitcast_fusion
  135.5 62.6 %reduce-scatter.5.cloned.1.call-done = f32[192,1024]{1,0:T(8,128)} async-done(((f32[1536,1024]{1,0:T(8,128)}), f32[192,1024]{1,0:T(8,128)}) %reduce-scatter.5.cloned.1.call-update) | async-done | bytes 786448 | tf_op jit(solution)/shard_map/reduce_scatter | solution.py:492
  198.2 1.2 reduce-precision_convert_fusion
  199.4 3.5 fusion.3
  202.9 1.2 fusion.2
  204.2 1.1 pad_maximum_fusion
  205.3 0.5 copy.55
  205.8 37.8 %all_to_all.20 = bf16[32,192,64]{1,2,0:T(8,128)(2,1)S(1)} all-to-all(bf16[32,192,64]{1,2,0:T(8,128)(2,1)S(1)} %bitcast.32), channel_id=1, replica_groups=mesh['table'=8,'rep'=4] {'table','rep'}, dimensions={0} | all-to-all | bytes 1572864 | tf_op jit(solution)/shard_map/all_to_all | solution.py:510
  243.6 0.6 copy.56
  244.1 1.1 reshape.140
  245.3 65.1 %all-gather.7.cloned.1.call-done.grads = bf16[6144,1024]{1,0:T(8,128)(2,1)} async-done(((bf16[192,1024]{1,0:T(8,128)(2,1)}), bf16[6144,1024]{1,0:T(8,128)(2,1)}) %all-gather.7.cloned.1.call-update) | async-done | bytes 12582928 | tf_op jit(solution)/shard_map/all_gather | solution.py:508
  310.4 7.5 %convolution_convert_fusion = bf16[64,1024]{1,0:T(8,128)(2,1)} fusion(bf16[6144,64]{0,1:T(8,128)(2,1)S(1)} %reshape.140, bf16[6144,1024]{1,0:T(8,128)(2,1)} %all-gather.7.cloned.1.call-done.grads), kind=kOutput, calls=%fused_computation.6 | convolution fusion | flops 805371904 | bytes 13500416 | tf_op jit(solution)/shard_map/dot_general | solution.py:518
  318.0 0.6 pad_add_fusion.place
  318.5 1.6 copy.57.codes
  320.1 1.6 copy.58.shares
  321.7 102.9 %owner_backward.1 = (bf16[4608,1024]{1,0:T(8,128)(2,1)}, bf16[4608,1024]{1,0:T(8,128)(2,1)}, f32[272,1024]{1,0:T(8,128)}, bf16[272,1024]{1,0:T(8,128)(2,1)}, f32[8,1024]{1,0:T(8,128)}) custom-call(s32[2]{0:T(128)} %pad_add_fusion.place, s32[32,4]{1,0:T(8,128)} %maximum_convert_fusion.bounds, s32[32,1,5376]{2,1,0:T(1,128)} %copy.57.codes, ...), custom_call_target="tpu_custom_call" | custom-call | flops 38654705664 | bytes 25165824 | tf_op jit(solution)/shard_map/owner_backward/pallas_call | solution.py:302
  424.6 0.9 collective-permute-start
  425.5 13.1 %table_columns_grad.3 = (bf16[4608,128]{1,0:T(8,128)(2,1)}, bf16[4608,128]{1,0:T(8,128)(2,1)}) custom-call(s32[1]{0:T(128)} %bitcast.10.place, bf16[4608,1024]{1,0:T(8,128)(2,1)} %get-tuple-element.49.grad_pre, bf16[4608,1024]{1,0:T(8,128)(2,1)} %get-tuple-element.50.self_sums, bf16[1024,1024]{1,0:T(8,128)(2,1)} %query.5, bf16[2048,1024]{1,0:T(8,128)(2,1)} %mix_self.3), custom_call_target="tpu_custom_call" | custom-call | flops 4831838208 | bytes 18874368 | tf_op jit(solution)/shard_map/table_columns_grad/pallas_call | solution.py:386
  438.7 1.2 collective-permute-start.1
  439.9 0.2 convert_add_fusion
  440.2 13.5 %all_to_all.21 = bf16[8,40,1024]{2,1,0:T(8,128)(2,1)S(1)} all-to-all(bf16[8,40,1024]{2,1,0:T(8,128)(2,1)S(1)} %pad_maximum_fusion.1), channel_id=1, replica_groups=mesh['table'=8,'rep'=4] {'table'}, dimensions={0} | all-to-all | bytes 1310720 | tf_op jit(solution)/shard_map/all_to_all | solution.py:562
  453.8 5.9 %collective-permute-done.1 = bf16[4608,128]{1,0:T(8,128)(2,1)S(1)} collective-permute-done((bf16[4608,128]{1,0:T(8,128)(2,1)}, bf16[4608,128]{1,0:T(8,128)(2,1)S(1)}, u32[]{:S(2)}, u32[]{:S(2)}) %collective-permute-start.1) | collective-permute-done | bytes 1179680 | tf_op jit(solution)/shard_map/ppermute | solution.py:553
  459.7 0.7 broadcast_in_dim.44
  460.4 3.4 all-to-all-start.2
  463.8 2.0 collective-permute-start.2
  465.8 4.9 all-to-all-done.2
  470.8 1.6 broadcast_in_dim.45
  472.4 7.6 %all-to-all-start.3 = ((bf16[8,4,32,1024]{3,2,1,0:T(8,128)(2,1)}), bf16[8,4,32,1024]{3,2,1,0:T(8,128)(2,1)S(1)}, u32[]{:S(2)}, u32[]{:S(2)}) async-start(bf16[8,4,32,1024]{3,2,1,0:T(8,128)(2,1)} %broadcast_in_dim.45), calls=%async_computation.5 | async-start | bytes 4194304 | tf_op jit(solution)/shard_map/all_to_all | solution.py:575
  479.9 0.5 broadcast_multiply_fusion.1
  480.5 0.6 reduce_sum.99
  481.1 13.6 %table_columns_grad.2 = f32[9216,256]{1,0:T(8,128)} custom-call(s32[1]{0:T(128)} %bitcast.9.place, bf16[4608,1024]{1,0:T(8,128)(2,1)} %get-tuple-element.49.grad_pre, bf16[4608,1024]{1,0:T(8,128)(2,1)} %get-tuple-element.50.self_sums, bf16[1024,1024]{1,0:T(8,128)(2,1)} %query.5, bf16[2048,1024]{1,0:T(8,128)(2,1)} %mix_self.3), custom_call_target="tpu_custom_call" | custom-call | flops 4831838208 | bytes 18874368 | tf_op jit(solution)/shard_map/table_columns_grad/pallas_call | solution.py:386
  494.7 0.6 slice.97
  495.3 6.6 %convert_element_type.117 = f32[2048,1024]{1,0:T(8,128)} convert(bf16[2048,1024]{1,0:T(8,128)(2,1)} %all-gather.9.cloned.1.call-done) | non-fusion elementwise | flops 2097152 | bytes 12582912 | tf_op jit(solution)/shard_map/convert_element_type | solution.py:552
  501.9 3.8 convert_dynamic-update-slice_fusion
  505.7 0.9 all-to-all-done.3
  506.5 2.5 copy_convert_fusion
  (57 shorter events, 1.3 us)
Async XLA Ops:
  8.0 122.1 %reduce-scatter.3.cloned.1.call-start = ((), (), s32[]{:S(2)}) async-start(), calls=%async_computation.6 | async-start | bytes 3538944 | tf_op jit(solution)/shard_map/reduce_scatter | solution.py:470
  36.8 16.2 %copy-start = (f32[8,1,11392]{2,0,1:T(8,128)}, f32[8,1,11392]{2,0,1:T(8,128)S(1)}, u32[]{:S(2)}) copy-start(f32[8,1,11392]{2,0,1:T(8,128)S(1)} %copy.63) | copy-start | bytes 1093636
  55.1 1.0 copy-start.1
  55.1 75.2 %all-gather.11.cloned.1.call-start = ((), (), s32[]{:S(2)}) async-start(), calls=%async_computation.10 | async-start | bytes 1822720 | tf_op jit(solution)/shard_map/all_gather | solution.py:471
  55.7 142.4 %reduce-scatter.5.cloned.1.call-start = ((), (), s32[]{:S(2)}) async-start(), calls=%async_computation.7 | async-start | bytes 7077888 | tf_op jit(solution)/shard_map/reduce_scatter | solution.py:492
  130.1 69.3 %copy-start.3 = (bf16[192,1024]{1,0:T(8,128)(2,1)S(1)}, bf16[192,1024]{1,0:T(8,128)(2,1)}, u32[]{:S(2)}) copy-start(bf16[192,1024]{1,0:T(8,128)(2,1)} %param.17) | copy-start | bytes 1179652
  130.1 69.3 %copy-start.5 = (f32[1024]{0:T(1024)S(1)}, f32[1024]{0:T(1024)}, u32[]{:S(2)}) copy-start(f32[1024]{0:T(1024)} %param.13) | copy-start | bytes 12292
  130.1 180.3 %all-gather.7.cloned.1.call-start = ((), (), s32[]{:S(2)}) async-start(), calls=%async_computation.8 | async-start | bytes 12976128 | tf_op jit(solution)/shard_map/all_gather | solution.py:508
  204.2 234.5 %all-gather.9.cloned.1.call-start = ((), (), s32[]{:S(2)}) async-start(), calls=%async_computation.9 | async-start | bytes 4325376 | tf_op jit(solution)/shard_map/all_gather | solution.py:522
  424.6 15.3 %collective-permute-start = (bf16[272,1024]{1,0:T(8,128)(2,1)}, bf16[272,1024]{1,0:T(8,128)(2,1)S(1)}, u32[]{:S(2)}, u32[]{:S(2)}) collective-permute-start(bf16[272,1024]{1,0:T(8,128)(2,1)} %get-tuple-element.52), channel_id=1, source_target_pairs={{0,1},{1,0},{2,3},{3,2},{4,5},{5,4},{6,7},{7,6},{8,9},{9,8},{10,11... | collective-permute-start | bytes 1671176 | tf_op jit(solution)/shard_map/ppermute | solution.py:550
  425.5 14.3 %copy-start.2 = (f32[272,1024]{1,0:T(8,128)S(1)}, f32[272,1024]{1,0:T(8,128)}, u32[]{:S(2)}) copy-start(f32[272,1024]{1,0:T(8,128)} %get-tuple-element.51) | copy-start | bytes 3342340
  438.7 21.0 %collective-permute-start.1 = (bf16[4608,128]{1,0:T(8,128)(2,1)}, bf16[4608,128]{1,0:T(8,128)(2,1)S(1)}, u32[]{:S(2)}, u32[]{:S(2)}) collective-permute-start(bf16[4608,128]{1,0:T(8,128)(2,1)} %get-tuple-element.55), channel_id=1, source_target_pairs={{0,1},{1,0},{2,3},{3,2},{4,5},{5,4},{6,7},{7,6},{8,9},{9,8},{10,11... | collective-permute-start | bytes 3538952 | tf_op jit(solution)/shard_map/ppermute | solution.py:553
  460.4 10.4 %all-to-all-start.2 = ((bf16[4,32,1024]{2,1,0:T(8,128)(2,1)}), bf16[4,32,1024]{2,1,0:T(8,128)(2,1)S(1)}, u32[]{:S(2)}, u32[]{:S(2)}) async-start(bf16[4,32,1024]{2,1,0:T(8,128)(2,1)} %broadcast_in_dim.44), calls=%async_computation.4 | async-start | bytes 524288 | tf_op jit(solution)/shard_map/all_to_all | solution.py:568
  463.8 16.6 %copy-start.4 = (f32[8,1024]{1,0:T(8,128)S(1)}, f32[8,1024]{1,0:T(8,128)}, u32[]{:S(2)}) copy-start(f32[8,1024]{1,0:T(8,128)} %get-tuple-element.60) | copy-start | bytes 98308
  463.8 38.0 %collective-permute-start.2 = (bf16[4608,128]{1,0:T(8,128)(2,1)}, bf16[4608,128]{1,0:T(8,128)(2,1)}, u32[]{:S(2)}, u32[]{:S(2)}) collective-permute-start(bf16[4608,128]{1,0:T(8,128)(2,1)} %get-tuple-element.57), channel_id=1, source_target_pairs={{0,1},{1,0},{2,3},{3,2},{4,5},{5,4},{6,7},{7,6},{8,9},{9,8},{10,11... | collective-permute-start | bytes 3538952 | tf_op jit(solution)/shard_map/ppermute | solution.py:566
  472.4 34.2 %all-to-all-start.3 = ((bf16[8,4,32,1024]{3,2,1,0:T(8,128)(2,1)}), bf16[8,4,32,1024]{3,2,1,0:T(8,128)(2,1)S(1)}, u32[]{:S(2)}, u32[]{:S(2)}) async-start(bf16[8,4,32,1024]{3,2,1,0:T(8,128)(2,1)} %broadcast_in_dim.45), calls=%async_computation.5 | async-start | bytes 4194304 | tf_op jit(solution)/shard_map/all_to_all | solution.py:575
Sparse Core Ops, SparseCore 0:
  55.3 46.3 reduce-scatter.2
  130.2 67.9 reduce-scatter.4
Sparse Core Ops, SparseCore 1:
  57.8 35.2 all-gather.10
  204.2 106.1 all-gather.6
  318.0 60.2 all-gather.8

commit v8 on v7

--- a/solution.py
+++ b/solution.py
@@ -562,7 +562,9 @@
     incoming = lax.all_to_all(outgoing.astype(BF16), "table", split_axis=0, concat_axis=0, tiled=True)
     summed = jnp.sum(incoming.astype(F32), axis=0)
     query_bias_grad = summed[query_rows]
-    summed, got_first = lax.optimization_barrier((summed, got_first))
+    summed, got_first, table_grad, mix_weight_grad = lax.optimization_barrier(
+        (summed, got_first, table_grad, mix_weight_grad)
+    )
     got_last = lax.ppermute(send_last, "rep", swap)
     table_got = jnp.concatenate([got_first, got_last], axis=1)
     column = lax.all_to_all(

time: 522 us -> 527 us (level); the launches traced: 517 us -> 531 us
  waiting for transfers between devices: 140 us -> 160 us
  blocking collectives: 62.3 us -> 48.8 us
  starting transfers between devices: 15.5 us -> 27.7 us
    ppermute x1, waiting for transfers between devices: 0.01 us -> 16 us  [local(): got_last = lax.ppermute(send_last, 'rep', swap)]
    all_to_all x0 -> x1, starting transfers between devices: none -> 15.6 us  [local(): lax.all_to_all(outgoing.astype(BF16), 'table', split_axis=0, concat_axis=...]
    all_to_all x1 -> x0, blocking collectives: 13.5 us -> none  [local(): lax.all_to_all(outgoing.astype(BF16), 'table', split_axis=0, concat_axis=...]
    ppermute x1, waiting for transfers between devices: 5.89 us -> 0.01 us  [local(): got_first = lax.ppermute(send_first, 'rep', swap)]
  transfers between devices with their start and end apart: 10 -> 11, of which waited for: 5 -> 5; matrix products, arithmetic and copies ran while one was open for 6% -> 6% of each run, Pallas kernels for 39% -> 37%
where the time goes in v8:
time: 527 us; the launch traced here: 531 us
  Pallas kernels  196 us (37%)
  waiting for transfers between devices  160 us (30%)
  blocking collectives  48.8 us (9%)
  other arithmetic  42.8 us (8%)
  local copies, waits for them, and re-layouts  28.7 us (5%)
  starting transfers between devices  27.7 us (5%)
  between operations  16 us (3%)
  matrix products  11 us (2%)
    pallas_call x1, Pallas kernels, owner_backward(): pl.pallas_call(functools.partial(backward_kernel, requesters, length), gr...  98.8 us
    pallas_call x1, Pallas kernels, owner_forward(): pl.pallas_call(functools.partial(forward_kernel, blocks, length), grid_sp...  70.2 us
    reduce_scatter x1, waiting for transfers between devices, local(): lax.psum_scatter(pooled_parts, 'table', scatter_dimension=0, tiled=True)  65.7 us
    all_gather x1, waiting for transfers between devices, local(): all_mixed = lax.all_gather(grad_mixed, ('table', 'rep'), axis=0, tiled=True)  65.1 us
    all_to_all x1, blocking collectives, local(): lax.all_to_all(joined.reshape(batch_rows, devices, mix_part).transpose(1,...  37.8 us
    pallas_call x2, Pallas kernels, table_columns_grad(): pl.pallas_call(table_kernel, grid_spec=pltpu.PrefetchScalarGridSpec(num_s...  26.8 us
    ppermute x1, waiting for transfers between devices, local(): got_last = lax.ppermute(send_last, 'rep', swap)  16 us
    gather x1, local copies, waits for them, and re-layouts, local(): found = feature_table[jnp.clip(wanted, 0, rows_owned - 1)]  15.9 us
  transfers between devices with their start and end apart: 11, of which 5 were waited for; matrix products, arithmetic and copies ran while one was open for 6% of the time, Pallas kernels for 37%

profile of v8, /device:TPU:0, one launch (start us, length us, event | category | flops | bytes accessed | tf_op | source)
XLA Modules:
  0.0 530.8 jit_solution(5052471151656808306)
XLA Ops:
  8.1 0.7 slice_convert_fusion.7
  8.8 0.8 add_select_fusion
  9.6 1.5 fusion.7
  11.1 3.2 sort.30
  14.3 0.2 convert_reduce_fusion.3
  14.4 0.8 divide_reduce-precision_fusion
  15.4 0.1 reshape.128
  15.6 0.1 reshape.127
  15.8 7.5 %sort.29 = (s32[9600]{0:T(1024)S(1)}, f32[9600]{0:T(1024)S(1)}) sort(s32[9600]{0:T(1024)S(1)} %reshape.127, f32[9600]{0:T(1024)S(1)} %reshape.128), dimensions={0}, to_apply=%region_1.2 | sort | flops 134400 | bytes 153600 | tf_op jit(solution)/shard_map/sort | solution.py:434
  23.3 0.2 convert_reduce_fusion.1
  23.6 0.7 select_dynamic-update-slice_fusion
  24.3 1.4 constant_dynamic-update-slice_fusion.1
  25.8 11.1 %all-gather.2 = f32[8,1,11392]{2,1,0:T(1,128)S(1)} all-gather(f32[1,1,11392]{2,1,0:T(1,128)S(1)} %reshape.151), channel_id=2, replica_groups=mesh['table'=8,'rep'=4] {'table'}, dimensions={0}, use_global_device_ids=true | all-gather | bytes 410112 | tf_op jit(solution)/shard_map/all_gather | solution.py:463
  37.1 15.9 %gather_fusion = bf16[1536,1024]{1,0:T(8,128)(2,1)S(1)} fusion(bf16[9216,1024]{1,0:T(8,128)(2,1)} %table_other.1, s32[2048]{0:T(1024)S(1)} %pad_clamp_fusion), kind=kCustom, calls=%fused_computation | custom fusion | bytes 6297600 | tf_op jit(solution)/shard_map/gather | solution.py:468
  53.0 2.1 broadcast_select_fusion
  55.2 0.5 all-gather.11.cloned.1.call-update
  55.8 0.3 copy-done.1
  56.3 0.8 copy.54.shares
  57.2 0.8 copy.53.codes
  58.1 0.7 maximum_convert_fusion.1.bounds
  58.7 70.2 %owner_forward.1 = (bf16[9216,1024]{1,0:T(8,128)(2,1)}, f32[1536,1024]{1,0:T(8,128)}) custom-call(s32[8,4]{1,0:T(8,128)} %maximum_convert_fusion.1.bounds, bf16[9216,1024]{1,0:T(8,128)(2,1)} %table_other.1, bf16[1024,1024]{1,0:T(8,128)(2,1)} %query.5, f32[1,1024]{1,0:T(1,128)} %bitcast.42, s32[8,1,5376]{2,1,0:T(1,128)} %copy.53.codes, f32[8,1,5376]{2,1,0:T(1,128)} %copy.54.shares), custom_call_target="tpu_custom_call" | custom-call | flops 19327352832 | bytes 37748736 | tf_op jit(solution)/shard_map/owner_forward/pallas_call | solution.py:127
  129.0 0.2 all-gather.7.cloned.1.call-start
  129.3 0.8 slice_convert_fusion.5
  130.1 0.6 reshape.135.self_codes
  130.7 0.8 slice.92
  131.6 0.7 maximum_convert_fusion.bounds
  132.3 0.8 slice_reduce_fusion
  133.1 1.4 slice_bitcast_fusion
  134.5 65.7 %reduce-scatter.5.cloned.1.call-done = f32[192,1024]{1,0:T(8,128)} async-done(((f32[1536,1024]{1,0:T(8,128)}), f32[192,1024]{1,0:T(8,128)}) %reduce-scatter.5.cloned.1.call-update) | async-done | bytes 786448 | tf_op jit(solution)/shard_map/reduce_scatter | solution.py:492
  200.2 1.2 reduce-precision_convert_fusion
  201.4 3.5 fusion.3
  204.9 1.2 fusion.2
  206.2 1.1 pad_maximum_fusion
  207.3 0.5 copy.55
  207.8 37.8 %all_to_all.20 = bf16[32,192,64]{1,2,0:T(8,128)(2,1)S(1)} all-to-all(bf16[32,192,64]{1,2,0:T(8,128)(2,1)S(1)} %bitcast.32), channel_id=1, replica_groups=mesh['table'=8,'rep'=4] {'table','rep'}, dimensions={0} | all-to-all | bytes 1572864 | tf_op jit(solution)/shard_map/all_to_all | solution.py:510
  245.5 0.6 copy.56
  246.1 1.1 reshape.137
  247.3 65.1 %all-gather.7.cloned.1.call-done.grads = bf16[6144,1024]{1,0:T(8,128)(2,1)} async-done(((bf16[192,1024]{1,0:T(8,128)(2,1)}), bf16[6144,1024]{1,0:T(8,128)(2,1)}) %all-gather.7.cloned.1.call-update) | async-done | bytes 12582928 | tf_op jit(solution)/shard_map/all_gather | solution.py:508
  312.4 7.5 %convolution_convert_fusion = bf16[64,1024]{1,0:T(8,128)(2,1)} fusion(bf16[6144,64]{0,1:T(8,128)(2,1)S(1)} %reshape.137, bf16[6144,1024]{1,0:T(8,128)(2,1)} %all-gather.7.cloned.1.call-done.grads), kind=kOutput, calls=%fused_computation.6 | convolution fusion | flops 805371904 | bytes 13500416 | tf_op jit(solution)/shard_map/dot_general | solution.py:518
  319.9 0.6 pad_add_fusion.place
  320.5 1.6 copy.57.codes
  322.1 1.6 copy.58.shares
  323.6 98.8 %owner_backward.1 = (bf16[4608,1024]{1,0:T(8,128)(2,1)}, bf16[4608,1024]{1,0:T(8,128)(2,1)}, f32[272,1024]{1,0:T(8,128)}, bf16[272,1024]{1,0:T(8,128)(2,1)}, f32[8,1024]{1,0:T(8,128)}) custom-call(s32[2]{0:T(128)} %pad_add_fusion.place, s32[32,4]{1,0:T(8,128)} %maximum_convert_fusion.bounds, s32[32,1,5376]{2,1,0:T(1,128)} %copy.57.codes, ...), custom_call_target="tpu_custom_call" | custom-call | flops 38654705664 | bytes 25165824 | tf_op jit(solution)/shard_map/owner_backward/pallas_call | solution.py:302
  422.5 0.7 collective-permute-start
  423.1 13.1 %table_columns_grad.2 = (bf16[4608,128]{1,0:T(8,128)(2,1)}, bf16[4608,128]{1,0:T(8,128)(2,1)}) custom-call(s32[1]{0:T(128)} %bitcast.10.place, bf16[4608,1024]{1,0:T(8,128)(2,1)} %get-tuple-element.53.grad_pre, bf16[4608,1024]{1,0:T(8,128)(2,1)} %get-tuple-element.54.self_sums, bf16[1024,1024]{1,0:T(8,128)(2,1)} %query.5, bf16[2048,1024]{1,0:T(8,128)(2,1)} %mix_self.3), custom_call_target="tpu_custom_call" | custom-call | flops 4831838208 | bytes 18874368 | tf_op jit(solution)/shard_map/table_columns_grad/pallas_call | solution.py:386
  436.3 1.5 collective-permute-start.1
  437.7 0.2 convert_add_fusion
  438.0 0.9 pad_maximum_fusion.1
  438.9 15.6 %all-to-all-start.1 = ((bf16[8,40,1024]{2,1,0:T(8,128)(2,1)}), bf16[8,40,1024]{2,1,0:T(8,128)(2,1)S(1)}, u32[]{:S(2)}, u32[]{:S(2)}) async-start(bf16[8,40,1024]{2,1,0:T(8,128)(2,1)} %pad_maximum_fusion.1), calls=%async_computation.3 | async-start | bytes 1310720 | tf_op jit(solution)/shard_map/all_to_all | solution.py:562
  454.5 13.6 %table_columns_grad.3 = f32[9216,256]{1,0:T(8,128)} custom-call(s32[1]{0:T(128)} %bitcast.9.place, bf16[4608,1024]{1,0:T(8,128)(2,1)} %get-tuple-element.53.grad_pre, bf16[4608,1024]{1,0:T(8,128)(2,1)} %get-tuple-element.54.self_sums, bf16[1024,1024]{1,0:T(8,128)(2,1)} %query.5, bf16[2048,1024]{1,0:T(8,128)(2,1)} %mix_self.3), custom_call_target="tpu_custom_call" | custom-call | flops 4831838208 | bytes 18874368 | tf_op jit(solution)/shard_map/table_columns_grad/pallas_call | solution.py:386
  468.2 6.6 %convert_element_type.113 = f32[2048,1024]{1,0:T(8,128)} convert(bf16[2048,1024]{1,0:T(8,128)(2,1)} %all-gather.9.cloned.1.call-done) | non-fusion elementwise | flops 2097152 | bytes 12582912 | tf_op jit(solution)/shard_map/convert_element_type | solution.py:552
  474.9 0.7 broadcast_in_dim.44
  475.6 3.6 all-to-all-start.2
  479.2 2.0 collective-permute-start.2
  481.2 7.4 %all-to-all-done.2 = bf16[4,32,1024]{2,1,0:T(8,128)(2,1)S(1)} async-done(((bf16[4,32,1024]{2,1,0:T(8,128)(2,1)}), bf16[4,32,1024]{2,1,0:T(8,128)(2,1)S(1)}, u32[]{:S(2)}, u32[]{:S(2)}) %all-to-all-start.2) | async-done | bytes 262176 | tf_op jit(solution)/shard_map/all_to_all | solution.py:570
  488.6 1.6 broadcast_in_dim.45
  490.2 3.9 all-to-all-start.3
  494.1 0.5 broadcast_multiply_fusion.1
  494.6 0.6 reduce_sum.99
  495.2 0.6 slice.97
  495.8 16.0 %collective-permute-done.2 = bf16[4608,128]{1,0:T(8,128)(2,1)} collective-permute-done((bf16[4608,128]{1,0:T(8,128)(2,1)}, bf16[4608,128]{1,0:T(8,128)(2,1)}, u32[]{:S(2)}, u32[]{:S(2)}) %collective-permute-start.2) | collective-permute-done | bytes 1179680 | tf_op jit(solution)/shard_map/ppermute | solution.py:568
  511.9 3.8 convert_dynamic-update-slice_fusion
  515.6 5.1 all-to-all-done.3
  520.7 2.5 copy_convert_fusion
  (58 shorter events, 1.4 us)
Async XLA Ops:
  8.0 121.0 %reduce-scatter.3.cloned.1.call-start = ((), (), s32[]{:S(2)}) async-start(), calls=%async_computation.6 | async-start | bytes 3538944 | tf_op jit(solution)/shard_map/reduce_scatter | solution.py:470
  36.8 16.2 %copy-start = (f32[8,1,11392]{2,0,1:T(8,128)}, f32[8,1,11392]{2,0,1:T(8,128)S(1)}, u32[]{:S(2)}) copy-start(f32[8,1,11392]{2,0,1:T(8,128)S(1)} %copy.63) | copy-start | bytes 1093636
  55.1 1.0 copy-start.1
  55.1 74.2 %all-gather.11.cloned.1.call-start = ((), (), s32[]{:S(2)}) async-start(), calls=%async_computation.10 | async-start | bytes 1822720 | tf_op jit(solution)/shard_map/all_gather | solution.py:471
  55.7 144.4 %reduce-scatter.5.cloned.1.call-start = ((), (), s32[]{:S(2)}) async-start(), calls=%async_computation.7 | async-start | bytes 7077888 | tf_op jit(solution)/shard_map/reduce_scatter | solution.py:492
  129.0 72.3 %copy-start.3 = (bf16[192,1024]{1,0:T(8,128)(2,1)S(1)}, bf16[192,1024]{1,0:T(8,128)(2,1)}, u32[]{:S(2)}) copy-start(bf16[192,1024]{1,0:T(8,128)(2,1)} %param.17) | copy-start | bytes 1179652
  129.0 72.3 %copy-start.5 = (f32[1024]{0:T(1024)S(1)}, f32[1024]{0:T(1024)}, u32[]{:S(2)}) copy-start(f32[1024]{0:T(1024)} %param.13) | copy-start | bytes 12292
  129.0 183.4 %all-gather.7.cloned.1.call-start = ((), (), s32[]{:S(2)}) async-start(), calls=%async_computation.8 | async-start | bytes 12976128 | tf_op jit(solution)/shard_map/all_gather | solution.py:508
  206.2 230.1 %all-gather.9.cloned.1.call-start = ((), (), s32[]{:S(2)}) async-start(), calls=%async_computation.9 | async-start | bytes 4325376 | tf_op jit(solution)/shard_map/all_gather | solution.py:522
  422.5 15.3 %collective-permute-start = (bf16[272,1024]{1,0:T(8,128)(2,1)}, bf16[272,1024]{1,0:T(8,128)(2,1)S(1)}, u32[]{:S(2)}, u32[]{:S(2)}) collective-permute-start(bf16[272,1024]{1,0:T(8,128)(2,1)} %get-tuple-element.52), channel_id=1, source_target_pairs={{0,1},{1,0},{2,3},{3,2},{4,5},{5,4},{6,7},{7,6},{8,9},{9,8},{10,11... | collective-permute-start | bytes 1671176 | tf_op jit(solution)/shard_map/ppermute | solution.py:550
  423.1 14.6 %copy-start.2 = (f32[272,1024]{1,0:T(8,128)S(1)}, f32[272,1024]{1,0:T(8,128)}, u32[]{:S(2)}) copy-start(f32[272,1024]{1,0:T(8,128)} %get-tuple-element.51) | copy-start | bytes 3342340
  436.3 38.6 %collective-permute-start.1 = (bf16[4608,128]{1,0:T(8,128)(2,1)}, bf16[4608,128]{1,0:T(8,128)(2,1)S(1)}, u32[]{:S(2)}, u32[]{:S(2)}) collective-permute-start(bf16[4608,128]{1,0:T(8,128)(2,1)} %get-tuple-element.57), channel_id=1, source_target_pairs={{0,1},{1,0},{2,3},{3,2},{4,5},{5,4},{6,7},{7,6},{8,9},{9,8},{10,11... | collective-permute-start | bytes 3538952 | tf_op jit(solution)/shard_map/ppermute | solution.py:553
  438.9 29.3 %all-to-all-start.1 = ((bf16[8,40,1024]{2,1,0:T(8,128)(2,1)}), bf16[8,40,1024]{2,1,0:T(8,128)(2,1)S(1)}, u32[]{:S(2)}, u32[]{:S(2)}) async-start(bf16[8,40,1024]{2,1,0:T(8,128)(2,1)} %pad_maximum_fusion.1), calls=%async_computation.3 | async-start | bytes 1310720 | tf_op jit(solution)/shard_map/all_to_all | solution.py:562
  475.6 13.0 %all-to-all-start.2 = ((bf16[4,32,1024]{2,1,0:T(8,128)(2,1)}), bf16[4,32,1024]{2,1,0:T(8,128)(2,1)S(1)}, u32[]{:S(2)}, u32[]{:S(2)}) async-start(bf16[4,32,1024]{2,1,0:T(8,128)(2,1)} %broadcast_in_dim.44), calls=%async_computation.4 | async-start | bytes 524288 | tf_op jit(solution)/shard_map/all_to_all | solution.py:570
  479.2 15.4 %copy-start.4 = (f32[8,1024]{1,0:T(8,128)S(1)}, f32[8,1024]{1,0:T(8,128)}, u32[]{:S(2)}) copy-start(f32[8,1024]{1,0:T(8,128)} %get-tuple-element.64) | copy-start | bytes 98308
  479.2 32.7 %collective-permute-start.2 = (bf16[4608,128]{1,0:T(8,128)(2,1)}, bf16[4608,128]{1,0:T(8,128)(2,1)}, u32[]{:S(2)}, u32[]{:S(2)}) collective-permute-start(bf16[4608,128]{1,0:T(8,128)(2,1)} %get-tuple-element.61), channel_id=1, source_target_pairs={{0,1},{1,0},{2,3},{3,2},{4,5},{5,4},{6,7},{7,6},{8,9},{9,8},{10,11... | collective-permute-start | bytes 3538952 | tf_op jit(solution)/shard_map/ppermute | solution.py:568
  490.2 30.6 %all-to-all-start.3 = ((bf16[8,4,32,1024]{3,2,1,0:T(8,128)(2,1)}), bf16[8,4,32,1024]{3,2,1,0:T(8,128)(2,1)S(1)}, u32[]{:S(2)}, u32[]{:S(2)}) async-start(bf16[8,4,32,1024]{3,2,1,0:T(8,128)(2,1)} %broadcast_in_dim.45), calls=%async_computation.5 | async-start | bytes 4194304 | tf_op jit(solution)/shard_map/all_to_all | solution.py:577
Sparse Core Ops, SparseCore 0:
  55.3 46.3 reduce-scatter.2
  129.1 70.9 reduce-scatter.4
Sparse Core Ops, SparseCore 1:
  57.8 35.2 all-gather.10
  206.2 106.1 all-gather.6
  320.0 60.3 all-gather.8

commit v9 on v7

--- a/solution.py
+++ b/solution.py
@@ -4,6 +4,7 @@
 import jax.numpy as jnp
 from jax import lax
 from jax.experimental import pallas as pl
+from jax.experimental.layout import Layout, with_layout_constraint
 from jax.experimental.pallas import tpu as pltpu
 from jax.sharding import PartitionSpec as P
 
@@ -434,15 +435,12 @@
     keys, sorted_shares = lax.sort((keys.reshape(-1), shares.reshape(-1)), num_keys=1, is_stable=False)
     keys = keys[:live_most]
     sorted_shares = sorted_shares[:live_most]
-    own_keys = lax.sort(lookup_ids[:, 0] * SHIFT + target)
     edges = jnp.arange(owners * SPLIT + 1, dtype=I32) * (rows_owned // SPLIT * SHIFT)
     starts = jnp.sum((keys[None, :] < edges[:, None]).astype(I32), axis=1)
-    own_starts = jnp.sum((own_keys[None, :] < edges[:, None]).astype(I32), axis=1)
     own_length = SHIFT
     meta = jnp.concatenate(
         [
             starts.astype(F32),
-            own_starts.astype(F32),
             jnp.stack([jnp.sum(present), jnp.sum(masked_weight)]),
         ]
     )
@@ -455,7 +453,6 @@
         [
             padded(as_code(keys), length),
             padded(sorted_shares, length),
-            padded(as_code(own_keys), own_length),
             padded(meta, meta_length),
             padded(lookup_ids[:, 0].astype(F32), own_length),
         ]
@@ -475,15 +472,20 @@
         at = 2 * length
         codes = lists[:, :length].astype(I32).reshape(count, 1, length)
         parts = lists[:, length:at].reshape(count, 1, length)
-        own_codes = lists[:, at : at + own_length].astype(I32).reshape(count, 1, own_length)
-        notes = lists[:, at + own_length :]
-        first = lax.dynamic_slice(notes, (0, start), (count, stride + 1))[:, ::stride]
-        own_first = lax.dynamic_slice(notes, (0, start + owners * SPLIT + 1), (count, stride + 1))[:, ::stride]
-        bounds = jnp.concatenate([first, own_first], axis=1).astype(I32)
-        sums = jnp.sum(notes[:, 2 * (owners * SPLIT + 1) : 2 * (owners * SPLIT + 2)], axis=0)
-        return codes, parts, own_codes, bounds, sums
-
-    codes, parts, _, bounds, _ = unpack(plane, owner * SPLIT, SPLIT)
+        notes = lists[:, at : at + meta_length]
+        bounds = lax.dynamic_slice(notes, (0, start), (count, stride + 1))[:, ::stride].astype(I32)
+        sums = jnp.sum(notes[:, owners * SPLIT + 1 : owners * SPLIT + 3], axis=0)
+        return codes, parts, bounds, sums
+
+    def own_lists(lists, start):
+        ids = lists[:, -own_length:][:, :batch_rows].astype(I32)
+        keys = lax.sort(ids * SHIFT + target[None, :], dimension=1)
+        ends = (start + jnp.arange(2, dtype=I32)) * (rows_owned // SPLIT * SHIFT)
+        own_bounds = jnp.sum((keys[:, None, :] < ends[None, :, None]).astype(I32), axis=2)
+        own_codes = jnp.pad(keys % (rows_owned * SHIFT), ((0, 0), (0, own_length - batch_rows)))
+        return own_codes.reshape(-1, 1, own_length), own_bounds
+
+    codes, parts, bounds, _ = unpack(plane, owner * SPLIT, SPLIT)
     bounds, _ = lax.optimization_barrier((bounds, found))
     hidden, pooled_parts = owner_forward(
         feature_table, neighbour_query_weight, query_bias, codes, parts, bounds, batch_rows
@@ -491,7 +493,13 @@
     pooled_parts, self_rows = lax.optimization_barrier((pooled_parts, self_rows))
     pooled = lax.psum_scatter(pooled_parts, "table", scatter_dimension=0, tiled=True)
     half = lax.rem(group, SPLIT)
-    pooled, lists = lax.optimization_barrier((pooled, unpack(every, owner * SPLIT + half, 1)))
+    all_codes, all_parts, all_bounds, sums = unpack(every, owner * SPLIT + half, 1)
+    all_own_codes, own_bounds = own_lists(every, owner * SPLIT + half)
+    all_bounds = jnp.concatenate([all_bounds, own_bounds], axis=1)
+    rows_major = Layout(major_to_minor=(0, 1, 2))
+    all_codes = with_layout_constraint(all_codes, rows_major)
+    all_parts = with_layout_constraint(all_parts, rows_major)
+    pooled, lists = lax.optimization_barrier((pooled, (all_codes, all_parts, all_own_codes, all_bounds, sums)))
     all_codes, all_parts, all_own_codes, all_bounds, sums = lists
     pooled = lax.reduce_precision(pooled, 8, 7).astype(BF16)
 
@@ -562,7 +570,7 @@
     incoming = lax.all_to_all(outgoing.astype(BF16), "table", split_axis=0, concat_axis=0, tiled=True)
     summed = jnp.sum(incoming.astype(F32), axis=0)
     query_bias_grad = summed[query_rows]
-    summed, got_first = lax.optimization_barrier((summed, got_first))
+    summed, got_first, table_grad = lax.optimization_barrier((summed, got_first, table_grad))
     got_last = lax.ppermute(send_last, "rep", swap)
     table_got = jnp.concatenate([got_first, got_last], axis=1)
     column = lax.all_to_all(

time: 522 us -> 517 us (level)
  Pallas kernels: 201 us -> 184 us
  waiting for transfers between devices: 140 us -> 154 us
  blocking collectives: 62.3 us -> 48.8 us
  starting transfers between devices: 15.5 us -> 27.8 us
    all_to_all x0 -> x1, starting transfers between devices: none -> 15.9 us  [local(): lax.all_to_all(outgoing.astype(BF16), 'table', split_axis=0, concat_axis=...]
    all_to_all x1 -> x0, blocking collectives: 13.5 us -> none  [local(): lax.all_to_all(outgoing.astype(BF16), 'table', split_axis=0, concat_axis=...]
    pallas_call x1, Pallas kernels: 103 us -> 92.9 us  [owner_backward(): pl.pallas_call(functools.partial(backward_kernel, requesters, length), gr...]
    ppermute x1, waiting for transfers between devices: 0.01 us -> 9.58 us  [local(): got_last = lax.ppermute(send_last, 'rep', swap)]
    pallas_call x1, Pallas kernels: 71.3 us -> 63.9 us  [owner_forward(): pl.pallas_call(functools.partial(forward_kernel, blocks, length), grid_sp...]
    ppermute x1, waiting for transfers between devices: 5.89 us -> 0.01 us  [local(): got_first = lax.ppermute(send_first, 'rep', swap)]
  transfers between devices with their start and end apart: 10 -> 11, of which waited for: 5 -> 5; matrix products, arithmetic and copies ran while one was open for 6% -> 6% of each run, Pallas kernels for 39% -> 36%
where the time goes in v9:
time: 517 us; the launch traced here: 512 us
  Pallas kernels  184 us (36%)
  waiting for transfers between devices  154 us (30%)
  blocking collectives  48.8 us (9%)
  other arithmetic  41.8 us (8%)
  local copies, waits for them, and re-layouts  29 us (6%)
  starting transfers between devices  27.8 us (5%)
  between operations  16 us (3%)
  matrix products  10.9 us (2%)
    pallas_call x1, Pallas kernels, owner_backward(): pl.pallas_call(functools.partial(backward_kernel, requesters, length), gr...  92.9 us
    all_gather x1, waiting for transfers between devices, local(): all_mixed = lax.all_gather(grad_mixed, ('table', 'rep'), axis=0, tiled=True)  66 us
    reduce_scatter x1, waiting for transfers between devices, local(): lax.psum_scatter(pooled_parts, 'table', scatter_dimension=0, tiled=True)  65.4 us
    pallas_call x1, Pallas kernels, owner_forward(): pl.pallas_call(functools.partial(forward_kernel, blocks, length), grid_sp...  63.9 us
    all_to_all x1, blocking collectives, local(): lax.all_to_all(joined.reshape(batch_rows, devices, mix_part).transpose(1,...  37.8 us
    pallas_call x2, Pallas kernels, table_columns_grad(): pl.pallas_call(table_kernel, grid_spec=pltpu.PrefetchScalarGridSpec(num_s...  26.8 us
    all_to_all x1, starting transfers between devices, local(): lax.all_to_all(outgoing.astype(BF16), 'table', split_axis=0, concat_axis=...  15.9 us
    gather x1, local copies, waits for them, and re-layouts, local(): found = feature_table[jnp.clip(wanted, 0, rows_owned - 1)]  15.9 us
  transfers between devices with their start and end apart: 11, of which 5 were waited for; matrix products, arithmetic and copies ran while one was open for 6% of the time, Pallas kernels for 36%

profile of v9, /device:TPU:0, one launch (start us, length us, event | category | flops | bytes accessed | tf_op | source)
XLA Modules:
  0.0 511.8 jit_solution(15797379876669178480)
XLA Ops:
  8.1 0.7 slice_convert_fusion.7
  8.8 0.8 add_select_fusion
  9.6 1.5 fusion.8
  11.1 0.8 divide_reduce-precision_fusion
  11.9 0.1 copy.58
  12.0 0.1 reshape.131
  12.1 0.1 copy.57
  12.2 0.1 reshape.130
  12.4 7.5 %sort.29 = (s32[9600]{0:T(1024)S(1)}, f32[9600]{0:T(1024)S(1)}) sort(s32[9600]{0:T(1024)S(1)} %reshape.130, f32[9600]{0:T(1024)S(1)} %reshape.131), dimensions={0}, to_apply=%region_1.2 | sort | flops 134400 | bytes 153600 | tf_op jit(solution)/shard_map/sort | solution.py:435
  19.9 0.2 convert_reduce_fusion.1
  20.2 0.7 slice_select_fusion
  20.9 1.4 select_maximum_fusion.2
  22.3 11.0 %all-gather.2 = f32[8,1,11136]{2,1,0:T(1,128)S(1)} all-gather(f32[1,1,11136]{2,1,0:T(1,128)S(1)} %reshape.154), channel_id=2, replica_groups=mesh['table'=8,'rep'=4] {'table'}, dimensions={0}, use_global_device_ids=true | all-gather | bytes 400896 | tf_op jit(solution)/shard_map/all_gather | solution.py:460
  33.7 15.9 %gather_fusion = bf16[1536,1024]{1,0:T(8,128)(2,1)S(1)} fusion(bf16[9216,1024]{1,0:T(8,128)(2,1)} %table_other.1, s32[2048]{0:T(1024)S(1)} %pad_clamp_fusion), kind=kCustom, calls=%fused_computation | custom fusion | bytes 6297600 | tf_op jit(solution)/shard_map/gather | solution.py:465
  49.6 2.1 broadcast_select_fusion
  51.8 0.5 all-gather.11.cloned.1.call-update
  52.3 0.3 copy-done.1
  52.8 0.6 convert_element_type.90.bounds
  53.4 0.9 copy.60.shares
  54.3 0.8 copy.59.codes
  55.1 63.9 %owner_forward.1 = (bf16[9216,1024]{1,0:T(8,128)(2,1)}, f32[1536,1024]{1,0:T(8,128)}) custom-call(s32[8,2]{1,0:T(8,128)} %convert_element_type.90.bounds, bf16[9216,1024]{1,0:T(8,128)(2,1)} %table_other.1, bf16[1024,1024]{1,0:T(8,128)(2,1)} %query.5, f32[1,1024]{1,0:T(1,128)} %bitcast.38, s32[8,1,5376]{2,1,0:T(1,128)} %copy.59.codes, f32[8,1,5376]{2,1,0:T(1,128)} %copy.60.shares), custom_call_target="tpu_custom_call" | custom-call | flops 19327352832 | bytes 37748736 | tf_op jit(solution)/shard_map/owner_forward/pallas_call | solution.py:128
  119.1 0.2 all-gather.7.cloned.1.call-start
  119.3 0.7 slice.89
  120.2 1.5 fusion.16
  121.7 1.3 reshape.137.shares
  123.0 0.8 fusion.11
  123.8 3.7 sort.30
  127.6 0.6 reshape.138.self_codes
  128.2 1.6 copy.61.codes
  129.8 0.2 convert_reduce_fusion.3
  130.0 0.8 slice_reduce_fusion
  130.8 65.4 %reduce-scatter.5.cloned.1.call-done = f32[192,1024]{1,0:T(8,128)} async-done(((f32[1536,1024]{1,0:T(8,128)}), f32[192,1024]{1,0:T(8,128)}) %reduce-scatter.5.cloned.1.call-update) | async-done | bytes 786448 | tf_op jit(solution)/shard_map/reduce_scatter | solution.py:494
  196.1 1.2 reduce-precision_convert_fusion
  197.3 3.4 fusion.3
  200.7 1.3 fusion.2
  202.1 0.5 copy.63
  202.6 37.8 %all_to_all.20 = bf16[32,192,64]{1,2,0:T(8,128)(2,1)S(1)} all-to-all(bf16[32,192,64]{1,2,0:T(8,128)(2,1)S(1)} %bitcast.29), channel_id=1, replica_groups=mesh['table'=8,'rep'=4] {'table','rep'}, dimensions={0} | all-to-all | bytes 1572864 | tf_op jit(solution)/shard_map/all_to_all | solution.py:518
  240.4 0.6 copy.64
  241.0 1.1 reshape.140
  242.1 66.0 %all-gather.7.cloned.1.call-done.grads = bf16[6144,1024]{1,0:T(8,128)(2,1)} async-done(((bf16[192,1024]{1,0:T(8,128)(2,1)}), bf16[6144,1024]{1,0:T(8,128)(2,1)}) %all-gather.7.cloned.1.call-update) | async-done | bytes 12582928 | tf_op jit(solution)/shard_map/all_gather | solution.py:516
  308.1 7.5 %convolution_convert_fusion = bf16[64,1024]{1,0:T(8,128)(2,1)} fusion(bf16[6144,64]{0,1:T(8,128)(2,1)S(1)} %reshape.140, bf16[6144,1024]{1,0:T(8,128)(2,1)} %all-gather.7.cloned.1.call-done.grads), kind=kOutput, calls=%fused_computation.6 | convolution fusion | flops 805371904 | bytes 13500416 | tf_op jit(solution)/shard_map/dot_general | solution.py:526
  315.6 0.6 pad_add_fusion.1.place
  316.2 0.7 copy.65.bounds
  316.9 92.9 %owner_backward.1 = (bf16[4608,1024]{1,0:T(8,128)(2,1)}, bf16[4608,1024]{1,0:T(8,128)(2,1)}, f32[272,1024]{1,0:T(8,128)}, bf16[272,1024]{1,0:T(8,128)(2,1)}, f32[8,1024]{1,0:T(8,128)}) custom-call(s32[2]{0:T(128)} %pad_add_fusion.1.place, s32[32,4]{1,0:T(8,128)} %copy.65.bounds, s32[32,1,5376]{2,1,0:T(1,128)} %copy.61.codes, ...), custom_call_target="tpu_custom_call" | custom-call | flops 38654705664 | bytes 25165824 | tf_op jit(solution)/shard_map/owner_backward/pallas_call | solution.py:303
  409.8 2.3 collective-permute-start
  412.1 13.1 %table_columns_grad.2 = (bf16[4608,128]{1,0:T(8,128)(2,1)}, bf16[4608,128]{1,0:T(8,128)(2,1)}) custom-call(s32[1]{0:T(128)} %bitcast.8.place, bf16[4608,1024]{1,0:T(8,128)(2,1)} %get-tuple-element.52.grad_pre, bf16[4608,1024]{1,0:T(8,128)(2,1)} %get-tuple-element.53.self_sums, bf16[1024,1024]{1,0:T(8,128)(2,1)} %query.5, bf16[2048,1024]{1,0:T(8,128)(2,1)} %mix_self.3), custom_call_target="tpu_custom_call" | custom-call | flops 4831838208 | bytes 18874368 | tf_op jit(solution)/shard_map/table_columns_grad/pallas_call | solution.py:387
  425.3 0.2 convert_add_fusion
  425.6 0.9 pad_maximum_fusion.1
  426.5 15.9 %all-to-all-start.1 = ((bf16[8,40,1024]{2,1,0:T(8,128)(2,1)}), bf16[8,40,1024]{2,1,0:T(8,128)(2,1)S(1)}, u32[]{:S(2)}, u32[]{:S(2)}) async-start(bf16[8,40,1024]{2,1,0:T(8,128)(2,1)} %pad_maximum_fusion.1), calls=%async_computation.3 | async-start | bytes 1310720 | tf_op jit(solution)/shard_map/all_to_all | solution.py:570
  442.4 13.6 %table_columns_grad.3 = f32[9216,256]{1,0:T(8,128)} custom-call(s32[1]{0:T(128)} %bitcast.7.place, bf16[4608,1024]{1,0:T(8,128)(2,1)} %get-tuple-element.52.grad_pre, bf16[4608,1024]{1,0:T(8,128)(2,1)} %get-tuple-element.53.self_sums, bf16[1024,1024]{1,0:T(8,128)(2,1)} %query.5, bf16[2048,1024]{1,0:T(8,128)(2,1)} %mix_self.3), custom_call_target="tpu_custom_call" | custom-call | flops 4831838208 | bytes 18874368 | tf_op jit(solution)/shard_map/table_columns_grad/pallas_call | solution.py:387
  456.1 0.7 broadcast_in_dim.28
  456.9 3.5 all-to-all-start.2
  460.3 2.0 collective-permute-start.2
  462.4 7.6 %all-to-all-done.2 = bf16[4,32,1024]{2,1,0:T(8,128)(2,1)S(1)} async-done(((bf16[4,32,1024]{2,1,0:T(8,128)(2,1)}), bf16[4,32,1024]{2,1,0:T(8,128)(2,1)S(1)}, u32[]{:S(2)}, u32[]{:S(2)}) %all-to-all-start.2) | async-done | bytes 262176 | tf_op jit(solution)/shard_map/all_to_all | solution.py:576
  470.0 1.6 broadcast_in_dim.46
  471.6 3.6 all-to-all-start.3
  475.2 0.5 broadcast_multiply_fusion.1
  475.7 0.6 reduce_sum.99
  476.3 0.6 slice.94
  476.9 6.6 %convert_element_type.108 = f32[2048,1024]{1,0:T(8,128)} convert(bf16[2048,1024]{1,0:T(8,128)(2,1)} %all-gather.9.cloned.1.call-done) | non-fusion elementwise | flops 2097152 | bytes 12582912 | tf_op jit(solution)/shard_map/convert_element_type | solution.py:560
  483.6 9.6 %collective-permute-done.2 = bf16[4608,128]{1,0:T(8,128)(2,1)} collective-permute-done((bf16[4608,128]{1,0:T(8,128)(2,1)}, bf16[4608,128]{1,0:T(8,128)(2,1)}, u32[]{:S(2)}, u32[]{:S(2)}) %collective-permute-start.2) | collective-permute-done | bytes 1179680 | tf_op jit(solution)/shard_map/ppermute | solution.py:574
  493.2 3.8 convert_dynamic-update-slice_fusion
  496.9 4.8 all-to-all-done.3
  501.8 2.5 copy_convert_fusion
  (58 shorter events, 1.3 us)
Async XLA Ops:
  8.0 111.0 %reduce-scatter.3.cloned.1.call-start = ((), (), s32[]{:S(2)}) async-start(), calls=%async_computation.6 | async-start | bytes 3538944 | tf_op jit(solution)/shard_map/reduce_scatter | solution.py:467
  33.4 16.2 %copy-start = (f32[8,1,11136]{2,0,1:T(8,128)}, f32[8,1,11136]{2,0,1:T(8,128)S(1)}, u32[]{:S(2)}) copy-start(f32[8,1,11136]{2,0,1:T(8,128)S(1)} %copy.70) | copy-start | bytes 1069060
  51.7 1.0 copy-start.1
  51.7 67.6 %all-gather.11.cloned.1.call-start = ((), (), s32[]{:S(2)}) async-start(), calls=%async_computation.10 | async-start | bytes 1781760 | tf_op jit(solution)/shard_map/all_gather | solution.py:468
  52.3 143.8 %reduce-scatter.5.cloned.1.call-start = ((), (), s32[]{:S(2)}) async-start(), calls=%async_computation.7 | async-start | bytes 7077888 | tf_op jit(solution)/shard_map/reduce_scatter | solution.py:494
  119.1 189.0 %all-gather.7.cloned.1.call-start = ((), (), s32[]{:S(2)}) async-start(), calls=%async_computation.8 | async-start | bytes 12976128 | tf_op jit(solution)/shard_map/all_gather | solution.py:516
  120.2 77.1 %copy-start.3 = (bf16[192,1024]{1,0:T(8,128)(2,1)S(1)}, bf16[192,1024]{1,0:T(8,128)(2,1)}, u32[]{:S(2)}) copy-start(bf16[192,1024]{1,0:T(8,128)(2,1)} %param.17) | copy-start | bytes 1179652
  120.2 77.1 %copy-start.4 = (bf16[192,1024]{1,0:T(8,128)(2,1)S(1)}, bf16[192,1024]{1,0:T(8,128)(2,1)}, u32[]{:S(2)}) copy-start(bf16[192,1024]{1,0:T(8,128)(2,1)} %reduce-scatter.3.cloned.1.call-done) | copy-start | bytes 1179652
  120.2 77.1 %copy-start.6 = (f32[1024]{0:T(1024)S(1)}, f32[1024]{0:T(1024)}, u32[]{:S(2)}) copy-start(f32[1024]{0:T(1024)} %param.13) | copy-start | bytes 12292
  202.0 223.2 %all-gather.9.cloned.1.call-start = ((), (), s32[]{:S(2)}) async-start(), calls=%async_computation.9 | async-start | bytes 4325376 | tf_op jit(solution)/shard_map/all_gather | solution.py:530
  409.8 15.5 %collective-permute-start = (bf16[272,1024]{1,0:T(8,128)(2,1)}, bf16[272,1024]{1,0:T(8,128)(2,1)S(1)}, u32[]{:S(2)}, u32[]{:S(2)}) collective-permute-start(bf16[272,1024]{1,0:T(8,128)(2,1)} %get-tuple-element.51), channel_id=1, source_target_pairs={{0,1},{1,0},{2,3},{3,2},{4,5},{5,4},{6,7},{7,6},{8,9},{9,8},{10,11... | collective-permute-start | bytes 1671176 | tf_op jit(solution)/shard_map/ppermute | solution.py:558
  412.1 13.2 %copy-start.2 = (f32[272,1024]{1,0:T(8,128)S(1)}, f32[272,1024]{1,0:T(8,128)}, u32[]{:S(2)}) copy-start(f32[272,1024]{1,0:T(8,128)} %get-tuple-element.50) | copy-start | bytes 3342340
  425.2 30.9 %collective-permute-start.1 = (bf16[4608,128]{1,0:T(8,128)(2,1)}, bf16[4608,128]{1,0:T(8,128)(2,1)S(1)}, u32[]{:S(2)}, u32[]{:S(2)}) collective-permute-start(bf16[4608,128]{1,0:T(8,128)(2,1)} %get-tuple-element.56), channel_id=1, source_target_pairs={{0,1},{1,0},{2,3},{3,2},{4,5},{5,4},{6,7},{7,6},{8,9},{9,8},{10,11... | collective-permute-start | bytes 3538952 | tf_op jit(solution)/shard_map/ppermute | solution.py:561
  426.5 29.5 %all-to-all-start.1 = ((bf16[8,40,1024]{2,1,0:T(8,128)(2,1)}), bf16[8,40,1024]{2,1,0:T(8,128)(2,1)S(1)}, u32[]{:S(2)}, u32[]{:S(2)}) async-start(bf16[8,40,1024]{2,1,0:T(8,128)(2,1)} %pad_maximum_fusion.1), calls=%async_computation.3 | async-start | bytes 1310720 | tf_op jit(solution)/shard_map/all_to_all | solution.py:570
  456.9 13.1 %all-to-all-start.2 = ((bf16[4,32,1024]{2,1,0:T(8,128)(2,1)}), bf16[4,32,1024]{2,1,0:T(8,128)(2,1)S(1)}, u32[]{:S(2)}, u32[]{:S(2)}) async-start(bf16[4,32,1024]{2,1,0:T(8,128)(2,1)} %broadcast_in_dim.28), calls=%async_computation.4 | async-start | bytes 524288 | tf_op jit(solution)/shard_map/all_to_all | solution.py:576
  460.3 15.4 %copy-start.5 = (f32[8,1024]{1,0:T(8,128)S(1)}, f32[8,1024]{1,0:T(8,128)}, u32[]{:S(2)}) copy-start(f32[8,1024]{1,0:T(8,128)} %get-tuple-element.62) | copy-start | bytes 98308
  460.3 32.8 %collective-permute-start.2 = (bf16[4608,128]{1,0:T(8,128)(2,1)}, bf16[4608,128]{1,0:T(8,128)(2,1)}, u32[]{:S(2)}, u32[]{:S(2)}) collective-permute-start(bf16[4608,128]{1,0:T(8,128)(2,1)} %get-tuple-element.59), channel_id=1, source_target_pairs={{0,1},{1,0},{2,3},{3,2},{4,5},{5,4},{6,7},{7,6},{8,9},{9,8},{10,11... | collective-permute-start | bytes 3538952 | tf_op jit(solution)/shard_map/ppermute | solution.py:574
  471.6 30.2 %all-to-all-start.3 = ((bf16[8,4,32,1024]{3,2,1,0:T(8,128)(2,1)}), bf16[8,4,32,1024]{3,2,1,0:T(8,128)(2,1)S(1)}, u32[]{:S(2)}, u32[]{:S(2)}) async-start(bf16[8,4,32,1024]{3,2,1,0:T(8,128)(2,1)} %broadcast_in_dim.46), calls=%async_computation.5 | async-start | bytes 4194304 | tf_op jit(solution)/shard_map/all_to_all | solution.py:583
Sparse Core Ops, SparseCore 0:
  51.8 46.4 reduce-scatter.2
  119.2 76.8 reduce-scatter.4
Sparse Core Ops, SparseCore 1:
  54.3 34.6 all-gather.10
  202.1 105.9 all-gather.6
  315.7 60.3 all-gather.8

commit v10 on v9

--- a/solution.py
+++ b/solution.py
@@ -570,9 +570,6 @@
     incoming = lax.all_to_all(outgoing.astype(BF16), "table", split_axis=0, concat_axis=0, tiled=True)
     summed = jnp.sum(incoming.astype(F32), axis=0)
     query_bias_grad = summed[query_rows]
-    summed, got_first, table_grad = lax.optimization_barrier((summed, got_first, table_grad))
-    got_last = lax.ppermute(send_last, "rep", swap)
-    table_got = jnp.concatenate([got_first, got_last], axis=1)
     column = lax.all_to_all(
         jnp.broadcast_to(summed[:query_rows].astype(BF16), (groups, query_rows, width)),
         "rep",
@@ -580,6 +577,9 @@
         concat_axis=0,
         tiled=True,
     )
+    column, got_first = lax.optimization_barrier((column, got_first))
+    got_last = lax.ppermute(send_last, "rep", swap)
+    table_got = jnp.concatenate([got_first, got_last], axis=1)
     gathered = lax.all_to_all(
         jnp.broadcast_to(column, (owners, groups, query_rows, width)), "table", split_axis=0, concat_axis=0, tiled=True
     )

time: 517 us -> 506 us (0.979); the launches traced: 512 us -> 506 us
  blocking collectives: 48.8 us -> 74.9 us
  waiting for transfers between devices: 154 us -> 135 us
  starting transfers between devices: 27.8 us -> 14.7 us
    all_to_all x0 -> x1, blocking collectives: none -> 26.1 us  [local(): lax.all_to_all(outgoing.astype(BF16), 'table', split_axis=0, concat_axis=...]
    all_to_all x1 -> x0, starting transfers between devices: 15.9 us -> none  [local(): lax.all_to_all(outgoing.astype(BF16), 'table', split_axis=0, concat_axis=...]
    ppermute x1, waiting for transfers between devices: 9.58 us -> 0.01 us  [local(): got_last = lax.ppermute(send_last, 'rep', swap)]
  transfers between devices with their start and end apart: 11 -> 10, of which waited for: 5 -> 4; matrix products, arithmetic and copies ran while one was open for 6% -> 6% of each run, Pallas kernels for 36% -> 37%
where the time goes in v10:
time: 506 us
  Pallas kernels  185 us (37%)
  waiting for transfers between devices  135 us (27%)
  blocking collectives  74.9 us (15%)
  other arithmetic  41 us (8%)
  local copies, waits for them, and re-layouts  29 us (6%)
  between operations  16 us (3%)
  starting transfers between devices  14.7 us (3%)
  matrix products  10.9 us (2%)
    pallas_call x1, Pallas kernels, owner_backward(): pl.pallas_call(functools.partial(backward_kernel, requesters, length), gr...  94.1 us
    all_gather x1, waiting for transfers between devices, local(): all_mixed = lax.all_gather(grad_mixed, ('table', 'rep'), axis=0, tiled=True)  66 us
    pallas_call x1, Pallas kernels, owner_forward(): pl.pallas_call(functools.partial(forward_kernel, blocks, length), grid_sp...  64.4 us
    reduce_scatter x1, waiting for transfers between devices, local(): lax.psum_scatter(pooled_parts, 'table', scatter_dimension=0, tiled=True)  61.3 us
    all_to_all x1, blocking collectives, local(): lax.all_to_all(joined.reshape(batch_rows, devices, mix_part).transpose(1,...  37.8 us
    pallas_call x2, Pallas kernels, table_columns_grad(): pl.pallas_call(table_kernel, grid_spec=pltpu.PrefetchScalarGridSpec(num_s...  26.7 us
    all_to_all x1, blocking collectives, local(): lax.all_to_all(outgoing.astype(BF16), 'table', split_axis=0, concat_axis=...  26.1 us
    gather x1, local copies, waits for them, and re-layouts, local(): found = feature_table[jnp.clip(wanted, 0, rows_owned - 1)]  15.9 us
  transfers between devices with their start and end apart: 10, of which 4 were waited for; matrix products, arithmetic and copies ran while one was open for 6% of the time, Pallas kernels for 37%

profile of v10, /device:TPU:0, one launch (start us, length us, event | category | flops | bytes accessed | tf_op | source)
XLA Modules:
  0.0 506.4 jit_solution(2474878021584869900)
XLA Ops:
  8.1 0.7 slice_convert_fusion.7
  8.8 0.8 add_select_fusion
  9.6 1.5 fusion.8
  11.1 0.8 divide_reduce-precision_fusion
  11.9 0.1 copy.58
  12.0 0.1 reshape.133
  12.1 0.1 copy.57
  12.2 0.1 reshape.132
  12.4 7.5 %sort.29 = (s32[9600]{0:T(1024)S(1)}, f32[9600]{0:T(1024)S(1)}) sort(s32[9600]{0:T(1024)S(1)} %reshape.132, f32[9600]{0:T(1024)S(1)} %reshape.133), dimensions={0}, to_apply=%region_1.2 | sort | flops 134400 | bytes 153600 | tf_op jit(solution)/shard_map/sort | solution.py:435
  19.9 0.2 convert_reduce_fusion.1
  20.2 0.7 slice_select_fusion
  20.9 1.4 select_maximum_fusion.2
  22.3 11.0 %all-gather.2 = f32[8,1,11136]{2,1,0:T(1,128)S(1)} all-gather(f32[1,1,11136]{2,1,0:T(1,128)S(1)} %reshape.157), channel_id=2, replica_groups=mesh['table'=8,'rep'=4] {'table'}, dimensions={0}, use_global_device_ids=true | all-gather | bytes 400896 | tf_op jit(solution)/shard_map/all_gather | solution.py:460
  33.7 15.9 %gather_fusion = bf16[1536,1024]{1,0:T(8,128)(2,1)S(1)} fusion(bf16[9216,1024]{1,0:T(8,128)(2,1)} %table_other.1, s32[2048]{0:T(1024)S(1)} %pad_clamp_fusion), kind=kCustom, calls=%fused_computation | custom fusion | bytes 6297600 | tf_op jit(solution)/shard_map/gather | solution.py:465
  49.6 2.1 broadcast_select_fusion
  51.8 0.5 all-gather.11.cloned.1.call-update
  52.3 0.3 copy-done.1
  52.8 0.6 convert_element_type.90.bounds
  53.4 0.9 copy.60.shares
  54.3 0.8 copy.59.codes
  55.1 64.4 %owner_forward.1 = (bf16[9216,1024]{1,0:T(8,128)(2,1)}, f32[1536,1024]{1,0:T(8,128)}) custom-call(s32[8,2]{1,0:T(8,128)} %convert_element_type.90.bounds, bf16[9216,1024]{1,0:T(8,128)(2,1)} %table_other.1, bf16[1024,1024]{1,0:T(8,128)(2,1)} %query.5, f32[1,1024]{1,0:T(1,128)} %bitcast.38, s32[8,1,5376]{2,1,0:T(1,128)} %copy.59.codes, f32[8,1,5376]{2,1,0:T(1,128)} %copy.60.shares), custom_call_target="tpu_custom_call" | custom-call | flops 19327352832 | bytes 37748736 | tf_op jit(solution)/shard_map/owner_forward/pallas_call | solution.py:128
  119.6 0.2 all-gather.7.cloned.1.call-start
  119.9 0.7 slice.89
  120.8 1.5 fusion.16
  122.3 1.3 reshape.139.shares
  123.6 0.8 fusion.11
  124.3 3.7 sort.30
  128.1 0.6 reshape.140.self_codes
  128.7 1.6 copy.61.codes
  130.3 0.2 convert_reduce_fusion.3
  130.5 0.8 slice_reduce_fusion
  131.3 61.3 %reduce-scatter.5.cloned.1.call-done = f32[192,1024]{1,0:T(8,128)} async-done(((f32[1536,1024]{1,0:T(8,128)}), f32[192,1024]{1,0:T(8,128)}) %reduce-scatter.5.cloned.1.call-update) | async-done | bytes 786448 | tf_op jit(solution)/shard_map/reduce_scatter | solution.py:494
  192.6 1.2 reduce-precision_convert_fusion
  193.8 3.4 fusion.3
  197.2 1.3 fusion.2
  198.6 0.5 copy.63
  199.1 37.8 %all_to_all.20 = bf16[32,192,64]{1,2,0:T(8,128)(2,1)S(1)} all-to-all(bf16[32,192,64]{1,2,0:T(8,128)(2,1)S(1)} %bitcast.29), channel_id=1, replica_groups=mesh['table'=8,'rep'=4] {'table','rep'}, dimensions={0} | all-to-all | bytes 1572864 | tf_op jit(solution)/shard_map/all_to_all | solution.py:518
  236.9 0.6 copy.64
  237.5 1.1 reshape.143
  238.6 66.0 %all-gather.7.cloned.1.call-done.grads = bf16[6144,1024]{1,0:T(8,128)(2,1)} async-done(((bf16[192,1024]{1,0:T(8,128)(2,1)}), bf16[6144,1024]{1,0:T(8,128)(2,1)}) %all-gather.7.cloned.1.call-update) | async-done | bytes 12582928 | tf_op jit(solution)/shard_map/all_gather | solution.py:516
  304.6 7.5 %convolution_convert_fusion = bf16[64,1024]{1,0:T(8,128)(2,1)} fusion(bf16[6144,64]{0,1:T(8,128)(2,1)S(1)} %reshape.143, bf16[6144,1024]{1,0:T(8,128)(2,1)} %all-gather.7.cloned.1.call-done.grads), kind=kOutput, calls=%fused_computation.6 | convolution fusion | flops 805371904 | bytes 13500416 | tf_op jit(solution)/shard_map/dot_general | solution.py:526
  312.1 0.6 pad_add_fusion.1.place
  312.7 0.7 copy.65.bounds
  313.4 94.1 %owner_backward.1 = (bf16[4608,1024]{1,0:T(8,128)(2,1)}, bf16[4608,1024]{1,0:T(8,128)(2,1)}, f32[272,1024]{1,0:T(8,128)}, bf16[272,1024]{1,0:T(8,128)(2,1)}, f32[8,1024]{1,0:T(8,128)}) custom-call(s32[2]{0:T(128)} %pad_add_fusion.1.place, s32[32,4]{1,0:T(8,128)} %copy.65.bounds, s32[32,1,5376]{2,1,0:T(1,128)} %copy.61.codes, ...), custom_call_target="tpu_custom_call" | custom-call | flops 38654705664 | bytes 25165824 | tf_op jit(solution)/shard_map/owner_backward/pallas_call | solution.py:303
  407.5 1.6 collective-permute-start
  409.1 13.1 %table_columns_grad.3 = (bf16[4608,128]{1,0:T(8,128)(2,1)}, bf16[4608,128]{1,0:T(8,128)(2,1)}) custom-call(s32[1]{0:T(128)} %bitcast.8.place, bf16[4608,1024]{1,0:T(8,128)(2,1)} %get-tuple-element.49.grad_pre, bf16[4608,1024]{1,0:T(8,128)(2,1)} %get-tuple-element.50.self_sums, bf16[1024,1024]{1,0:T(8,128)(2,1)} %query.5, bf16[2048,1024]{1,0:T(8,128)(2,1)} %mix_self.3), custom_call_target="tpu_custom_call" | custom-call | flops 4831838208 | bytes 18874368 | tf_op jit(solution)/shard_map/table_columns_grad/pallas_call | solution.py:387
  422.3 0.2 convert_add_fusion
  422.5 0.5 collective-permute-start.1
  423.1 26.1 %all_to_all.21 = bf16[8,40,1024]{2,1,0:T(8,128)(2,1)S(1)} all-to-all(bf16[8,40,1024]{2,1,0:T(8,128)(2,1)S(1)} %pad_maximum_fusion.1), channel_id=1, replica_groups=mesh['table'=8,'rep'=4] {'table'}, dimensions={0} | all-to-all | bytes 1310720 | tf_op jit(solution)/shard_map/all_to_all | solution.py:570
  449.2 0.1 convert_reduce_fusion
  449.3 0.7 broadcast_in_dim.28
  450.1 3.7 all-to-all-start.2
  453.7 2.0 collective-permute-start.2
  455.8 5.9 %all-to-all-done.2 = bf16[4,32,1024]{2,1,0:T(8,128)(2,1)S(1)} async-done(((bf16[4,32,1024]{2,1,0:T(8,128)(2,1)}), bf16[4,32,1024]{2,1,0:T(8,128)(2,1)S(1)}, u32[]{:S(2)}, u32[]{:S(2)}) %all-to-all-start.2) | async-done | bytes 262176 | tf_op jit(solution)/shard_map/all_to_all | solution.py:573
  461.7 1.6 broadcast_in_dim.46
  463.3 6.4 %all-to-all-start.3 = ((bf16[8,4,32,1024]{3,2,1,0:T(8,128)(2,1)}), bf16[8,4,32,1024]{3,2,1,0:T(8,128)(2,1)S(1)}, u32[]{:S(2)}, u32[]{:S(2)}) async-start(bf16[8,4,32,1024]{3,2,1,0:T(8,128)(2,1)} %broadcast_in_dim.46), calls=%async_computation.5 | async-start | bytes 4194304 | tf_op jit(solution)/shard_map/all_to_all | solution.py:583
  469.7 0.5 broadcast_multiply_fusion.1
  470.2 0.6 reduce_sum.99
  470.8 13.6 %table_columns_grad.2 = f32[9216,256]{1,0:T(8,128)} custom-call(s32[1]{0:T(128)} %bitcast.7.place, bf16[4608,1024]{1,0:T(8,128)(2,1)} %get-tuple-element.49.grad_pre, bf16[4608,1024]{1,0:T(8,128)(2,1)} %get-tuple-element.50.self_sums, bf16[1024,1024]{1,0:T(8,128)(2,1)} %query.5, bf16[2048,1024]{1,0:T(8,128)(2,1)} %mix_self.3), custom_call_target="tpu_custom_call" | custom-call | flops 4831838208 | bytes 18874368 | tf_op jit(solution)/shard_map/table_columns_grad/pallas_call | solution.py:387
  484.4 0.6 slice.94
  485.0 6.6 %convert_element_type.108 = f32[2048,1024]{1,0:T(8,128)} convert(bf16[2048,1024]{1,0:T(8,128)(2,1)} %all-gather.9.cloned.1.call-done) | non-fusion elementwise | flops 2097152 | bytes 12582912 | tf_op jit(solution)/shard_map/convert_element_type | solution.py:560
  491.6 3.8 convert_dynamic-update-slice_fusion
  495.4 0.9 all-to-all-done.3
  496.3 2.5 copy_convert_fusion
  (57 shorter events, 1.2 us)
Async XLA Ops:
  8.0 111.6 %reduce-scatter.3.cloned.1.call-start = ((), (), s32[]{:S(2)}) async-start(), calls=%async_computation.6 | async-start | bytes 3538944 | tf_op jit(solution)/shard_map/reduce_scatter | solution.py:467
  33.4 16.2 %copy-start = (f32[8,1,11136]{2,0,1:T(8,128)}, f32[8,1,11136]{2,0,1:T(8,128)S(1)}, u32[]{:S(2)}) copy-start(f32[8,1,11136]{2,0,1:T(8,128)S(1)} %copy.70) | copy-start | bytes 1069060
  51.7 1.0 copy-start.1
  51.7 68.2 %all-gather.11.cloned.1.call-start = ((), (), s32[]{:S(2)}) async-start(), calls=%async_computation.10 | async-start | bytes 1781760 | tf_op jit(solution)/shard_map/all_gather | solution.py:468
  52.3 140.3 %reduce-scatter.5.cloned.1.call-start = ((), (), s32[]{:S(2)}) async-start(), calls=%async_computation.7 | async-start | bytes 7077888 | tf_op jit(solution)/shard_map/reduce_scatter | solution.py:494
  119.6 185.0 %all-gather.7.cloned.1.call-start = ((), (), s32[]{:S(2)}) async-start(), calls=%async_computation.8 | async-start | bytes 12976128 | tf_op jit(solution)/shard_map/all_gather | solution.py:516
  120.8 73.0 %copy-start.3 = (bf16[192,1024]{1,0:T(8,128)(2,1)S(1)}, bf16[192,1024]{1,0:T(8,128)(2,1)}, u32[]{:S(2)}) copy-start(bf16[192,1024]{1,0:T(8,128)(2,1)} %param.17) | copy-start | bytes 1179652
  120.8 73.0 %copy-start.4 = (bf16[192,1024]{1,0:T(8,128)(2,1)S(1)}, bf16[192,1024]{1,0:T(8,128)(2,1)}, u32[]{:S(2)}) copy-start(bf16[192,1024]{1,0:T(8,128)(2,1)} %reduce-scatter.3.cloned.1.call-done) | copy-start | bytes 1179652
  120.8 73.0 %copy-start.6 = (f32[1024]{0:T(1024)S(1)}, f32[1024]{0:T(1024)}, u32[]{:S(2)}) copy-start(f32[1024]{0:T(1024)} %param.13) | copy-start | bytes 12292
  198.5 224.0 %all-gather.9.cloned.1.call-start = ((), (), s32[]{:S(2)}) async-start(), calls=%async_computation.9 | async-start | bytes 4325376 | tf_op jit(solution)/shard_map/all_gather | solution.py:530
  407.5 14.8 %collective-permute-start = (bf16[272,1024]{1,0:T(8,128)(2,1)}, bf16[272,1024]{1,0:T(8,128)(2,1)S(1)}, u32[]{:S(2)}, u32[]{:S(2)}) collective-permute-start(bf16[272,1024]{1,0:T(8,128)(2,1)} %get-tuple-element.52), channel_id=1, source_target_pairs={{0,1},{1,0},{2,3},{3,2},{4,5},{5,4},{6,7},{7,6},{8,9},{9,8},{10,11... | collective-permute-start | bytes 1671176 | tf_op jit(solution)/shard_map/ppermute | solution.py:558
  409.1 13.2 %copy-start.2 = (f32[272,1024]{1,0:T(8,128)S(1)}, f32[272,1024]{1,0:T(8,128)}, u32[]{:S(2)}) copy-start(f32[272,1024]{1,0:T(8,128)} %get-tuple-element.51) | copy-start | bytes 3342340
  422.5 39.2 %collective-permute-start.1 = (bf16[4608,128]{1,0:T(8,128)(2,1)}, bf16[4608,128]{1,0:T(8,128)(2,1)S(1)}, u32[]{:S(2)}, u32[]{:S(2)}) collective-permute-start(bf16[4608,128]{1,0:T(8,128)(2,1)} %get-tuple-element.55), channel_id=1, source_target_pairs={{0,1},{1,0},{2,3},{3,2},{4,5},{5,4},{6,7},{7,6},{8,9},{9,8},{10,11... | collective-permute-start | bytes 3538952 | tf_op jit(solution)/shard_map/ppermute | solution.py:561
  450.1 11.6 %all-to-all-start.2 = ((bf16[4,32,1024]{2,1,0:T(8,128)(2,1)}), bf16[4,32,1024]{2,1,0:T(8,128)(2,1)S(1)}, u32[]{:S(2)}, u32[]{:S(2)}) async-start(bf16[4,32,1024]{2,1,0:T(8,128)(2,1)} %broadcast_in_dim.28), calls=%async_computation.4 | async-start | bytes 524288 | tf_op jit(solution)/shard_map/all_to_all | solution.py:573
  453.7 16.5 %copy-start.5 = (f32[8,1024]{1,0:T(8,128)S(1)}, f32[8,1024]{1,0:T(8,128)}, u32[]{:S(2)}) copy-start(f32[8,1024]{1,0:T(8,128)} %get-tuple-element.60) | copy-start | bytes 98308
  453.7 37.9 %collective-permute-start.2 = (bf16[4608,128]{1,0:T(8,128)(2,1)}, bf16[4608,128]{1,0:T(8,128)(2,1)}, u32[]{:S(2)}, u32[]{:S(2)}) collective-permute-start(bf16[4608,128]{1,0:T(8,128)(2,1)} %get-tuple-element.57), channel_id=1, source_target_pairs={{0,1},{1,0},{2,3},{3,2},{4,5},{5,4},{6,7},{7,6},{8,9},{9,8},{10,11... | collective-permute-start | bytes 3538952 | tf_op jit(solution)/shard_map/ppermute | solution.py:581
  463.3 33.0 %all-to-all-start.3 = ((bf16[8,4,32,1024]{3,2,1,0:T(8,128)(2,1)}), bf16[8,4,32,1024]{3,2,1,0:T(8,128)(2,1)S(1)}, u32[]{:S(2)}, u32[]{:S(2)}) async-start(bf16[8,4,32,1024]{3,2,1,0:T(8,128)(2,1)} %broadcast_in_dim.46), calls=%async_computation.5 | async-start | bytes 4194304 | tf_op jit(solution)/shard_map/all_to_all | solution.py:583
Sparse Core Ops, SparseCore 0:
  51.8 46.4 reduce-scatter.2
  119.7 72.8 reduce-scatter.4
Sparse Core Ops, SparseCore 1:
  54.3 34.6 all-gather.10
  198.6 105.9 all-gather.6
  312.2 60.4 all-gather.8

commit v11 on v10

--- a/solution.py
+++ b/solution.py
@@ -577,7 +577,7 @@
         concat_axis=0,
         tiled=True,
     )
-    column, got_first = lax.optimization_barrier((column, got_first))
+    column, got_first, mix_weight_grad = lax.optimization_barrier((column, got_first, mix_weight_grad))
     got_last = lax.ppermute(send_last, "rep", swap)
     table_got = jnp.concatenate([got_first, got_last], axis=1)
     gathered = lax.all_to_all(

time: 506 us -> 508 us (level)
  Pallas kernels: 185 us -> 195 us
  blocking collectives: 74.9 us -> 68.8 us
    pallas_call x1, Pallas kernels: 94.1 us -> 101 us  [owner_backward(): pl.pallas_call(functools.partial(backward_kernel, requesters, length), gr...]
    all_to_all x1, blocking collectives: 26.1 us -> 20 us  [local(): lax.all_to_all(outgoing.astype(BF16), 'table', split_axis=0, concat_axis=...]
    all_to_all x1, waiting for transfers between devices: 5.94 us -> 0.01 us  [local(): lax.all_to_all(jnp.broadcast_to(summed[:query_rows].astype(BF16), (groups...]
  transfers between devices with their start and end apart: 10 -> 10, of which waited for: 4 -> 4; matrix products, arithmetic and copies ran while one was open for 6% -> 6% of each run, Pallas kernels for 37% -> 39%
where the time goes in v11:
time: 508 us; the launch traced here: 506 us
  Pallas kernels  195 us (38%)
  waiting for transfers between devices  133 us (26%)
  blocking collectives  68.8 us (14%)
  other arithmetic  41 us (8%)
  local copies, waits for them, and re-layouts  29 us (6%)
  between operations  16 us (3%)
  starting transfers between devices  11.8 us (2%)
  matrix products  10.9 us (2%)
    pallas_call x1, Pallas kernels, owner_backward(): pl.pallas_call(functools.partial(backward_kernel, requesters, length), gr...  101 us
    pallas_call x1, Pallas kernels, owner_forward(): pl.pallas_call(functools.partial(forward_kernel, blocks, length), grid_sp...  67.7 us
    all_gather x1, waiting for transfers between devices, local(): all_mixed = lax.all_gather(grad_mixed, ('table', 'rep'), axis=0, tiled=True)  66 us
    reduce_scatter x1, waiting for transfers between devices, local(): lax.psum_scatter(pooled_parts, 'table', scatter_dimension=0, tiled=True)  58.8 us
    all_to_all x1, blocking collectives, local(): lax.all_to_all(joined.reshape(batch_rows, devices, mix_part).transpose(1,...  37.8 us
    pallas_call x2, Pallas kernels, table_columns_grad(): pl.pallas_call(table_kernel, grid_spec=pltpu.PrefetchScalarGridSpec(num_s...  26.7 us
    all_to_all x1, blocking collectives, local(): lax.all_to_all(outgoing.astype(BF16), 'table', split_axis=0, concat_axis=...  20 us
    gather x1, local copies, waits for them, and re-layouts, local(): found = feature_table[jnp.clip(wanted, 0, rows_owned - 1)]  15.9 us
  transfers between devices with their start and end apart: 10, of which 4 were waited for; matrix products, arithmetic and copies ran while one was open for 6% of the time, Pallas kernels for 39%

profile of v11, /device:TPU:0, one launch (start us, length us, event | category | flops | bytes accessed | tf_op | source)
XLA Modules:
  0.0 505.5 jit_solution(2094284405043963288)
XLA Ops:
  8.1 0.7 slice_convert_fusion.7
  8.8 0.8 add_select_fusion
  9.6 1.5 fusion.8
  11.1 0.8 divide_reduce-precision_fusion
  11.9 0.1 copy.58
  12.0 0.1 reshape.133
  12.1 0.1 copy.57
  12.2 0.1 reshape.132
  12.4 7.5 %sort.29 = (s32[9600]{0:T(1024)S(1)}, f32[9600]{0:T(1024)S(1)}) sort(s32[9600]{0:T(1024)S(1)} %reshape.132, f32[9600]{0:T(1024)S(1)} %reshape.133), dimensions={0}, to_apply=%region_1.2 | sort | flops 134400 | bytes 153600 | tf_op jit(solution)/shard_map/sort | solution.py:435
  19.9 0.2 convert_reduce_fusion.1
  20.2 0.7 slice_select_fusion
  20.9 1.4 select_maximum_fusion.2
  22.3 11.0 %all-gather.2 = f32[8,1,11136]{2,1,0:T(1,128)S(1)} all-gather(f32[1,1,11136]{2,1,0:T(1,128)S(1)} %reshape.157), channel_id=2, replica_groups=mesh['table'=8,'rep'=4] {'table'}, dimensions={0}, use_global_device_ids=true | all-gather | bytes 400896 | tf_op jit(solution)/shard_map/all_gather | solution.py:460
  33.7 15.9 %gather_fusion = bf16[1536,1024]{1,0:T(8,128)(2,1)S(1)} fusion(bf16[9216,1024]{1,0:T(8,128)(2,1)} %table_other.1, s32[2048]{0:T(1024)S(1)} %pad_clamp_fusion), kind=kCustom, calls=%fused_computation | custom fusion | bytes 6297600 | tf_op jit(solution)/shard_map/gather | solution.py:465
  49.6 2.1 broadcast_select_fusion
  51.8 0.5 all-gather.11.cloned.1.call-update
  52.3 0.3 copy-done.1
  52.8 0.6 convert_element_type.90.bounds
  53.4 0.9 copy.60.shares
  54.3 0.8 copy.59.codes
  55.1 67.7 %owner_forward.1 = (bf16[9216,1024]{1,0:T(8,128)(2,1)}, f32[1536,1024]{1,0:T(8,128)}) custom-call(s32[8,2]{1,0:T(8,128)} %convert_element_type.90.bounds, bf16[9216,1024]{1,0:T(8,128)(2,1)} %table_other.1, bf16[1024,1024]{1,0:T(8,128)(2,1)} %query.5, f32[1,1024]{1,0:T(1,128)} %bitcast.38, s32[8,1,5376]{2,1,0:T(1,128)} %copy.59.codes, f32[8,1,5376]{2,1,0:T(1,128)} %copy.60.shares), custom_call_target="tpu_custom_call" | custom-call | flops 19327352832 | bytes 37748736 | tf_op jit(solution)/shard_map/owner_forward/pallas_call | solution.py:128
  122.8 0.2 all-gather.7.cloned.1.call-start
  123.1 0.7 slice.89
  124.0 1.5 fusion.16
  125.5 1.3 reshape.139.shares
  126.8 0.8 fusion.11
  127.6 3.7 sort.30
  131.4 0.6 reshape.140.self_codes
  132.0 1.6 copy.61.codes
  133.6 0.2 convert_reduce_fusion.3
  133.7 0.8 slice_reduce_fusion
  134.6 58.8 %reduce-scatter.5.cloned.1.call-done = f32[192,1024]{1,0:T(8,128)} async-done(((f32[1536,1024]{1,0:T(8,128)}), f32[192,1024]{1,0:T(8,128)}) %reduce-scatter.5.cloned.1.call-update) | async-done | bytes 786448 | tf_op jit(solution)/shard_map/reduce_scatter | solution.py:494
  193.4 1.2 reduce-precision_convert_fusion
  194.6 3.4 fusion.3
  198.0 1.3 fusion.2
  199.4 0.5 copy.63
  199.9 37.8 %all_to_all.20 = bf16[32,192,64]{1,2,0:T(8,128)(2,1)S(1)} all-to-all(bf16[32,192,64]{1,2,0:T(8,128)(2,1)S(1)} %bitcast.29), channel_id=1, replica_groups=mesh['table'=8,'rep'=4] {'table','rep'}, dimensions={0} | all-to-all | bytes 1572864 | tf_op jit(solution)/shard_map/all_to_all | solution.py:518
  237.6 0.6 copy.64
  238.2 1.1 reshape.143
  239.4 66.0 %all-gather.7.cloned.1.call-done.grads = bf16[6144,1024]{1,0:T(8,128)(2,1)} async-done(((bf16[192,1024]{1,0:T(8,128)(2,1)}), bf16[6144,1024]{1,0:T(8,128)(2,1)}) %all-gather.7.cloned.1.call-update) | async-done | bytes 12582928 | tf_op jit(solution)/shard_map/all_gather | solution.py:516
  305.3 7.5 %convolution_convert_fusion = bf16[64,1024]{1,0:T(8,128)(2,1)} fusion(bf16[6144,64]{0,1:T(8,128)(2,1)S(1)} %reshape.143, bf16[6144,1024]{1,0:T(8,128)(2,1)} %all-gather.7.cloned.1.call-done.grads), kind=kOutput, calls=%fused_computation.6 | convolution fusion | flops 805371904 | bytes 13500416 | tf_op jit(solution)/shard_map/dot_general | solution.py:526
  312.9 0.6 pad_add_fusion.1.place
  313.5 0.7 copy.65.bounds
  314.1 100.8 %owner_backward.1 = (bf16[4608,1024]{1,0:T(8,128)(2,1)}, bf16[4608,1024]{1,0:T(8,128)(2,1)}, f32[272,1024]{1,0:T(8,128)}, bf16[272,1024]{1,0:T(8,128)(2,1)}, f32[8,1024]{1,0:T(8,128)}) custom-call(s32[2]{0:T(128)} %pad_add_fusion.1.place, s32[32,4]{1,0:T(8,128)} %copy.65.bounds, s32[32,1,5376]{2,1,0:T(1,128)} %copy.61.codes, ...), custom_call_target="tpu_custom_call" | custom-call | flops 38654705664 | bytes 25165824 | tf_op jit(solution)/shard_map/owner_backward/pallas_call | solution.py:303
  415.0 1.8 collective-permute-start
  416.7 13.1 %table_columns_grad.3 = (bf16[4608,128]{1,0:T(8,128)(2,1)}, bf16[4608,128]{1,0:T(8,128)(2,1)}) custom-call(s32[1]{0:T(128)} %bitcast.8.place, bf16[4608,1024]{1,0:T(8,128)(2,1)} %get-tuple-element.50.grad_pre, bf16[4608,1024]{1,0:T(8,128)(2,1)} %get-tuple-element.51.self_sums, bf16[1024,1024]{1,0:T(8,128)(2,1)} %query.5, bf16[2048,1024]{1,0:T(8,128)(2,1)} %mix_self.3), custom_call_target="tpu_custom_call" | custom-call | flops 4831838208 | bytes 18874368 | tf_op jit(solution)/shard_map/table_columns_grad/pallas_call | solution.py:387
  429.9 0.2 convert_add_fusion
  430.1 0.4 collective-permute-start.1
  430.6 20.0 %all_to_all.21 = bf16[8,40,1024]{2,1,0:T(8,128)(2,1)S(1)} all-to-all(bf16[8,40,1024]{2,1,0:T(8,128)(2,1)S(1)} %pad_maximum_fusion.1), channel_id=1, replica_groups=mesh['table'=8,'rep'=4] {'table'}, dimensions={0} | all-to-all | bytes 1310720 | tf_op jit(solution)/shard_map/all_to_all | solution.py:570
  450.6 0.1 convert_reduce_fusion
  450.7 0.7 broadcast_in_dim.28
  451.4 3.6 all-to-all-start.2
  455.0 2.0 collective-permute-start.2
  457.1 6.6 %convert_element_type.104 = f32[2048,1024]{1,0:T(8,128)} convert(bf16[2048,1024]{1,0:T(8,128)(2,1)} %all-gather.9.cloned.1.call-done) | non-fusion elementwise | flops 2097152 | bytes 12582912 | tf_op jit(solution)/shard_map/convert_element_type | solution.py:560
  463.7 1.6 broadcast_in_dim.46
  465.3 3.6 all-to-all-start.3
  468.9 0.5 broadcast_multiply_fusion.1
  469.4 0.6 reduce_sum.99
  470.0 13.6 %table_columns_grad.2 = f32[9216,256]{1,0:T(8,128)} custom-call(s32[1]{0:T(128)} %bitcast.7.place, bf16[4608,1024]{1,0:T(8,128)(2,1)} %get-tuple-element.50.grad_pre, bf16[4608,1024]{1,0:T(8,128)(2,1)} %get-tuple-element.51.self_sums, bf16[1024,1024]{1,0:T(8,128)(2,1)} %query.5, bf16[2048,1024]{1,0:T(8,128)(2,1)} %mix_self.3), custom_call_target="tpu_custom_call" | custom-call | flops 4831838208 | bytes 18874368 | tf_op jit(solution)/shard_map/table_columns_grad/pallas_call | solution.py:387
  483.6 0.6 slice.94
  484.2 2.5 collective-permute-done.2
  486.7 3.8 convert_dynamic-update-slice_fusion
  490.5 5.0 all-to-all-done.3
  495.5 2.5 copy_convert_fusion
  (57 shorter events, 1.2 us)
Async XLA Ops:
  8.0 114.8 %reduce-scatter.3.cloned.1.call-start = ((), (), s32[]{:S(2)}) async-start(), calls=%async_computation.6 | async-start | bytes 3538944 | tf_op jit(solution)/shard_map/reduce_scatter | solution.py:467
  33.4 16.2 %copy-start = (f32[8,1,11136]{2,0,1:T(8,128)}, f32[8,1,11136]{2,0,1:T(8,128)S(1)}, u32[]{:S(2)}) copy-start(f32[8,1,11136]{2,0,1:T(8,128)S(1)} %copy.70) | copy-start | bytes 1069060
  51.7 1.0 copy-start.1
  51.7 71.4 %all-gather.11.cloned.1.call-start = ((), (), s32[]{:S(2)}) async-start(), calls=%async_computation.10 | async-start | bytes 1781760 | tf_op jit(solution)/shard_map/all_gather | solution.py:468
  52.3 141.1 %reduce-scatter.5.cloned.1.call-start = ((), (), s32[]{:S(2)}) async-start(), calls=%async_computation.7 | async-start | bytes 7077888 | tf_op jit(solution)/shard_map/reduce_scatter | solution.py:494
  122.8 182.5 %all-gather.7.cloned.1.call-start = ((), (), s32[]{:S(2)}) async-start(), calls=%async_computation.8 | async-start | bytes 12976128 | tf_op jit(solution)/shard_map/all_gather | solution.py:516
  124.0 70.5 %copy-start.3 = (bf16[192,1024]{1,0:T(8,128)(2,1)S(1)}, bf16[192,1024]{1,0:T(8,128)(2,1)}, u32[]{:S(2)}) copy-start(bf16[192,1024]{1,0:T(8,128)(2,1)} %param.17) | copy-start | bytes 1179652
  124.0 70.5 %copy-start.4 = (bf16[192,1024]{1,0:T(8,128)(2,1)S(1)}, bf16[192,1024]{1,0:T(8,128)(2,1)}, u32[]{:S(2)}) copy-start(bf16[192,1024]{1,0:T(8,128)(2,1)} %reduce-scatter.3.cloned.1.call-done) | copy-start | bytes 1179652
  124.0 70.5 %copy-start.6 = (f32[1024]{0:T(1024)S(1)}, f32[1024]{0:T(1024)}, u32[]{:S(2)}) copy-start(f32[1024]{0:T(1024)} %param.13) | copy-start | bytes 12292
  199.3 230.9 %all-gather.9.cloned.1.call-start = ((), (), s32[]{:S(2)}) async-start(), calls=%async_computation.9 | async-start | bytes 4325376 | tf_op jit(solution)/shard_map/all_gather | solution.py:530
  415.0 14.9 %collective-permute-start = (bf16[272,1024]{1,0:T(8,128)(2,1)}, bf16[272,1024]{1,0:T(8,128)(2,1)S(1)}, u32[]{:S(2)}, u32[]{:S(2)}) collective-permute-start(bf16[272,1024]{1,0:T(8,128)(2,1)} %get-tuple-element.53), channel_id=1, source_target_pairs={{0,1},{1,0},{2,3},{3,2},{4,5},{5,4},{6,7},{7,6},{8,9},{9,8},{10,11... | collective-permute-start | bytes 1671176 | tf_op jit(solution)/shard_map/ppermute | solution.py:558
  416.7 13.2 %copy-start.2 = (f32[272,1024]{1,0:T(8,128)S(1)}, f32[272,1024]{1,0:T(8,128)}, u32[]{:S(2)}) copy-start(f32[272,1024]{1,0:T(8,128)} %get-tuple-element.52) | copy-start | bytes 3342340
  430.1 33.6 %collective-permute-start.1 = (bf16[4608,128]{1,0:T(8,128)(2,1)}, bf16[4608,128]{1,0:T(8,128)(2,1)S(1)}, u32[]{:S(2)}, u32[]{:S(2)}) collective-permute-start(bf16[4608,128]{1,0:T(8,128)(2,1)} %get-tuple-element.56), channel_id=1, source_target_pairs={{0,1},{1,0},{2,3},{3,2},{4,5},{5,4},{6,7},{7,6},{8,9},{9,8},{10,11... | collective-permute-start | bytes 3538952 | tf_op jit(solution)/shard_map/ppermute | solution.py:561
  451.4 12.3 %all-to-all-start.2 = ((bf16[4,32,1024]{2,1,0:T(8,128)(2,1)}), bf16[4,32,1024]{2,1,0:T(8,128)(2,1)S(1)}, u32[]{:S(2)}, u32[]{:S(2)}) async-start(bf16[4,32,1024]{2,1,0:T(8,128)(2,1)} %broadcast_in_dim.28), calls=%async_computation.4 | async-start | bytes 524288 | tf_op jit(solution)/shard_map/all_to_all | solution.py:573
  455.0 31.7 %collective-permute-start.2 = (bf16[4608,128]{1,0:T(8,128)(2,1)}, bf16[4608,128]{1,0:T(8,128)(2,1)}, u32[]{:S(2)}, u32[]{:S(2)}) collective-permute-start(bf16[4608,128]{1,0:T(8,128)(2,1)} %get-tuple-element.59), channel_id=1, source_target_pairs={{0,1},{1,0},{2,3},{3,2},{4,5},{5,4},{6,7},{7,6},{8,9},{9,8},{10,11... | collective-permute-start | bytes 3538952 | tf_op jit(solution)/shard_map/ppermute | solution.py:581
  463.7 5.7 %copy-start.5 = (f32[8,1024]{1,0:T(8,128)S(1)}, f32[8,1024]{1,0:T(8,128)}, u32[]{:S(2)}) copy-start(f32[8,1024]{1,0:T(8,128)} %get-tuple-element.62) | copy-start | bytes 98308
  465.3 30.2 %all-to-all-start.3 = ((bf16[8,4,32,1024]{3,2,1,0:T(8,128)(2,1)}), bf16[8,4,32,1024]{3,2,1,0:T(8,128)(2,1)S(1)}, u32[]{:S(2)}, u32[]{:S(2)}) async-start(bf16[8,4,32,1024]{3,2,1,0:T(8,128)(2,1)} %broadcast_in_dim.46), calls=%async_computation.5 | async-start | bytes 4194304 | tf_op jit(solution)/shard_map/all_to_all | solution.py:583
Sparse Core Ops, SparseCore 0:
  51.8 46.4 reduce-scatter.2
  123.0 70.3 reduce-scatter.4
Sparse Core Ops, SparseCore 1:
  54.3 34.6 all-gather.10
  199.3 105.9 all-gather.6
  312.9 60.3 all-gather.8
